TPU v7x, 512 devices: a whole 4x8x8 slice. The times are simulated.
512 devices in a mesh: elem: 32 (over x, y), four: 16 (over z, core).
Axes of the slice: x: 4, y: 8, z: 8, core: 2. Of those that a mesh axis runs over, the one named last changes fastest.
Arguments:
- adjoint_velocity: float32 [3, 2, 11, 1441792], P(None, None, None, ('elem', 'four')), may hold values from -6 to 6
- base_flow: bfloat16 [3, 2, 11, 1441792], P(None, None, None, ('elem', 'four')), may hold values from -6 to 6
- column_widths: float32 [512], P('elem'), may hold values from 0.03 to 0.65
- row_heights: float32 [2], replicated, may hold values from 0.06 to 0.18
- base_phase: int32 [1], replicated, may hold values from 0 to 255
Outputs:
- adjoint_next: float32 [3, 2, 11, 1441792], P(None, None, None, ('elem', 'four'))
All inputs are finite; a program needn't handle non-finite values.
Results may differ from a plain program's by a relative error of at most 0.0003.
Values sent between devices are 32-bit elements; how exact they have to be, the bound alone decides.
No kernel may reach another device: no remote copies, remote signals or barrier semaphores. Data moves between devices by JAX's collectives and lax.ppermute only.
A program may use at most 128 MiB of HBM per device.

v0:
```python
import jax
import jax.numpy as jnp
import numpy as np
from jax import lax
from jax.sharding import PartitionSpec as P

ITERS = 3


NU = 0.005
DT = 0.01
SIGMA = 1.0 / (NU * DT)
HIGHEST = lax.Precision.HIGHEST


def padded(x, sides, width):
    for axis, dim in sides:
        count, length = (lax.axis_size(axis), x.shape[dim])
        up = [(i, (i + 1) % count) for i in range(count - 1)]
        down = [(j, i) for i, j in up]
        last = lax.slice_in_dim(x, length - width, length, axis=dim)
        first = lax.slice_in_dim(x, 0, width, axis=dim)
        before = lax.ppermute(last, axis, up)
        after = lax.ppermute(first, axis, down)
        x = jnp.concatenate([before, x, after], axis=dim)
    return x


def legendre_values(points, node_count):
    table_rows = np.zeros((points.shape[0], node_count))
    table_rows[:, 0] = 1.0
    table_rows[:, 1] = points
    for degree_now in range(2, node_count):
        table_rows[:, degree_now] = (
            (2 * degree_now - 1) * points * table_rows[:, degree_now - 1]
            - (degree_now - 1) * table_rows[:, degree_now - 2]
        ) / degree_now
    return table_rows


def gll_tables(node_count):
    degree = node_count - 1
    points = np.cos(np.pi * np.arange(node_count) / degree)
    for newton_step in range(60):
        legendre = legendre_values(points, node_count)
        points = points - (points * legendre[:, degree] - legendre[:, degree - 1]) / (
            node_count * legendre[:, degree]
        )
    legendre = legendre_values(points, node_count)
    weights = 2.0 / (degree * node_count * legendre[:, degree] ** 2)
    points = points[::-1]
    weights = weights[::-1]
    end_values = legendre[::-1, degree]
    derivative = np.zeros((node_count, node_count))
    for row_index in range(node_count):
        for column in range(node_count):
            if row_index != column:
                derivative[row_index, column] = end_values[row_index] / (
                    end_values[column] * (points[row_index] - points[column])
                )
    derivative[0, 0] = -degree * node_count / 4.0
    derivative[degree, degree] = degree * node_count / 4.0
    return (jnp.asarray(derivative.astype(np.float32)), jnp.asarray(weights.astype(np.float32)))


def fourier_table(plane_count):
    positions = np.arange(plane_count)
    basis_rows = np.zeros((plane_count, plane_count))
    basis_rows[0] = 1.0 / np.sqrt(plane_count)
    basis_rows[1] = np.cos(np.pi * positions) / np.sqrt(plane_count)
    for wave_index in range(1, plane_count // 2):
        basis_rows[2 * wave_index] = np.sqrt(2.0 / plane_count) * np.cos(
            2.0 * np.pi * wave_index * positions / plane_count
        )
        basis_rows[2 * wave_index + 1] = np.sqrt(2.0 / plane_count) * np.sin(
            2.0 * np.pi * wave_index * positions / plane_count
        )
    wave_counts = np.arange(plane_count) // 2
    wave_counts[1] = plane_count // 2
    wave_counts[0] = 0
    wavenumbers = 2.0 * np.pi * wave_counts / (plane_count / 64.0)
    rotate = np.zeros((plane_count, plane_count))
    for wave_index in range(1, plane_count // 2):
        rotate[2 * wave_index, 2 * wave_index + 1] = wavenumbers[2 * wave_index]
        rotate[2 * wave_index + 1, 2 * wave_index] = -wavenumbers[2 * wave_index]
    span_slope = basis_rows.T @ rotate @ basis_rows
    return (
        jnp.asarray(basis_rows.astype(np.float32)),
        jnp.asarray(wavenumbers.astype(np.float32)),
        jnp.asarray(span_slope.astype(np.float32)),
    )


def slope_height(values, heights, derivative):
    turned = jnp.einsum("km,...ympx->...ykpx", derivative, values, precision=HIGHEST)
    return turned * (2.0 / heights).reshape(-1, 1, 1, 1)


def line_slope_width(values, widths, derivative):
    node_count = derivative.shape[0]
    shaped = values.reshape(values.shape[:-2] + (widths.shape[0], node_count, values.shape[-1]))
    turned = jnp.einsum("km,...cmz->...ckz", derivative, shaped, precision=HIGHEST)
    return (turned * (2.0 / widths)[:, None, None]).reshape(values.shape)


def line_slope_span(values, span_slope):
    return jnp.einsum("zw,...w->...z", span_slope, values, precision=HIGHEST)


def line_gradients(values, widths, heights, derivative, span_slope):
    return (
        line_slope_width(values, widths, derivative),
        slope_height(values, heights, derivative),
        line_slope_span(values, span_slope),
    )


def advect(line_values, slopes, base_now, base_slopes):
    pieces = []
    for component in range(3):
        summed = (
            base_now[0] * slopes[0][component]
            + base_now[1] * slopes[1][component]
            + base_now[2] * slopes[2][component]
        )
        summed = summed - (
            line_values[0] * base_slopes[component][0]
            + line_values[1] * base_slopes[component][1]
            + line_values[2] * base_slopes[component][2]
        )
        pieces.append(summed)
    return jnp.stack(pieces)


def assemble_rows(joined, node_count):
    first_row = joined[..., :, 0, :, :]
    last_row = joined[..., :, node_count - 1, :, :]
    shared = last_row[..., :-1, :, :] + first_row[..., 1:, :, :]
    new_first = jnp.concatenate([first_row[..., :1, :, :], shared], axis=-3)
    new_last = jnp.concatenate([shared, last_row[..., -1:, :, :]], axis=-3)
    return jnp.concatenate(
        [
            new_first[..., :, None, :, :],
            joined[..., :, 1 : node_count - 1, :, :],
            new_last[..., :, None, :, :],
        ],
        axis=-3,
    )


def edge_assemble(values, is_first, is_last, node_count):
    extended = padded(values, (("elem", 4),), 1)
    following = extended[..., 2:]
    preceding = extended[..., :-2]
    joined = values + jnp.where(is_last, following, 0.0) + jnp.where(is_first, preceding, 0.0)
    return assemble_rows(joined, node_count)


def inner_product(left, right, weight):
    return jnp.sum(left * right * weight, axis=(-4, -3, -1), keepdims=True)


def residual_sum(residual, weight):
    return lax.psum(inner_product(residual, residual, weight), "elem")


def local(adjoint_velocity, base_flow, column_widths, row_heights, base_phase):
    node_count = adjoint_velocity.shape[2]
    row_count = adjoint_velocity.shape[1]
    columns_here = column_widths.shape[0]
    part_nodes = columns_here * node_count
    planes_local = adjoint_velocity.shape[3] // part_nodes
    adjoint_local = adjoint_velocity.reshape(3, row_count, node_count, planes_local, part_nodes)
    plane_parts = lax.axis_size("four")
    plane_total = planes_local * plane_parts
    columns_line = columns_here // plane_parts
    line_nodes = columns_line * node_count
    base_local = base_flow.reshape(3, row_count, node_count, line_nodes, plane_total)
    basis_rows, wavenumbers, span_slope = fourier_table(plane_total)
    derivative, weights = gll_tables(node_count)
    wave_local = lax.dynamic_slice_in_dim(
        wavenumbers, lax.axis_index("four") * planes_local, planes_local
    )
    line_widths = lax.dynamic_slice_in_dim(
        column_widths, lax.axis_index("four") * columns_line, columns_line
    )
    node_widths = jnp.repeat(column_widths, node_count)
    node_weights = jnp.tile(weights, columns_here)
    eye_cols = jnp.eye(columns_here, dtype=jnp.float32)
    block_turn = jnp.kron(eye_cols, derivative.T)
    block_back = jnp.kron(eye_cols, derivative)
    base_now = jnp.roll(base_local.astype(jnp.float32), base_phase[0], axis=4)
    base_slopes = line_gradients(base_now, line_widths, row_heights, derivative, span_slope)
    sending = jnp.transpose(adjoint_local, (0, 1, 2, 4, 3))
    arrived = lax.all_to_all(sending, "four", split_axis=3, concat_axis=4, tiled=True)
    line_values = jnp.einsum("jz,...xj->...xz", basis_rows, arrived, precision=HIGHEST)
    slopes = line_gradients(line_values, line_widths, row_heights, derivative, span_slope)
    advection = advect(line_values, slopes, base_now, base_slopes)
    advection_hat = jnp.einsum("jz,...xz->...xj", basis_rows, advection, precision=HIGHEST)
    returned = lax.all_to_all(advection_hat, "four", split_axis=4, concat_axis=3, tiled=True)
    returned = jnp.transpose(returned, (0, 1, 2, 4, 3))
    node_x = jnp.arange(part_nodes, dtype=jnp.int32)
    place_x = node_x % node_count
    is_first = place_x == 0
    is_last = place_x == node_count - 1
    height_b = row_heights.reshape(-1, 1, 1, 1)
    weight_y = weights.reshape(-1, 1, 1)
    source = SIGMA * adjoint_local + returned / NU
    local_side = node_widths * height_b * 0.25 * weight_y * node_weights * source
    right_side = edge_assemble(local_side, is_first, is_last, node_count)
    column_x = lax.axis_index("elem") * columns_here + node_x // node_count
    last_column = columns_here * lax.axis_size("elem") - 1
    shared_x = is_first & (column_x > 0) | is_last & (column_x < last_column)
    node_y = jnp.arange(row_count * node_count, dtype=jnp.int32)
    place_y = node_y % node_count
    row_y = node_y // node_count
    shared_y = (place_y == 0) & (row_y > 0) | (place_y == node_count - 1) & (row_y < row_count - 1)
    mult_x = 1.0 + shared_x.astype(jnp.float32)
    mult_y = 1.0 + shared_y.astype(jnp.float32)
    weight = (1.0 / (mult_y[:, None] * mult_x[None, :])).reshape(
        row_count, node_count, 1, part_nodes
    )
    wave_b = (wave_local * wave_local).reshape(-1, 1)
    solution = jnp.zeros_like(right_side)
    residual = right_side
    direction = right_side
    norm_now = residual_sum(residual, weight)
    for iteration in range(ITERS):
        along_x = (
            jnp.einsum("...n,nm->...m", direction, block_turn, precision=HIGHEST) * node_weights
        )
        back_x = jnp.einsum("...n,nm->...m", along_x, block_back, precision=HIGHEST)
        along_y = (
            jnp.einsum("km,...ympx->...ykpx", derivative, direction, precision=HIGHEST) * weight_y
        )
        back_y = jnp.einsum("km,...ykpx->...ympx", derivative, along_y, precision=HIGHEST)
        summed = (
            height_b / node_widths * weight_y * back_x
            + node_widths / height_b * node_weights * back_y
        )
        summed = (
            summed
            + (wave_b + SIGMA)
            * (node_widths * height_b * 0.25)
            * weight_y
            * node_weights
            * direction
        )
        image_vec = edge_assemble(summed, is_first, is_last, node_count)
        curvature = lax.psum(inner_product(direction, image_vec, weight), "elem")
        step_size = norm_now / curvature
        solution = solution + step_size * direction
        residual = residual - step_size * image_vec
        if iteration + 1 < ITERS:
            norm_next = residual_sum(residual, weight)
            direction = residual + norm_next / norm_now * direction
            norm_now = norm_next
    return solution.reshape(3, row_count, node_count, planes_local * part_nodes)


def solution(mesh):
    return jax.shard_map(
        local,
        mesh=mesh,
        in_specs=(
            P(None, None, None, ("elem", "four")),
            P(None, None, None, ("elem", "four")),
            P("elem"),
            P(),
            P(),
        ),
        out_specs=P(None, None, None, ("elem", "four")),
        check_vma=False,
    )
```

profile of v0, /device:TPU:8, one launch (start us, length us, event | category | flops | bytes accessed | tf_op | source)
XLA Modules:
  0.0 668.8 jit_solution(208875317141560853)
XLA Ops:
  2.4 5.8 copy.249
  8.3 9.2 %reshape.312 = f32[16,1,11616]{2,1,0:T(1,128)} reshape(f32[176,11,3,2,16]{4,3,2,1,0:T(2,128)} %bitcast.240) | data formatting | bytes 1486848
  17.4 10.8 %all-to-all-start = ((f32[16,1,11616]{2,1,0:T(1,128)}), f32[16,1,11616]{2,1,0:T(1,128)}, u32[]{:S(2)}, u32[]{:S(2)}) async-start(f32[16,1,11616]{2,1,0:T(1,128)} %reshape.312), calls=%async_computation | async-start | bytes 1490944 | tf_op jit(solution)/shard_map/all_to_all | solution.py:195
  38.6 9.6 %all-to-all-done = f32[16,1,11616]{2,1,0:T(1,128)} async-done(((f32[16,1,11616]{2,1,0:T(1,128)}), f32[16,1,11616]{2,1,0:T(1,128)}, u32[]{:S(2)}, u32[]{:S(2)}) %all-to-all-start) | async-done | bytes 743456 | tf_op jit(solution)/shard_map/all_to_all | solution.py:195
  48.9 4.4 reduce
  53.3 6.5 reshape.313
  59.8 6.1 copy.419
  65.9 6.0 all_to_all.23
  82.9 9.9 %copy.257 = f32[3,2,11,11,256]{3,1,2,0,4:T(2,128)} copy(f32[3,2,11,11,256]{4,3,2,1,0:T(8,128)S(1)} %fusion.39) | data formatting | bytes 1486848 | tf_op jit(solution)/shard_map/jz,...xz->...xj/dot_general | solution.py:199
  92.8 14.4 %reshape.314 = f32[16,1,11616]{2,1,0:T(1,128)} reshape(f32[256,3,11,2,11]{4,3,2,1,0:T(2,128)} %bitcast.235) | data formatting | bytes 1486848
  107.3 5.6 all-to-all-start.1
  117.2 15.9 %all-to-all-done.1 = f32[16,1,11616]{2,1,0:T(1,128)S(1)} async-done(((f32[16,1,11616]{2,1,0:T(1,128)}), f32[16,1,11616]{2,1,0:T(1,128)S(1)}, u32[]{:S(2)}, u32[]{:S(2)}) %all-to-all-start.1) | async-done | bytes 743456 | tf_op jit(solution)/shard_map/all_to_all | solution.py:200
  135.5 17.5 %reshape.315 = f32[256,3,11,2,11]{4,3,2,1,0:T(2,128)} reshape(f32[16,11616]{1,0:T(8,128)S(1)} %reduce.1) | data formatting | bytes 1486848
  153.0 12.0 %copy.258 = f32[3,2,11,11,256]{4,1,3,2,0:T(2,128)S(1)} copy(f32[3,2,11,11,256]{3,1,2,0,4:T(2,128)} %bitcast.236) | data formatting | bytes 1486848 | tf_op jit(solution)/shard_map/all_to_all | solution.py:200
  165.4 4.0 div.128
  169.4 10.4 %copy.330 = f32[3,2,11,16,11,16]{4,3,5,1,0,2:T(8,128)} copy(f32[3,2,11,16,11,16]{5,3,1,4,2,0:T(8,128)} %bitcast.239) | data formatting | bytes 1486848 | tf_op jit(solution)/shard_map/div | solution.py:208
  179.8 6.6 reshape.308
  227.1 73.3 %all-reduce = (f32[3,1,1,16,1]{3,0,4,2,1:T(4,128)}, f32[3,1,1,16,1]{3,0,4,2,1:T(4,128)}) all-reduce(f32[3,1,1,16,1]{3,0,4,2,1:T(4,128)} %bitcast.248, f32[3,1,1,16,1]{3,0,4,2,1:T(4,128)} %bitcast.252), channel_id=1, replica_groups=mesh['elem'=32,'four'=16] {'elem'}, use_global_device_ids=true, to_apply=%region_1.2 | all-reduce | flops 96 | bytes 768 | tf_op jit(solution)/shard_map/psum | solution.py:164
  303.7 74.6 %psum.44 = f32[3,1,1,16,1]{3,0,4,2,1:T(4,128)S(1)} all-reduce(f32[3,1,1,16,1]{3,0,4,2,1:T(4,128)} %bitcast.251), channel_id=1, replica_groups=mesh['elem'=32,'four'=16] {'elem'}, use_global_device_ids=true, to_apply=%region_5.6 | all-reduce | flops 48 | bytes 384 | tf_op jit(solution)/shard_map/psum | solution.py:164
  391.1 3.9 collective-permute-start.5
  403.3 69.8 %psum.45 = f32[3,1,1,16,1]{3,0,4,2,1:T(4,128)} all-reduce(f32[3,1,1,16,1]{3,0,4,2,1:T(4,128)} %bitcast.250), channel_id=1, replica_groups=mesh['elem'=32,'four'=16] {'elem'}, use_global_device_ids=true, to_apply=%region_7.8 | all-reduce | flops 48 | bytes 384 | tf_op jit(solution)/shard_map/psum | solution.py:250
  476.1 72.2 %psum.46 = f32[3,1,1,16,1]{3,0,4,2,1:T(4,128)S(1)} all-reduce(f32[3,1,1,16,1]{3,0,4,2,1:T(4,128)} %bitcast.253), channel_id=1, replica_groups=mesh['elem'=32,'four'=16] {'elem'}, use_global_device_ids=true, to_apply=%region_9.10 | all-reduce | flops 48 | bytes 384 | tf_op jit(solution)/shard_map/psum | solution.py:164
  565.2 4.2 collective-permute-start.7
  594.7 70.2 %psum.47 = f32[3,1,1,16,1]{3,0,4,2,1:T(4,128)S(1)} all-reduce(f32[3,1,1,16,1]{3,0,4,2,1:T(4,128)S(1)} %bitcast.249), channel_id=1, replica_groups=mesh['elem'=32,'four'=16] {'elem'}, use_global_device_ids=true, to_apply=%region_11.12 | all-reduce | flops 48 | bytes 384 | tf_op jit(solution)/shard_map/psum | solution.py:250
  (287 shorter events, 142.6 us)
Async XLA Ops:
  17.4 12.1 %copy-start.28 = (bf16[3,2,11,2816]{3,1,2,0:T(2,128)(2,1)S(1)}, bf16[3,2,11,2816]{3,1,2,0:T(2,128)(2,1)}, u32[]{:S(2)}) copy-start(bf16[3,2,11,2816]{3,1,2,0:T(2,128)(2,1)} %param.11) | copy-start | bytes 1115140
  17.4 12.8 %copy-start.56 = (f32[11]{0:T(128)S(1)}, f32[11]{0:T(128)}, u32[]{:S(2)}) copy-start(f32[11]{0:T(128)} %constant.108.clone) | copy-start | bytes 136
  17.4 12.9 %copy-start.70 = (f32[16]{0:T(128)S(1)}, f32[16]{0:T(128)}, u32[]{:S(2)}) copy-start(f32[16]{0:T(128)} %param.12) | copy-start | bytes 196
  17.4 15.0 %copy-start.72 = (f32[256]{0:T(256)S(1)}, f32[256]{0:T(256)}, u32[]{:S(2)}) copy-start(f32[256]{0:T(256)} %constant.105.clone) | copy-start | bytes 3076
  17.4 30.8 %all-to-all-start = ((f32[16,1,11616]{2,1,0:T(1,128)}), f32[16,1,11616]{2,1,0:T(1,128)}, u32[]{:S(2)}, u32[]{:S(2)}) async-start(f32[16,1,11616]{2,1,0:T(1,128)} %reshape.312), calls=%async_computation | async-start | bytes 1490944 | tf_op jit(solution)/shard_map/all_to_all | solution.py:195
  30.4 84.1 %copy-start.39 = (f32[176]{0:T(256)}, f32[176]{0:T(256)S(1)}, u32[]{:S(2)}) copy-start(f32[176]{0:T(256)S(1)} %mul.718) | copy-start | bytes 2116
  107.3 25.7 %all-to-all-start.1 = ((f32[16,1,11616]{2,1,0:T(1,128)}), f32[16,1,11616]{2,1,0:T(1,128)S(1)}, u32[]{:S(2)}, u32[]{:S(2)}) async-start(f32[16,1,11616]{2,1,0:T(1,128)} %reshape.314), calls=%async_computation.1 | async-start | bytes 1490944 | tf_op jit(solution)/shard_map/all_to_all | solution.py:200
  187.4 9.9 %collective-permute-start = (f32[3,2,11,16,1]{3,1,4,2,0:T(2,128)S(1)}, f32[3,2,11,16,1]{3,1,4,2,0:T(2,128)S(1)}, u32[]{:S(2)}, u32[]{:S(2)}) collective-permute-start(f32[3,2,11,16,1]{3,1,4,2,0:T(2,128)S(1)} %copy.261), channel_id=1, source_target_pairs={{16,0},{32,16},{48,32},{64,48},{80,64},{96,80},{112,96},{128,112},... | collective-permute-start | bytes 12680 | tf_op jit(solution)/shard_map/ppermute | solution.py:24
  190.3 7.5 %collective-permute-start.1 = (f32[3,2,11,16,1]{3,1,4,2,0:T(2,128)S(1)}, f32[3,2,11,16,1]{3,1,4,2,0:T(2,128)S(1)}, u32[]{:S(2)}, u32[]{:S(2)}) collective-permute-start(f32[3,2,11,16,1]{3,1,4,2,0:T(2,128)S(1)} %copy.263), channel_id=1, source_target_pairs={{0,16},{16,32},{32,48},{48,64},{64,80},{80,96},{96,112},{112,128},... | collective-permute-start | bytes 12680 | tf_op jit(solution)/shard_map/ppermute | solution.py:23
  210.6 8.6 %collective-permute-start.2 = (f32[3,2,11,16,1]{3,1,4,2,0:T(2,128)}, f32[3,2,11,16,1]{3,1,4,2,0:T(2,128)}, u32[]{:S(2)}, u32[]{:S(2)}) collective-permute-start(f32[3,2,11,16,1]{3,1,4,2,0:T(2,128)} %copy.273), channel_id=1, source_target_pairs={{16,0},{32,16},{48,32},{64,48},{80,64},{96,80},{112,96},{128,112},... | collective-permute-start | bytes 12680 | tf_op jit(solution)/shard_map/ppermute | solution.py:24
  215.1 6.2 collective-permute-start.3
  225.3 75.8 %copy-start.1 = (f32[3,2,9,16,176]{4,3,1,0,2:T(8,128)}, f32[3,2,9,16,176]{4,3,1,0,2:T(8,128)S(1)}, u32[]{:S(2)}) copy-start(f32[3,2,9,16,176]{4,3,1,0,2:T(8,128)S(1)} %slice.338) | copy-start | bytes 1824772
  388.7 6.3 collective-permute-start.4
  391.1 5.9 collective-permute-start.5
  401.5 72.3 %copy-start = (f32[3,2,11,16,176]{4,3,1,0,2:T(8,128)}, f32[3,2,11,16,176]{4,3,1,0,2:T(8,128)S(1)}, u32[]{:S(2)}) copy-start(f32[3,2,11,16,176]{4,3,1,0,2:T(8,128)S(1)} %fusion.28) | copy-start | bytes 2230276
  561.2 26.9 %collective-permute-start.6 = (f32[3,2,11,16,1]{3,1,4,2,0:T(2,128)S(1)}, f32[3,2,11,16,1]{3,1,4,2,0:T(2,128)}, u32[]{:S(2)}, u32[]{:S(2)}) collective-permute-start(f32[3,2,11,16,1]{3,1,4,2,0:T(2,128)S(1)} %copy.305), channel_id=1, source_target_pairs={{16,0},{32,16},{48,32},{64,48},{80,64},{96,80},{112,96},{128,112},... | collective-permute-start | bytes 12680 | tf_op jit(solution)/shard_map/ppermute | solution.py:24
  565.2 24.9 %collective-permute-start.7 = (f32[3,2,11,16,1]{3,1,4,2,0:T(2,128)}, f32[3,2,11,16,1]{3,1,4,2,0:T(2,128)}, u32[]{:S(2)}, u32[]{:S(2)}) collective-permute-start(f32[3,2,11,16,1]{3,1,4,2,0:T(2,128)} %copy.307), channel_id=1, source_target_pairs={{0,16},{16,32},{32,48},{48,64},{64,80},{80,96},{96,112},{112,128},... | collective-permute-start | bytes 12680 | tf_op jit(solution)/shard_map/ppermute | solution.py:23
  594.3 70.6 %copy-start.52 = (f32[3,1,1,16,1]{3,0,4,2,1:T(4,128)S(1)}, f32[3,1,1,16,1]{3,0,4,2,1:T(4,128)}, u32[]{:S(2)}) copy-start(f32[3,1,1,16,1]{3,0,4,2,1:T(4,128)} %copy-done.51) | copy-start | bytes 580
  594.3 70.8 %copy-start.15 = (f32[3,2,9,2816]{3,1,0,2:T(2,128)S(1)}, f32[3,2,9,2816]{3,1,0,2:T(2,128)}, u32[]{:S(2)}) copy-start(f32[3,2,9,2816]{3,1,0,2:T(2,128)} %concatenate.129) | copy-start | bytes 1824772
  594.3 70.8 %copy-start.32 = (f32[3,2,1,2816]{3,1,0,2:T(2,128)S(1)}, f32[3,2,1,2816]{3,1,0,2:T(2,128)}, u32[]{:S(2)}) copy-start(f32[3,2,1,2816]{3,1,0,2:T(2,128)} %concatenate.110) | copy-start | bytes 202756
  594.3 70.8 %copy-start.33 = (f32[3,2,1,2816]{3,1,0,2:T(2,128)S(1)}, f32[3,2,1,2816]{3,1,0,2:T(2,128)}, u32[]{:S(2)}) copy-start(f32[3,2,1,2816]{3,1,0,2:T(2,128)} %concatenate.112) | copy-start | bytes 202756
  594.3 70.8 %copy-start.34 = (f32[3,2,1,2816]{3,1,0,2:T(2,128)S(1)}, f32[3,2,1,2816]{3,1,0,2:T(2,128)}, u32[]{:S(2)}) copy-start(f32[3,2,1,2816]{3,1,0,2:T(2,128)} %concatenate.119) | copy-start | bytes 202756
  594.3 70.8 %copy-start.35 = (f32[3,2,1,2816]{3,1,0,2:T(2,128)S(1)}, f32[3,2,1,2816]{3,1,0,2:T(2,128)}, u32[]{:S(2)}) copy-start(f32[3,2,1,2816]{3,1,0,2:T(2,128)} %concatenate.121) | copy-start | bytes 202756
  594.3 70.8 %copy-start.36 = (f32[3,2,1,2816]{3,1,0,2:T(2,128)S(1)}, f32[3,2,1,2816]{3,1,0,2:T(2,128)}, u32[]{:S(2)}) copy-start(f32[3,2,1,2816]{3,1,0,2:T(2,128)} %concatenate.128) | copy-start | bytes 202756
  (60 other events, 198.7 us)
where the time goes:
time: 675 us; the launch traced here: 669 us
  blocking collectives  360 us (53%)
  local copies, waits for them, and re-layouts  164 us (24%)
  other arithmetic  44.8 us (7%)
  starting transfers between devices  40.3 us (6%)
  matrix products  30.5 us (5%)
  waiting for transfers between devices  26.1 us (4%)
    psum x3, blocking collectives, residual_sum(): return lax.psum(inner_product(residual, residual, weight), 'elem')  220 us
    psum x2, blocking collectives, local(): curvature = lax.psum(inner_product(direction, image_vec, weight), 'elem')  140 us
    unnamed x152, local copies, waits for them, and re-layouts  53.1 us
    div x3, local copies, waits for them, and re-layouts, local(): source = SIGMA * adjoint_local + returned / NU  21 us
    all_to_all x1, waiting for transfers between devices, local(): lax.all_to_all(advection_hat, 'four', split_axis=4, concat_axis=3, tiled=...  15.9 us
    ppermute x4, starting transfers between devices, padded(): before = lax.ppermute(last, axis, up)  15.3 us
  transfers between devices with their start and end apart: 10, of which 3 were waited for; matrix products, arithmetic and copies ran while one was open for 7% of the time, Pallas kernels for 0%

commit v1 on v0

v1 whole, which is shorter than its diff:
```python
import jax
import jax.numpy as jnp
import numpy as np
from jax import lax
from jax.experimental import pallas as pl
from jax.experimental.pallas import tpu as pltpu
from jax.sharding import PartitionSpec as P

Q = 11
PLANES = 256
PEERS = 16
LOCAL = 16
COLUMNS = 16
GHOST = 3
ROWS = 21
NODES = Q * Q
LANES = 128
NU = 0.005
DT = 0.01
SIGMA = 1.0 / (NU * DT)
HIGHEST = lax.Precision.HIGHEST
F32 = jnp.float32
BF16 = jnp.bfloat16


def legendre_values(points, node_count):
    table_rows = np.zeros((points.shape[0], node_count))
    table_rows[:, 0] = 1.0
    table_rows[:, 1] = points
    for degree_now in range(2, node_count):
        table_rows[:, degree_now] = (
            (2 * degree_now - 1) * points * table_rows[:, degree_now - 1]
            - (degree_now - 1) * table_rows[:, degree_now - 2]
        ) / degree_now
    return table_rows


def gll_tables(node_count):
    degree = node_count - 1
    points = np.cos(np.pi * np.arange(node_count) / degree)
    for newton_step in range(60):
        legendre = legendre_values(points, node_count)
        points = points - (points * legendre[:, degree] - legendre[:, degree - 1]) / (
            node_count * legendre[:, degree]
        )
    legendre = legendre_values(points, node_count)
    weights = 2.0 / (degree * node_count * legendre[:, degree] ** 2)
    points = points[::-1]
    weights = weights[::-1]
    end_values = legendre[::-1, degree]
    derivative = np.zeros((node_count, node_count))
    for row_index in range(node_count):
        for column in range(node_count):
            if row_index != column:
                derivative[row_index, column] = end_values[row_index] / (
                    end_values[column] * (points[row_index] - points[column])
                )
    derivative[0, 0] = -degree * node_count / 4.0
    derivative[degree, degree] = degree * node_count / 4.0
    return derivative, weights


def fourier_table(plane_count):
    positions = np.arange(plane_count)
    basis_rows = np.zeros((plane_count, plane_count))
    basis_rows[0] = 1.0 / np.sqrt(plane_count)
    basis_rows[1] = np.cos(np.pi * positions) / np.sqrt(plane_count)
    for wave_index in range(1, plane_count // 2):
        angle = 2.0 * np.pi * wave_index * positions / plane_count
        basis_rows[2 * wave_index] = np.sqrt(2.0 / plane_count) * np.cos(angle)
        basis_rows[2 * wave_index + 1] = np.sqrt(2.0 / plane_count) * np.sin(angle)
    wave_counts = np.arange(plane_count) // 2
    wave_counts[1] = plane_count // 2
    wave_counts[0] = 0
    wavenumbers = 2.0 * np.pi * wave_counts / (plane_count / 64.0)
    rotate = np.zeros((plane_count, plane_count))
    for wave_index in range(1, plane_count // 2):
        rotate[2 * wave_index, 2 * wave_index + 1] = wavenumbers[2 * wave_index]
        rotate[2 * wave_index + 1, 2 * wave_index] = -wavenumbers[2 * wave_index]
    return basis_rows, rotate.T @ basis_rows, basis_rows.T @ rotate @ basis_rows


def halves(array):
    high = np.asarray(array, np.float32).astype(jnp.bfloat16)
    low = (np.asarray(array, np.float64) - high.astype(np.float64)).astype(jnp.bfloat16)
    return high, low


def split(value):
    high = value.astype(BF16)
    return high, (value - high.astype(F32)).astype(BF16)


def dot(left, right):
    return jnp.dot(left, right, preferred_element_type=F32)


def dot_full(left, right):
    return jnp.dot(left, right, precision=HIGHEST, preferred_element_type=F32)


def lane_ids(shape):
    return lax.broadcasted_iota(jnp.int32, shape, len(shape) - 1)


def turn(value, shift):
    shift = shift % LANES
    return value if shift == 0 else pltpu.roll(value, shift, value.ndim - 1)


def block_transpose(arrays, count):
    lane = lane_ids(arrays[0].shape)
    turned = [turn(array, Q * k) for k, array in enumerate(arrays)]
    results = []
    for place in range(count):
        distance = (lane - Q * place) & (LANES - 1)
        chosen = turned[0]
        for k in range(1, len(turned)):
            chosen = jnp.where(distance >= Q * k, turned[k], chosen)
        chosen = jnp.where(distance < NODES, chosen, 0.0)
        results.append(turn(chosen, -Q * place))
    return results


def pack_body(in_ref, out_ref, scr0, scr1):
    lane = lane_ids((Q, LANES))
    scratches = (scr0, scr1)
    for j in range(LOCAL):
        for t in range(2):
            offset = j * COLUMNS * Q + NODES * t
            tile, shift = offset // LANES, offset % LANES
            first = in_ref[0, 0, :, tile * LANES : (tile + 1) * LANES]
            if shift and tile + 1 < COLUMNS * Q * LOCAL // LANES:
                second = in_ref[0, 0, :, (tile + 1) * LANES : (tile + 2) * LANES]
                first = jnp.where(lane >= shift, first, second)
            scratches[t][j * 16 : j * 16 + Q, :] = turn(first, -shift)
    for t in range(2):
        rows = [scratches[t][pl.ds(qy, LOCAL, stride=16), :] for qy in range(Q)]
        for place, value in enumerate(block_transpose(rows, Q if t == 0 else COLUMNS - Q)):
            out_ref[Q * t + place, 0, 0] = value


def pack(adjoint):
    return pl.pallas_call(
        pack_body,
        grid=(6,),
        in_specs=[pl.BlockSpec((1, 1, Q, COLUMNS * Q * LOCAL), lambda i: (i // 2, i % 2, 0, 0))],
        out_specs=pl.BlockSpec((PEERS, 1, 1, LOCAL, LANES), lambda i: (0, i // 2, i % 2, 0, 0)),
        out_shape=jax.ShapeDtypeStruct((PEERS, 3, 2, LOCAL, LANES), F32),
        scratch_shapes=[pltpu.VMEM((256, LANES), F32)] * 2,
        name="pack",
    )(adjoint)


def base_body(ints, widths, heights, base_ref, table_ref, stack_ref, dzh_ref, dzl_ref,
              field_ref, fgh_ref, fgl_ref, fh_ref, fl_ref, scr):
    step = pl.program_id(0)

    @pl.when(step == 0)
    def _():
        scr[...] = jnp.zeros_like(scr)
        rows = pltpu.roll(table_ref[...], (PLANES - ints[1]) % PLANES, 0)
        for k in range(2):
            high, low = split(rows[:, k * PLANES : (k + 1) * PLANES])
            fgh_ref[k * PLANES : (k + 1) * PLANES, :] = high
            fgl_ref[k * PLANES : (k + 1) * PLANES, :] = low
        high, low = split(jnp.transpose(rows[:, :PLANES]))
        fh_ref[...] = high
        fl_ref[...] = low

    for qx in range(Q):
        part = base_ref[0, 0, :, qx * PLANES : (qx + 1) * PLANES]
        scr[qx * 16 : qx * 16 + Q, :] = part
        scr[176 + qx * 16 : 176 + qx * 16 + Q, :] = part
    mixed = lax.dot_general(
        scr[...], stack_ref[...], (((0,), (0,)), ((), ())), preferred_element_type=F32
    )
    plain = mixed[:, :LANES]
    field_ref[0, 0, 0] = plain
    field_ref[1, 0, 0] = mixed[:, LANES : 2 * LANES] * (2.0 / widths[ints[0]])
    field_ref[2, 0, 0] = mixed[:, 2 * LANES :] * (2.0 / heights[step % 2])
    exact = plain.astype(BF16)
    field_ref[3, 0, 0] = dot(dzh_ref[...], exact) + dot(dzl_ref[...], exact)


def base_stage(ints, widths, heights, base, table, stack, dz_high, dz_low):
    smem = pl.BlockSpec(memory_space=pltpu.SMEM)

    def whole(shape):
        return pl.BlockSpec(shape, lambda i: (0,) * len(shape))

    return pl.pallas_call(
        base_body,
        grid=(6,),
        in_specs=[
            smem, smem, smem,
            pl.BlockSpec((1, 1, Q, Q * PLANES), lambda i: (i // 2, i % 2, 0, 0)),
            whole(table.shape), whole(stack.shape), whole(dz_high.shape), whole(dz_low.shape),
        ],
        out_specs=[
            pl.BlockSpec((4, 1, 1, PLANES, LANES), lambda i: (0, i // 2, i % 2, 0, 0)),
            whole((2 * PLANES, PLANES)), whole((2 * PLANES, PLANES)),
            whole((PLANES, PLANES)), whole((PLANES, PLANES)),
        ],
        out_shape=[
            jax.ShapeDtypeStruct((4, 3, 2, PLANES, LANES), F32),
            jax.ShapeDtypeStruct((2 * PLANES, PLANES), BF16),
            jax.ShapeDtypeStruct((2 * PLANES, PLANES), BF16),
            jax.ShapeDtypeStruct((PLANES, PLANES), BF16),
            jax.ShapeDtypeStruct((PLANES, PLANES), BF16),
        ],
        scratch_shapes=[pltpu.VMEM((352, PLANES), BF16)],
        name="base_stage",
    )(ints, widths, heights, base, table, stack, dz_high, dz_low)


def lines_body(ints, widths, heights, in_ref, field_ref, fgh_ref, fgl_ref, fh_ref, fl_ref,
               dh_ref, dl_ref, mass_ref, out_ref):
    ey = pl.program_id(0)
    width, height = widths[ints[0]], heights[ey]
    coeffs = [in_ref[:, c, 0].reshape(PLANES, LANES) for c in range(3)]
    high, low = split(jnp.concatenate(coeffs, axis=1))
    both = dot(fgh_ref[...], high) + dot(fgh_ref[...], low) + dot(fgl_ref[...], high)
    lines = [both[:PLANES, c * LANES : (c + 1) * LANES] for c in range(3)]
    slopes = [None, None, [both[PLANES:, c * LANES : (c + 1) * LANES] for c in range(3)]]
    high, low = split(jnp.concatenate(lines, axis=0))
    plane = dot(high, dh_ref[...]) + dot(low, dh_ref[...]) + dot(high, dl_ref[...])
    per_c = [plane[c * PLANES : (c + 1) * PLANES] for c in range(3)]
    slopes[0] = [part[:, :LANES] * (2.0 / width) for part in per_c]
    slopes[1] = [part[:, LANES:] * (2.0 / height) for part in per_c]
    pieces = []
    for c in range(3):
        total = field_ref[0, 0, 0] * slopes[0][c]
        for d in range(1, 3):
            total = total + field_ref[0, d, 0] * slopes[d][c]
        for d in range(3):
            total = total - lines[d] * field_ref[1 + c, d, 0]
        pieces.append(total)
    high, low = split(jnp.concatenate(pieces, axis=1))
    hat = dot(fh_ref[...], high) + dot(fh_ref[...], low) + dot(fl_ref[...], high)
    mass = mass_ref[...] * (width * height * 0.25)
    lane = lane_ids((PLANES, LANES))
    for c in range(3):
        source = SIGMA * coeffs[c] + hat[:, c * LANES : (c + 1) * LANES] * (1.0 / NU)
        value = jnp.where(lane < NODES, mass * source, width)
        out_ref[:, c, 0] = value.reshape(PEERS, LOCAL, LANES)


def lines_stage(ints, widths, heights, arrived, fields, tables, d_high, d_low, mass):
    smem = pl.BlockSpec(memory_space=pltpu.SMEM)

    def whole(array):
        return pl.BlockSpec(array.shape, lambda i: (0,) * array.ndim)

    block = pl.BlockSpec((PEERS, 3, 1, LOCAL, LANES), lambda i: (0, 0, i, 0, 0))
    return pl.pallas_call(
        lines_body,
        grid=(2,),
        in_specs=[
            smem, smem, smem, block,
            pl.BlockSpec((4, 3, 1, PLANES, LANES), lambda i: (0, 0, i, 0, 0)),
        ] + [whole(a) for a in tables] + [whole(d_high), whole(d_low), whole(mass)],
        out_specs=block,
        out_shape=jax.ShapeDtypeStruct((PEERS, 3, 2, LOCAL, LANES), F32),
        name="lines_stage",
    )(ints, widths, heights, arrived, fields, *tables, d_high, d_low, mass)


def krylov_body(stiff_y, weights, ints, heights, own_ref, left_ref, right_ref, kb_ref, join_ref, wx_ref,
                v0_ref, v1_ref, v2_ref, mom_ref, loc, kxs, kbs, vec, prod, tmp):
    comp = pl.program_id(0)
    column_refs = (
        [left_ref.at[k] for k in range(GHOST)]
        + [own_ref.at[k] for k in range(COLUMNS)]
        + [right_ref.at[k] for k in range(GHOST)]
    )

    @pl.when(comp == 0)
    def _():
        lane = lane_ids((8, LANES))
        for t in range(2):
            here = jnp.zeros((8, LANES), F32)
            for place in range(Q):
                width = column_refs[Q * t + place][0, 0, 0:8, NODES : NODES + 1]
                inside = (lane >= Q * place) & (lane < Q * place + Q)
                here = jnp.where(inside, width, here)
            vec[0, :, t * LANES : (t + 1) * LANES] = here
        here = vec[0]
        inverse = jnp.where(here > 0.0, 1.0 / jnp.where(here > 0.0, here, 1.0), 0.0)
        line = lane_ids((8, 2 * LANES))
        own = ((line >= GHOST * Q) & (line < NODES)) | (
            (line >= LANES) & (line < LANES + (Q - GHOST) * Q)
        )
        own = own.astype(F32)
        mass_x = here * wx_ref[...]
        vec[1] = dot_full(mass_x, join_ref[...])
        vec[2] = mass_x * own
        place = jnp.where(line >= LANES, line - LANES, line)
        place = place - Q * ((place * 5958) >> 16)
        edge = (place == 0) | (place == Q - 1)
        left_end = (line == GHOST * Q) & (pltpu.roll(here, 1, 1) == 0.0)
        right_end = (line == LANES + (Q - GHOST) * Q - 1) & (
            pltpu.roll(here, 2 * LANES - 1, 1) == 0.0
        )
        shared = edge & jnp.logical_not(left_end | right_end)
        vec[3] = own * jnp.where(shared, 0.5, 1.0)
        scaled = kb_ref[...] * inverse[0:1]
        kxs[...] = dot_full(scaled, join_ref[...])
        kbs[...] = scaled * own[0:1]

    for t in range(2):
        before = None
        for ey in range(2):
            chunks = [column_refs[Q * t + place][0, ey] for place in range(Q)]
            placed = block_transpose(chunks, Q)
            for qy in range(Q):
                value = placed[qy]
                y = qy + (Q - 1) * ey
                if ey == 0 and qy == Q - 1:
                    before = value
                    continue
                if ey == 1 and qy == 0:
                    value = value + before
                loc[y * LOCAL : (y + 1) * LOCAL, t * LANES : (t + 1) * LANES] = value

    h0, h1 = heights[0], heights[1]
    inv0, inv1 = 1.0 / h0, 1.0 / h1
    mass_y = []
    for y in range(ROWS):
        if y < Q - 1:
            mass_y.append(h0 * weights[y])
        elif y == Q - 1:
            mass_y.append(h0 * weights[y] + h1 * weights[0])
        else:
            mass_y.append(h1 * weights[y - Q + 1])

    def products(source_ref, body):
        for half in range(2):
            plane = ints[0] * LOCAL + half * 8 + lax.broadcasted_iota(jnp.int32, (8, LANES), 0)
            kappa = jnp.where(plane == 1, PLANES // 2, plane >> 1).astype(F32)
            beta = kappa * (2.0 * np.pi / (PLANES / 64.0))
            lam = (beta * beta + SIGMA) * 0.25
            for t in range(2):
                rows = [pl.ds(y * LOCAL + half * 8, 8) for y in range(ROWS)]
                lanes = pl.ds(t * LANES, LANES)
                values = [source_ref[r, lanes] for r in rows]
                for y in range(ROWS):
                    total = (lam * mass_y[y]) * values[y]
                    if y <= Q - 1:
                        inner = stiff_y[y][0] * values[0]
                        for m in range(1, Q):
                            inner = inner + stiff_y[y][m] * values[m]
                        total = total + inv0 * inner
                    if y >= Q - 1:
                        inner = stiff_y[y - Q + 1][0] * values[Q - 1]
                        for m in range(1, Q):
                            inner = inner + stiff_y[y - Q + 1][m] * values[Q - 1 + m]
                        total = total + inv1 * inner
                    body(half, t, y, rows[y], lanes, values[y], total)

    first, second, third = v0_ref.at[0], v1_ref.at[0], v2_ref.at[0]
    first[...] = dot_full(loc[...], join_ref[...])
    sums = {}

    def add(key, half, t, value):
        key = (key, half, t)
        sums[key] = value if key not in sums else sums[key] + value

    def step(target, low_key, previous):
        def body(half, t, y, r, lanes, value, total):
            image = mass_y[y] * tmp[r, lanes] + vec[1, :, lanes] * total
            target[r, lanes] = image
            weighted = value * vec[3, :, lanes]
            add(low_key, half, t, weighted * value)
            add(low_key + 1, half, t, weighted * image)
        return body

    def last(half, t, y, r, lanes, value, total):
        image = mass_y[y] * tmp[r, lanes] + vec[2, :, lanes] * total
        add(4, half, t, value * vec[3, :, lanes] * value)
        add(5, half, t, value * image)

    tmp[...] = dot_full(first[...], kxs[...])
    products(first, step(second, 0, None))
    tmp[...] = dot_full(second[...], kxs[...])
    products(second, step(third, 2, None))
    tmp[...] = dot_full(third[...], kbs[...])
    products(third, last)
    prod[...] = jnp.zeros_like(prod)
    for key in range(6):
        for half in range(2):
            prod[key * LOCAL + half * 8 : key * LOCAL + half * 8 + 8, :] = (
                sums[(key, half, 0)] + sums[(key, half, 1)]
            )
    row = lax.dot_general(
        jnp.ones((8, LANES), F32), prod[...], (((1,), (1,)), ((), ())),
        precision=HIGHEST, preferred_element_type=F32,
    )
    mom_ref[:, pl.ds(comp, 1), :] = jnp.broadcast_to(row[0:1][None], (mom_ref.shape[0], 1, LANES))


def krylov_stage(stiff_y, weights, ints, heights, own, left, right, kb, join, wx, peers):
    smem = pl.BlockSpec(memory_space=pltpu.SMEM)

    def whole(array):
        return pl.BlockSpec(array.shape, lambda i: (0,) * array.ndim)

    def chunk(count):
        return pl.BlockSpec((count, 1, 2, LOCAL, LANES), lambda i: (0, i, 0, 0, 0))

    vector = pl.BlockSpec((1, ROWS * LOCAL, 2 * LANES), lambda i: (i, 0, 0))
    shape = jax.ShapeDtypeStruct((3, ROWS * LOCAL, 2 * LANES), F32)

    def body(*refs):
        krylov_body(stiff_y, weights, *refs)

    return pl.pallas_call(
        body,
        grid=(3,),
        in_specs=[smem, smem, chunk(COLUMNS), chunk(GHOST), chunk(GHOST), whole(kb), whole(join), whole(wx)],
        out_specs=[vector, vector, vector, pl.BlockSpec((peers, 8, LANES), lambda i: (0, 0, 0))],
        out_shape=[shape, shape, shape, jax.ShapeDtypeStruct((peers, 8, LANES), F32)],
        scratch_shapes=[
            pltpu.VMEM((ROWS * LOCAL, 2 * LANES), F32),
            pltpu.VMEM((2 * LANES, 2 * LANES), F32),
            pltpu.VMEM((2 * LANES, 2 * LANES), F32),
            pltpu.VMEM((4, 8, 2 * LANES), F32),
            pltpu.VMEM((LANES, LANES), F32),
            pltpu.VMEM((ROWS * LOCAL, 2 * LANES), F32),
        ],
        name="krylov_stage",
    )(ints, heights, own, left, right, kb, join, wx)


def combine_body(mom_ref, v0_ref, v1_ref, v2_ref, out_ref, scr, coef):
    comp = pl.program_id(0)

    @pl.when(comp == 0)
    def _():
        total = jnp.sum(mom_ref[...], axis=0)
        used = (lane_ids((8, LANES)) < LOCAL) & (
            lax.broadcasted_iota(jnp.int32, (8, LANES), 0) < 3
        )
        m = [jnp.where(used, turn(total, -LOCAL * k), 1.0) for k in range(6)]
        inv = 1.0 / m[0]
        m = [value * inv for value in m]
        d0, d1, d2 = (1.0 / jnp.sqrt(m[k]) for k in (1, 3, 5))
        g0, g1, g2 = d0, m[1] * d1, m[2] * d2
        l10 = m[2] * d0 * d1
        l20 = m[3] * d0 * d2
        k21 = m[4] * d1 * d2
        p1 = 1.0 - l10 * l10
        e = k21 - l20 * l10
        l21 = e / p1
        p2 = 1.0 - l20 * l20 - l21 * e
        y1 = g1 - l10 * g0
        y2 = g2 - l20 * g0 - l21 * y1
        z2 = y2 / p2
        z1 = y1 / p1 - l21 * z2
        z0 = g0 - l10 * z1 - l20 * z2
        eye = (
            lax.broadcasted_iota(jnp.int32, (LOCAL, LANES), 0) == lane_ids((LOCAL, LANES))
        ).astype(F32)
        for k, value in enumerate((z0 * d0, z1 * d1, z2 * d2)):
            coef[k] = lax.dot_general(
                eye, jnp.where(used, value, 0.0), (((1,), (1,)), ((), ())),
                precision=HIGHEST, preferred_element_type=F32,
            )

    pick = lane_ids((LOCAL, 8)) == comp
    c0, c1, c2 = (
        jnp.broadcast_to(
            jnp.sum(jnp.where(pick, coef[k], 0.0), axis=1, keepdims=True), (LOCAL, LANES)
        )
        for k in range(3)
    )
    for y in range(ROWS):
        rows = slice(y * LOCAL, (y + 1) * LOCAL)
        for t in range(2):
            lanes = slice(t * LANES, (t + 1) * LANES)
            value = (
                c0 * v0_ref[0, rows, lanes] + c1 * v1_ref[0, rows, lanes] + c2 * v2_ref[0, rows, lanes]
            )
            if y <= Q - 1:
                scr[0, t, pl.ds(y, LOCAL, stride=16), :] = value
            if y >= Q - 1:
                scr[1, t, pl.ds(y - Q + 1, LOCAL, stride=16), :] = value
    lane = lane_ids((16, LANES))
    run = COLUMNS * Q // 2
    for ey in range(2):
        turned = []
        for r in range(2 * LOCAL):
            start = GHOST * Q if r % 2 == 0 else 0
            value = scr[ey, r % 2, (r // 2) * 16 : (r // 2) * 16 + 16, :]
            turned.append(turn(value, run * r - start))
        for tile in range(COLUMNS * Q * LOCAL // LANES):
            low, high = tile * LANES // run, (tile * LANES + LANES - 1) // run
            value = turned[low]
            for r in range(low + 1, high + 1):
                value = jnp.where(lane >= run * r - LANES * tile, turned[r], value)
            out_ref[0, ey, :, tile * LANES : (tile + 1) * LANES] = value[:Q]


def combine(moments, v0, v1, v2):
    vector = pl.BlockSpec((1, ROWS * LOCAL, 2 * LANES), lambda i: (i, 0, 0))
    return pl.pallas_call(
        combine_body,
        grid=(3,),
        in_specs=[pl.BlockSpec(moments.shape, lambda i: (0, 0, 0)), vector, vector, vector],
        out_specs=pl.BlockSpec((1, 2, Q, COLUMNS * Q * LOCAL), lambda i: (i, 0, 0, 0)),
        out_shape=jax.ShapeDtypeStruct((3, 2, Q, COLUMNS * Q * LOCAL), F32),
        scratch_shapes=[pltpu.VMEM((2, 2, 256, LANES), F32), pltpu.VMEM((3, LOCAL, 8), F32)],
        name="combine",
    )(moments, v0, v1, v2)


def make_tables():
    derivative, weights = gll_tables(Q)
    basis, basis_slope, span_slope = fourier_table(PLANES)
    table = np.concatenate([basis.T, basis_slope.T], axis=1)
    table = table.astype(np.float32)
    eye = np.eye(Q)
    nodes = np.zeros((2, LANES, LANES))
    nodes[0, :NODES, :NODES] = np.kron(eye, derivative.T)
    nodes[1, :NODES, :NODES] = np.kron(derivative.T, eye)
    order = np.zeros((176, LANES))
    for qx in range(Q):
        for qy in range(Q):
            order[qx * 16 + qy, qy * Q + qx] = 1.0
    stack = np.concatenate([order, order @ nodes[0], order @ nodes[1]], axis=1)
    stack = np.concatenate(halves(stack), axis=0)
    plane = np.concatenate([nodes[0], nodes[1]], axis=1)
    mass = np.zeros((1, LANES), np.float32)
    mass[0, :NODES] = np.kron(weights, weights)
    stiff = (derivative.T * weights) @ derivative
    kb = np.zeros((2 * LANES, 2 * LANES))
    join = np.eye(2 * LANES)
    wx = np.zeros((1, 2 * LANES), np.float32)
    ends = []
    for t in range(2):
        for place in range(Q):
            low = t * LANES + place * Q
            kb[low : low + Q, low : low + Q] = stiff
            wx[0, low : low + Q] = weights
            ends.append(low)
    for left, right in zip(ends[:-1], ends[1:]):
        join[left + Q - 1, right] = 1.0
        join[right, left + Q - 1] = 1.0
    for t in range(2):
        join[t * LANES + NODES : (t + 1) * LANES] = 0.0
    return dict(
        table=table, stack=stack, dz=halves(span_slope), plane=halves(plane), mass=mass,
        kb=kb.astype(np.float32), join=join.astype(np.float32), wx=wx,
        stiff=stiff.tolist(), weights=weights.tolist(),
    )


def local(adjoint_velocity, base_flow, column_widths, row_heights, base_phase):
    tables = make_tables()
    elem_count = lax.axis_size("elem")
    ints = jnp.stack([lax.axis_index("four").astype(jnp.int32), base_phase[0]])
    send = pack(adjoint_velocity)
    arrived = lax.all_to_all(send, "four", split_axis=0, concat_axis=0, tiled=True)
    fields, *turned = base_stage(
        ints, column_widths, row_heights, base_flow, jnp.asarray(tables["table"]),
        jnp.asarray(tables["stack"]), *(jnp.asarray(a) for a in tables["dz"]),
    )
    source = lines_stage(
        ints, column_widths, row_heights, arrived, fields, turned,
        *(jnp.asarray(a) for a in tables["plane"]), jnp.asarray(tables["mass"]),
    )
    own = lax.all_to_all(source, "four", split_axis=0, concat_axis=0, tiled=True)
    up = [(i, i + 1) for i in range(elem_count - 1)]
    left = lax.ppermute(own[COLUMNS - GHOST :], "elem", up)
    right = lax.ppermute(own[:GHOST], "elem", [(j, i) for i, j in up])
    v0, v1, v2, moments = krylov_stage(
        tables["stiff"], tables["weights"], ints, row_heights, own, left, right,
        jnp.asarray(tables["kb"]), jnp.asarray(tables["join"]), jnp.asarray(tables["wx"]), elem_count,
    )
    moments = lax.all_to_all(moments, "elem", split_axis=0, concat_axis=0, tiled=True)
    return combine(moments, v0, v1, v2)


def solution(mesh):
    split_spec = P(None, None, None, ("elem", "four"))
    return jax.shard_map(
        local,
        mesh=mesh,
        in_specs=(split_spec, split_spec, P("elem"), P(), P()),
        out_specs=split_spec,
        check_vma=False,
    )
```

time: 675 us -> 126 us (0.19)
  blocking collectives: 360 us -> 48.9 us
  local copies, waits for them, and re-layouts: 164 us -> 7.3 us
  other arithmetic: 44.8 us -> 0.59 us
  Pallas kernels: 0 us -> 34.9 us
  matrix products: 30.5 us -> 0 us
  starting transfers between devices: 40.3 us -> 16.4 us
  waiting for transfers between devices: 26.1 us -> 16.1 us
    psum x5 -> x0, blocking collectives: 360 us -> none  [the longest x3 220 us: residual_sum(): return lax.psum(inner_product(residual, residual, weight), 'elem')]
    all_to_all x0 -> x2, blocking collectives: none -> 48.9 us  [the longest x1 27.8 us: local(): lax.all_to_all(source, 'four', split_axis=0, concat_axis=0, tiled=True)]
    unnamed x152 -> x12, local copies, waits for them, and re-layouts: 53.1 us -> 4.61 us
    pallas_call x0 -> x5, Pallas kernels: none -> 34.9 us  [the longest x1 12.3 us: krylov_stage(): pl.pallas_call(body, grid=(3,), in_specs=[smem, smem, chunk(COLUMNS), chu...]
    dot_general x20 -> x0, matrix products: 30.5 us -> none  [the longest x3 6.73 us: local(): jnp.einsum('km,...ympx->...ykpx', derivative, direction, precision=HIGHEST)]
    all_to_all x4 -> x0, local copies, waits for them, and re-layouts: 24.8 us -> none  [the longest x3 12.8 us: local(): lax.all_to_all(sending, 'four', split_axis=3, concat_axis=4, tiled=True)]
    div x3 -> x0, local copies, waits for them, and re-layouts: 21 us -> none  [local(): source = SIGMA * adjoint_local + returned / NU]
    ppermute x8 -> x2, starting transfers between devices: 23.8 us -> 5.86 us  [the longest x1 3.52 us: local(): left = lax.ppermute(own[COLUMNS - GHOST:], 'elem', up)]
  transfers between devices with their start and end apart: 10 -> 3, of which waited for: 3 -> 3; matrix products, arithmetic and copies ran while one was open for 7% -> 1% of each run, Pallas kernels for 0% -> 6%
where the time goes in v1:
time: 126 us; the launch traced here: 125 us
  blocking collectives  48.9 us (39%)
  Pallas kernels  34.9 us (28%)
  starting transfers between devices  16.4 us (13%)
  waiting for transfers between devices  16.1 us (13%)
  local copies, waits for them, and re-layouts  7.3 us (6%)
    all_to_all x1, blocking collectives, local(): lax.all_to_all(source, 'four', split_axis=0, concat_axis=0, tiled=True)  27.8 us
    all_to_all x1, blocking collectives, local(): lax.all_to_all(moments, 'elem', split_axis=0, concat_axis=0, tiled=True)  21.2 us
    pallas_call x1, Pallas kernels, krylov_stage(): pl.pallas_call(body, grid=(3,), in_specs=[smem, smem, chunk(COLUMNS), chu...  12.3 us
    all_to_all x1, waiting for transfers between devices, local(): lax.all_to_all(send, 'four', split_axis=0, concat_axis=0, tiled=True)  11.6 us
    all_to_all x1, starting transfers between devices, local(): lax.all_to_all(send, 'four', split_axis=0, concat_axis=0, tiled=True)  10.6 us
    pallas_call x1, Pallas kernels, base_stage(): pl.pallas_call(base_body, grid=(6,), in_specs=[smem, smem, smem, pl.Block...  6.98 us
    pallas_call x1, Pallas kernels, lines_stage(): pl.pallas_call(lines_body, grid=(2,), in_specs=[smem, smem, smem, block,...  5.89 us
    pallas_call x1, Pallas kernels, pack(): pl.pallas_call(pack_body, grid=(6,), in_specs=[pl.BlockSpec((1, 1, Q, COL...  5.29 us
  transfers between devices with their start and end apart: 3, of which 3 were waited for; matrix products, arithmetic and copies ran while one was open for 1% of the time, Pallas kernels for 6%

profile of v1, /device:TPU:8, one launch (start us, length us, event | category | flops | bytes accessed | tf_op | source)
XLA Modules:
  0.0 125.0 jit_solution(51403583844897075)
XLA Ops:
  0.0 2.2 %copy.16.in_ref = f32[3,2,11,2816]{3,2,1,0:T(8,128)} copy(f32[3,2,11,2816]{3,1,2,0:T(2,128)} %param.15) | data formatting | bytes 1486848 | tf_op args[0]
  2.2 5.3 %pack.1 = f32[16,3,2,16,128]{4,3,2,1,0:T(8,128)} custom-call(f32[3,2,11,2816]{3,2,1,0:T(8,128)} %copy.16.in_ref), custom_call_target="tpu_custom_call" | custom-call | tf_op jit(solution)/shard_map/pack/pallas_call | solution.py:144
  7.5 0.0 copy-start.2
  7.5 10.6 %all-to-all-start = ((f32[16,3,2,16,128]{4,3,2,1,0:T(8,128)}), f32[16,3,2,16,128]{4,3,2,1,0:T(8,128)S(1)}, u32[]{:S(2)}, u32[]{:S(2)}) async-start(f32[16,3,2,16,128]{4,3,2,1,0:T(8,128)} %pack.1), calls=%async_computation | async-start | bytes 1572864 | tf_op jit(solution)/shard_map/all_to_all | solution.py:563
  18.7 0.0 copy-done.2
  18.7 0.9 copy.17.base_ref
  19.6 0.6 pad_add_fusion.ints.refs_0_
  20.1 7.0 %base_stage.1 = (f32[4,3,2,256,128]{4,3,2,1,0:T(8,128)}, bf16[512,256]{1,0:T(8,128)(2,1)}, bf16[512,256]{1,0:T(8,128)(2,1)}, bf16[256,256]{1,0:T(8,128)(2,1)}, bf16[256,256]{1,0:T(8,128)(2,1)}) custom-call(s32[2]{0:T(128)} %pad_add_fusion.ints.refs_0_, f32[16]{0:T(128)} %widths.3, f32[2]{0:T(128)} %refs_1_.1, bf16[3,2,11,2816]{3,2,1,0:T(8,128)(2,1)} %copy.17.base_ref, ...), custom_call_target="tpu_custom_call" | custom-call | tf_op jit(solution)/shard_map/base_stage/pallas_call | solution.py:192
  27.1 11.6 %all-to-all-done.in_ref = f32[16,3,2,16,128]{4,3,2,1,0:T(8,128)S(1)} async-done(((f32[16,3,2,16,128]{4,3,2,1,0:T(8,128)}), f32[16,3,2,16,128]{4,3,2,1,0:T(8,128)S(1)}, u32[]{:S(2)}, u32[]{:S(2)}) %all-to-all-start) | async-done | bytes 786464 | tf_op jit(solution)/shard_map/all_to_all | solution.py:563
  38.7 0.0 copy-start.1
  38.7 0.9 copy-done.1
  39.6 5.9 %lines_stage.1 = f32[16,3,2,16,128]{4,3,2,1,0:T(8,128)} custom-call(s32[2]{0:T(128)} %pad_add_fusion.ints.refs_0_, f32[16]{0:T(128)} %widths.3, f32[2]{0:T(128)} %refs_1_.1, f32[16,3,2,16,128]{4,3,2,1,0:T(8,128)} %copy-done.1, f32[4,3,2,256,128]{4,3,2,1,0:T(8,128)} %get-tuple-element.14.field_ref, bf16[512,256]{1,0:T(8,128)(2,1)} %get-tuple-element.15.fgh_ref, ...), custom_call_target="tpu_custom_call" | custom-call | tf_op jit(solution)/shard_map/lines_stage/pallas_call | solution.py:256
  45.5 27.8 %all_to_all.15.refs_2_ = f32[16,3,2,16,128]{4,3,2,1,0:T(8,128)S(1)} all-to-all(f32[16,3,2,16,128]{4,3,2,1,0:T(8,128)} %lines_stage.1), channel_id=1, replica_groups=mesh['elem'=32,'four'=16] {'four'}, dimensions={0} | all-to-all | bytes 1572864 | tf_op jit(solution)/shard_map/all_to_all | solution.py:572
  73.3 2.3 %collective-permute-start.1 = (f32[3,3,2,16,128]{4,3,2,1,0:T(8,128)S(1)}, f32[3,3,2,16,128]{4,3,2,1,0:T(8,128)S(1)}, u32[]{:S(2)}, u32[]{:S(2)}) collective-permute-start(f32[3,3,2,16,128]{4,3,2,1,0:T(8,128)S(1)} %get-tuple-element.23), channel_id=1, source_target_pairs={{16,0},{32,16},{48,32},{64,48},{80,64},{96,80},{112,96},{128,112},... | collective-permute-start | bytes 442376 | tf_op jit(solution)/shard_map/ppermute | solution.py:575
  75.7 3.5 %collective-permute-start = (f32[3,3,2,16,128]{4,3,2,1,0:T(8,128)S(1)}, f32[3,3,2,16,128]{4,3,2,1,0:T(8,128)S(1)}, u32[]{:S(2)}, u32[]{:S(2)}) collective-permute-start(f32[3,3,2,16,128]{4,3,2,1,0:T(8,128)S(1)} %get-tuple-element.24), channel_id=1, source_target_pairs={{0,16},{16,32},{32,48},{48,64},{64,80},{80,96},{96,112},{112,128},... | collective-permute-start | bytes 442376 | tf_op jit(solution)/shard_map/ppermute | solution.py:574
  79.2 2.4 %collective-permute-done.1.refs_4_ = f32[3,3,2,16,128]{4,3,2,1,0:T(8,128)S(1)} collective-permute-done((f32[3,3,2,16,128]{4,3,2,1,0:T(8,128)S(1)}, f32[3,3,2,16,128]{4,3,2,1,0:T(8,128)S(1)}, u32[]{:S(2)}, u32[]{:S(2)}) %collective-permute-start.1) | collective-permute-done | bytes 147488 | tf_op jit(solution)/shard_map/ppermute | solution.py:575
  81.6 2.1 %collective-permute-done.refs_3_ = f32[3,3,2,16,128]{4,3,2,1,0:T(8,128)S(1)} collective-permute-done((f32[3,3,2,16,128]{4,3,2,1,0:T(8,128)S(1)}, f32[3,3,2,16,128]{4,3,2,1,0:T(8,128)S(1)}, u32[]{:S(2)}, u32[]{:S(2)}) %collective-permute-start) | collective-permute-done | bytes 147488 | tf_op jit(solution)/shard_map/ppermute | solution.py:574
  83.7 0.0 copy-done
  83.7 0.0 copy-done.3
  83.7 0.7 copy-done.4
  84.4 12.3 %krylov_stage.1 = (f32[3,336,256]{2,1,0:T(8,128)}, f32[3,336,256]{2,1,0:T(8,128)}, f32[3,336,256]{2,1,0:T(8,128)}, f32[32,8,128]{2,1,0:T(8,128)}) custom-call(s32[2]{0:T(128)} %pad_add_fusion.ints.refs_0_, f32[2]{0:T(128)} %refs_1_.1, f32[16,3,2,16,128]{4,3,2,1,0:T(8,128)} %copy-done, f32[3,3,2,16,128]{4,3,2,1,0:T(8,128)} %copy-done.4, ...), custom_call_target="tpu_custom_call" | custom-call | tf_op jit(solution)/shard_map/krylov_stage/pallas_call | solution.py:417
  96.6 21.2 %all_to_all.16.mom_ref = f32[32,8,128]{2,1,0:T(8,128)} all-to-all(f32[32,8,128]{2,1,0:T(8,128)} %get-tuple-element.19), channel_id=1, replica_groups=mesh['elem'=32,'four'=16] {'elem'}, dimensions={0} | all-to-all | bytes 262144 | tf_op jit(solution)/shard_map/all_to_all | solution.py:580
  117.8 4.5 %combine.1 = f32[3,2,11,2816]{3,2,1,0:T(8,128)} custom-call(f32[32,8,128]{2,1,0:T(8,128)} %all_to_all.16.mom_ref, f32[3,336,256]{2,1,0:T(8,128)} %get-tuple-element.20.v0_ref, f32[3,336,256]{2,1,0:T(8,128)} %get-tuple-element.21.v1_ref, f32[3,336,256]{2,1,0:T(8,128)} %get-tuple-element.22.v2_ref), custom_call_target="tpu_custom_call" | custom-call | tf_op jit(solution)/shard_map/combine/pallas_call | solution.py:506
  122.3 2.7 %copy.18 = f32[3,2,11,2816]{3,1,2,0:T(2,128)} copy(f32[3,2,11,2816]{3,2,1,0:T(8,128)} %combine.1) | data formatting | bytes 1486848 | tf_op jit(solution)/shard_map/combine/pallas_call | solution.py:506
  (4 shorter events, 0.0 us)
Async XLA Ops:
  7.5 11.2 %copy-start.2 = (bf16[3,2,11,2816]{3,1,2,0:T(2,128)(2,1)S(1)}, bf16[3,2,11,2816]{3,1,2,0:T(2,128)(2,1)}, u32[]{:S(2)}) copy-start(bf16[3,2,11,2816]{3,1,2,0:T(2,128)(2,1)} %param.16) | copy-start | bytes 1115140
  7.5 31.2 %all-to-all-start = ((f32[16,3,2,16,128]{4,3,2,1,0:T(8,128)}), f32[16,3,2,16,128]{4,3,2,1,0:T(8,128)S(1)}, u32[]{:S(2)}, u32[]{:S(2)}) async-start(f32[16,3,2,16,128]{4,3,2,1,0:T(8,128)} %pack.1), calls=%async_computation | async-start | bytes 1572864 | tf_op jit(solution)/shard_map/all_to_all | solution.py:563
  38.7 0.9 copy-start.1
  73.3 10.4 %copy-start = (f32[16,3,2,16,128]{4,3,2,1,0:T(8,128)}, f32[16,3,2,16,128]{4,3,2,1,0:T(8,128)S(1)}, u32[]{:S(2)}) copy-start(f32[16,3,2,16,128]{4,3,2,1,0:T(8,128)S(1)} %all_to_all.15.refs_2_) | copy-start | bytes 2359300
  73.3 8.3 %collective-permute-start.1 = (f32[3,3,2,16,128]{4,3,2,1,0:T(8,128)S(1)}, f32[3,3,2,16,128]{4,3,2,1,0:T(8,128)S(1)}, u32[]{:S(2)}, u32[]{:S(2)}) collective-permute-start(f32[3,3,2,16,128]{4,3,2,1,0:T(8,128)S(1)} %get-tuple-element.23), channel_id=1, source_target_pairs={{16,0},{32,16},{48,32},{64,48},{80,64},{96,80},{112,96},{128,112},... | collective-permute-start | bytes 442376 | tf_op jit(solution)/shard_map/ppermute | solution.py:575
  75.7 8.0 %collective-permute-start = (f32[3,3,2,16,128]{4,3,2,1,0:T(8,128)S(1)}, f32[3,3,2,16,128]{4,3,2,1,0:T(8,128)S(1)}, u32[]{:S(2)}, u32[]{:S(2)}) collective-permute-start(f32[3,3,2,16,128]{4,3,2,1,0:T(8,128)S(1)} %get-tuple-element.24), channel_id=1, source_target_pairs={{0,16},{16,32},{32,48},{48,64},{64,80},{80,96},{96,112},{112,128},... | collective-permute-start | bytes 442376 | tf_op jit(solution)/shard_map/ppermute | solution.py:574
  81.6 2.1 %copy-start.3 = (f32[3,3,2,16,128]{4,3,2,1,0:T(8,128)}, f32[3,3,2,16,128]{4,3,2,1,0:T(8,128)S(1)}, u32[]{:S(2)}) copy-start(f32[3,3,2,16,128]{4,3,2,1,0:T(8,128)S(1)} %collective-permute-done.1.refs_4_) | copy-start | bytes 442372
  83.7 0.7 copy-start.4

commit v2 on v1

--- a/solution.py
+++ b/solution.py
@@ -122,34 +122,44 @@
     return results
 
 
-def pack_body(in_ref, out_ref, scr0, scr1):
-    lane = lane_ids((Q, LANES))
+def pack_body(in_ref, out_ref, flat, scr0, scr1):
+    lane = lane_ids((16, LANES))
     scratches = (scr0, scr1)
-    for j in range(LOCAL):
+    tiles = COLUMNS * Q * LOCAL // LANES
+    for qy in range(Q):
+        for tile in range(tiles):
+            flat[tile, pl.ds(qy, 2, stride=16), :] = in_ref[0, qy, :, tile * LANES : (tile + 1) * LANES]
+    for ey in range(2):
+        rows = slice(ey * 16, ey * 16 + 16)
+        for j in range(LOCAL):
+            for t in range(2):
+                offset = j * COLUMNS * Q + NODES * t
+                tile, shift = offset // LANES, offset % LANES
+                first = flat[tile, rows, :]
+                if shift and tile + 1 < tiles:
+                    first = jnp.where(lane >= shift, first, flat[tile + 1, rows, :])
+                scratches[t][ey, j * 16 : j * 16 + 16, :] = turn(first, -shift)
+    for ey in range(2):
         for t in range(2):
-            offset = j * COLUMNS * Q + NODES * t
-            tile, shift = offset // LANES, offset % LANES
-            first = in_ref[0, 0, :, tile * LANES : (tile + 1) * LANES]
-            if shift and tile + 1 < COLUMNS * Q * LOCAL // LANES:
-                second = in_ref[0, 0, :, (tile + 1) * LANES : (tile + 2) * LANES]
-                first = jnp.where(lane >= shift, first, second)
-            scratches[t][j * 16 : j * 16 + Q, :] = turn(first, -shift)
-    for t in range(2):
-        rows = [scratches[t][pl.ds(qy, LOCAL, stride=16), :] for qy in range(Q)]
-        for place, value in enumerate(block_transpose(rows, Q if t == 0 else COLUMNS - Q)):
-            out_ref[Q * t + place, 0, 0] = value
+            rows = [scratches[t][ey, pl.ds(qy, LOCAL, stride=16), :] for qy in range(Q)]
+            for place, value in enumerate(block_transpose(rows, Q if t == 0 else COLUMNS - Q)):
+                out_ref[Q * t + place, 0, ey] = value
 
 
 def pack(adjoint):
     return pl.pallas_call(
         pack_body,
-        grid=(6,),
-        in_specs=[pl.BlockSpec((1, 1, Q, COLUMNS * Q * LOCAL), lambda i: (i // 2, i % 2, 0, 0))],
-        out_specs=pl.BlockSpec((PEERS, 1, 1, LOCAL, LANES), lambda i: (0, i // 2, i % 2, 0, 0)),
+        grid=(3,),
+        in_specs=[pl.BlockSpec((1, Q, 2, COLUMNS * Q * LOCAL), lambda i: (i, 0, 0, 0))],
+        out_specs=pl.BlockSpec((PEERS, 1, 2, LOCAL, LANES), lambda i: (0, i, 0, 0, 0)),
         out_shape=jax.ShapeDtypeStruct((PEERS, 3, 2, LOCAL, LANES), F32),
-        scratch_shapes=[pltpu.VMEM((256, LANES), F32)] * 2,
+        scratch_shapes=[
+            pltpu.VMEM((COLUMNS * Q * LOCAL // LANES, 32, LANES), F32),
+            pltpu.VMEM((2, 256, LANES), F32),
+            pltpu.VMEM((2, 256, LANES), F32),
+        ],
         name="pack",
-    )(adjoint)
+    )(jnp.transpose(adjoint, (0, 2, 1, 3)))
 
 
 def base_body(ints, widths, heights, base_ref, table_ref, stack_ref, dzh_ref, dzl_ref,
@@ -432,8 +442,58 @@
     )(ints, heights, own, left, right, kb, join, wx)
 
 
-def combine_body(mom_ref, v0_ref, v1_ref, v2_ref, out_ref, scr, coef):
+def unpack_body(v0_ref, v1_ref, v2_ref, u0_ref, u1_ref, u2_ref, scr, flat):
+    lane = lane_ids((16, LANES))
+    run = COLUMNS * Q // 2
+    for vector, target in ((v0_ref, u0_ref), (v1_ref, u1_ref), (v2_ref, u2_ref)):
+        for y in range(ROWS):
+            rows = slice(y * LOCAL, (y + 1) * LOCAL)
+            for t in range(2):
+                value = vector[0, rows, t * LANES : (t + 1) * LANES]
+                if y <= Q - 1:
+                    scr[0, t, pl.ds(y, LOCAL, stride=16), :] = value
+                if y >= Q - 1:
+                    scr[1, t, pl.ds(y - Q + 1, LOCAL, stride=16), :] = value
+        for ey in range(2):
+            turned = []
+            for r in range(2 * LOCAL):
+                start = GHOST * Q if r % 2 == 0 else 0
+                value = scr[ey, r % 2, (r // 2) * 16 : (r // 2) * 16 + 16, :]
+                turned.append(turn(value, run * r - start))
+            for tile in range(COLUMNS * Q * LOCAL // LANES):
+                low, high = tile * LANES // run, (tile * LANES + LANES - 1) // run
+                value = turned[low]
+                for r in range(low + 1, high + 1):
+                    value = jnp.where(lane >= run * r - LANES * tile, turned[r], value)
+                flat[tile, ey * 16 : ey * 16 + 16, :] = value
+        for qy in range(Q):
+            for tile in range(COLUMNS * Q * LOCAL // LANES):
+                target[0, qy, :, tile * LANES : (tile + 1) * LANES] = flat[
+                    tile, pl.ds(qy, 2, stride=16), :
+                ]
+
+
+def unpack(v0, v1, v2):
+    vector = pl.BlockSpec((1, ROWS * LOCAL, 2 * LANES), lambda i: (i, 0, 0))
+    target = pl.BlockSpec((1, Q, 2, COLUMNS * Q * LOCAL), lambda i: (i, 0, 0, 0))
+    shape = jax.ShapeDtypeStruct((3, Q, 2, COLUMNS * Q * LOCAL), F32)
+    return pl.pallas_call(
+        unpack_body,
+        grid=(3,),
+        in_specs=[vector] * 3,
+        out_specs=[target] * 3,
+        out_shape=[shape] * 3,
+        scratch_shapes=[
+            pltpu.VMEM((2, 2, 256, LANES), F32),
+            pltpu.VMEM((COLUMNS * Q * LOCAL // LANES, 32, LANES), F32),
+        ],
+        name="unpack",
+    )(v0, v1, v2)
+
+
+def finish_body(mom_ref, u0_ref, u1_ref, u2_ref, out_ref, coef):
     comp = pl.program_id(0)
+    tiles = COLUMNS * Q * LOCAL // LANES
 
     @pl.when(comp == 0)
     def _():
@@ -458,60 +518,42 @@
         z2 = y2 / p2
         z1 = y1 / p1 - l21 * z2
         z0 = g0 - l10 * z1 - l20 * z2
-        eye = (
-            lax.broadcasted_iota(jnp.int32, (LOCAL, LANES), 0) == lane_ids((LOCAL, LANES))
-        ).astype(F32)
+        lane = lane_ids((8, LANES))
         for k, value in enumerate((z0 * d0, z1 * d1, z2 * d2)):
-            coef[k] = lax.dot_general(
-                eye, jnp.where(used, value, 0.0), (((1,), (1,)), ((), ())),
-                precision=HIGHEST, preferred_element_type=F32,
+            wide = [jnp.broadcast_to(value[:, j : j + 1], (8, LANES)) for j in range(LOCAL)]
+            for tile in range(tiles):
+                low = tile * LANES // (COLUMNS * Q)
+                high = (tile * LANES + LANES - 1) // (COLUMNS * Q)
+                chosen = wide[low]
+                if high > low:
+                    chosen = jnp.where(lane >= COLUMNS * Q * high - LANES * tile, wide[high], chosen)
+                coef[k, tile] = chosen
+
+    for tile in range(tiles):
+        lanes = slice(tile * LANES, (tile + 1) * LANES)
+        c0, c1, c2 = (
+            jnp.broadcast_to(coef[k, tile, pl.ds(comp, 1), :], (2, LANES)) for k in range(3)
+        )
+        for qy in range(Q):
+            out_ref[0, qy, :, lanes] = (
+                c0 * u0_ref[0, qy, :, lanes]
+                + c1 * u1_ref[0, qy, :, lanes]
+                + c2 * u2_ref[0, qy, :, lanes]
             )
 
-    pick = lane_ids((LOCAL, 8)) == comp
-    c0, c1, c2 = (
-        jnp.broadcast_to(
-            jnp.sum(jnp.where(pick, coef[k], 0.0), axis=1, keepdims=True), (LOCAL, LANES)
-        )
-        for k in range(3)
-    )
-    for y in range(ROWS):
-        rows = slice(y * LOCAL, (y + 1) * LOCAL)
-        for t in range(2):
-            lanes = slice(t * LANES, (t + 1) * LANES)
-            value = (
-                c0 * v0_ref[0, rows, lanes] + c1 * v1_ref[0, rows, lanes] + c2 * v2_ref[0, rows, lanes]
-            )
-            if y <= Q - 1:
-                scr[0, t, pl.ds(y, LOCAL, stride=16), :] = value
-            if y >= Q - 1:
-                scr[1, t, pl.ds(y - Q + 1, LOCAL, stride=16), :] = value
-    lane = lane_ids((16, LANES))
-    run = COLUMNS * Q // 2
-    for ey in range(2):
-        turned = []
-        for r in range(2 * LOCAL):
-            start = GHOST * Q if r % 2 == 0 else 0
-            value = scr[ey, r % 2, (r // 2) * 16 : (r // 2) * 16 + 16, :]
-            turned.append(turn(value, run * r - start))
-        for tile in range(COLUMNS * Q * LOCAL // LANES):
-            low, high = tile * LANES // run, (tile * LANES + LANES - 1) // run
-            value = turned[low]
-            for r in range(low + 1, high + 1):
-                value = jnp.where(lane >= run * r - LANES * tile, turned[r], value)
-            out_ref[0, ey, :, tile * LANES : (tile + 1) * LANES] = value[:Q]
-
-
-def combine(moments, v0, v1, v2):
-    vector = pl.BlockSpec((1, ROWS * LOCAL, 2 * LANES), lambda i: (i, 0, 0))
-    return pl.pallas_call(
-        combine_body,
+
+def finish(moments, u0, u1, u2):
+    target = pl.BlockSpec((1, Q, 2, COLUMNS * Q * LOCAL), lambda i: (i, 0, 0, 0))
+    out = pl.pallas_call(
+        finish_body,
         grid=(3,),
-        in_specs=[pl.BlockSpec(moments.shape, lambda i: (0, 0, 0)), vector, vector, vector],
-        out_specs=pl.BlockSpec((1, 2, Q, COLUMNS * Q * LOCAL), lambda i: (i, 0, 0, 0)),
-        out_shape=jax.ShapeDtypeStruct((3, 2, Q, COLUMNS * Q * LOCAL), F32),
-        scratch_shapes=[pltpu.VMEM((2, 2, 256, LANES), F32), pltpu.VMEM((3, LOCAL, 8), F32)],
-        name="combine",
-    )(moments, v0, v1, v2)
+        in_specs=[pl.BlockSpec(moments.shape, lambda i: (0, 0, 0)), target, target, target],
+        out_specs=target,
+        out_shape=jax.ShapeDtypeStruct((3, Q, 2, COLUMNS * Q * LOCAL), F32),
+        scratch_shapes=[pltpu.VMEM((3, COLUMNS * Q * LOCAL // LANES, 8, LANES), F32)],
+        name="finish",
+    )(moments, u0, u1, u2)
+    return jnp.transpose(out, (0, 2, 1, 3))
 
 
 def make_tables():
@@ -578,7 +620,7 @@
         jnp.asarray(tables["kb"]), jnp.asarray(tables["join"]), jnp.asarray(tables["wx"]), elem_count,
     )
     moments = lax.all_to_all(moments, "elem", split_axis=0, concat_axis=0, tiled=True)
-    return combine(moments, v0, v1, v2)
+    return finish(moments, *unpack(v0, v1, v2))
 
 
 def solution(mesh):

time: 126 us -> 120 us (0.952)
  blocking collectives: 48.9 us -> 27.8 us
  starting transfers between devices: 16.4 us -> 27.7 us
  waiting for transfers between devices: 16.1 us -> 20.7 us
  local copies, waits for them, and re-layouts: 7.3 us -> 3.11 us
  Pallas kernels: 34.9 us -> 38.3 us
    all_to_all x1 -> x0, blocking collectives: 21.2 us -> none  [local(): lax.all_to_all(moments, 'elem', split_axis=0, concat_axis=0, tiled=True)]
    all_to_all x0 -> x1, starting transfers between devices: none -> 11.4 us  [local(): lax.all_to_all(moments, 'elem', split_axis=0, concat_axis=0, tiled=True)]
    all_to_all x0 -> x1, waiting for transfers between devices: none -> 4.68 us  [local(): lax.all_to_all(moments, 'elem', split_axis=0, concat_axis=0, tiled=True)]
    pallas_call x2 -> x3, Pallas kernels: 9.8 us -> 13.2 us  [the longest x1 4.99 us: unpack(): pl.pallas_call(unpack_body, grid=(3,), in_specs=[vector] * 3, out_specs=[...]
    pallas_call x1 -> x0, local copies, waits for them, and re-layouts: 2.67 us -> none  [combine(): pl.pallas_call(combine_body, grid=(3,), in_specs=[pl.BlockSpec(moments.sh...]
    unnamed x12 -> x13, local copies, waits for them, and re-layouts: 4.61 us -> 3.09 us
  transfers between devices with their start and end apart: 3 -> 4, of which waited for: 3 -> 4; matrix products, arithmetic and copies ran while one was open for 1% -> 1% of each run, Pallas kernels for 6% -> 10%
where the time goes in v2:
time: 120 us; the launch traced here: 119 us
  Pallas kernels  38.3 us (32%)
  blocking collectives  27.8 us (23%)
  starting transfers between devices  27.7 us (23%)
  waiting for transfers between devices  20.7 us (17%)
  local copies, waits for them, and re-layouts  3.11 us (3%)
    all_to_all x1, blocking collectives, local(): lax.all_to_all(source, 'four', split_axis=0, concat_axis=0, tiled=True)  27.8 us
    pallas_call x1, Pallas kernels, krylov_stage(): pl.pallas_call(body, grid=(3,), in_specs=[smem, smem, chunk(COLUMNS), chu...  12.3 us
    all_to_all x1, waiting for transfers between devices, local(): lax.all_to_all(send, 'four', split_axis=0, concat_axis=0, tiled=True)  11.5 us
    all_to_all x1, starting transfers between devices, local(): lax.all_to_all(moments, 'elem', split_axis=0, concat_axis=0, tiled=True)  11.4 us
    all_to_all x1, starting transfers between devices, local(): lax.all_to_all(send, 'four', split_axis=0, concat_axis=0, tiled=True)  10.4 us
    pallas_call x1, Pallas kernels, base_stage(): pl.pallas_call(base_body, grid=(6,), in_specs=[smem, smem, smem, pl.Block...  6.97 us
    pallas_call x1, Pallas kernels, lines_stage(): pl.pallas_call(lines_body, grid=(2,), in_specs=[smem, smem, smem, block,...  5.88 us
    pallas_call x1, Pallas kernels, unpack(): pl.pallas_call(unpack_body, grid=(3,), in_specs=[vector] * 3, out_specs=[...  4.99 us
  transfers between devices with their start and end apart: 4, of which 4 were waited for; matrix products, arithmetic and copies ran while one was open for 1% of the time, Pallas kernels for 10%

profile of v2, /device:TPU:8, one launch (start us, length us, event | category | flops | bytes accessed | tf_op | source)
XLA Modules:
  0.0 119.0 jit_solution(14183000689546284535)
XLA Ops:
  0.0 0.0 copy-start.3
  0.0 4.1 %pack.1 = f32[16,3,2,16,128]{4,3,2,1,0:T(8,128)} custom-call(f32[3,11,2,2816]{3,2,1,0:T(2,128)} %bitcast.3), custom_call_target="tpu_custom_call" | custom-call | tf_op jit(solution)/shard_map/pack/pallas_call | solution.py:150
  4.1 10.4 %all-to-all-start = ((f32[16,3,2,16,128]{4,3,2,1,0:T(8,128)}), f32[16,3,2,16,128]{4,3,2,1,0:T(8,128)S(1)}, u32[]{:S(2)}, u32[]{:S(2)}) async-start(f32[16,3,2,16,128]{4,3,2,1,0:T(8,128)} %pack.1), calls=%async_computation | async-start | bytes 1572864 | tf_op jit(solution)/shard_map/all_to_all | solution.py:605
  15.2 0.0 copy-done.3
  15.2 0.9 copy.16.base_ref
  16.1 0.7 pad_add_fusion.ints.refs_0_
  16.7 7.0 %base_stage.1 = (f32[4,3,2,256,128]{4,3,2,1,0:T(8,128)}, bf16[512,256]{1,0:T(8,128)(2,1)}, bf16[512,256]{1,0:T(8,128)(2,1)}, bf16[256,256]{1,0:T(8,128)(2,1)}, bf16[256,256]{1,0:T(8,128)(2,1)}) custom-call(s32[2]{0:T(128)} %pad_add_fusion.ints.refs_0_, f32[16]{0:T(128)} %widths.3, f32[2]{0:T(128)} %refs_1_.1, bf16[3,2,11,2816]{3,2,1,0:T(8,128)(2,1)} %copy.16.base_ref, ...), custom_call_target="tpu_custom_call" | custom-call | tf_op jit(solution)/shard_map/base_stage/pallas_call | solution.py:202
  23.7 11.5 %all-to-all-done.in_ref = f32[16,3,2,16,128]{4,3,2,1,0:T(8,128)S(1)} async-done(((f32[16,3,2,16,128]{4,3,2,1,0:T(8,128)}), f32[16,3,2,16,128]{4,3,2,1,0:T(8,128)S(1)}, u32[]{:S(2)}, u32[]{:S(2)}) %all-to-all-start) | async-done | bytes 786464 | tf_op jit(solution)/shard_map/all_to_all | solution.py:605
  35.3 0.9 copy-done.1
  36.2 5.9 %lines_stage.1 = f32[16,3,2,16,128]{4,3,2,1,0:T(8,128)} custom-call(s32[2]{0:T(128)} %pad_add_fusion.ints.refs_0_, f32[16]{0:T(128)} %widths.3, f32[2]{0:T(128)} %refs_1_.1, f32[16,3,2,16,128]{4,3,2,1,0:T(8,128)} %copy-done.1, f32[4,3,2,256,128]{4,3,2,1,0:T(8,128)} %get-tuple-element.17.field_ref, bf16[512,256]{1,0:T(8,128)(2,1)} %get-tuple-element.18.fgh_ref, ...), custom_call_target="tpu_custom_call" | custom-call | tf_op jit(solution)/shard_map/lines_stage/pallas_call | solution.py:266
  42.0 27.8 %all_to_all.15.refs_2_ = f32[16,3,2,16,128]{4,3,2,1,0:T(8,128)S(1)} all-to-all(f32[16,3,2,16,128]{4,3,2,1,0:T(8,128)} %lines_stage.1), channel_id=1, replica_groups=mesh['elem'=32,'four'=16] {'four'}, dimensions={0} | all-to-all | bytes 1572864 | tf_op jit(solution)/shard_map/all_to_all | solution.py:614
  69.8 2.4 %collective-permute-start.1 = (f32[3,3,2,16,128]{4,3,2,1,0:T(8,128)S(1)}, f32[3,3,2,16,128]{4,3,2,1,0:T(8,128)S(1)}, u32[]{:S(2)}, u32[]{:S(2)}) collective-permute-start(f32[3,3,2,16,128]{4,3,2,1,0:T(8,128)S(1)} %get-tuple-element.29), channel_id=1, source_target_pairs={{16,0},{32,16},{48,32},{64,48},{80,64},{96,80},{112,96},{128,112},... | collective-permute-start | bytes 442376 | tf_op jit(solution)/shard_map/ppermute | solution.py:617
  72.2 3.5 %collective-permute-start = (f32[3,3,2,16,128]{4,3,2,1,0:T(8,128)S(1)}, f32[3,3,2,16,128]{4,3,2,1,0:T(8,128)S(1)}, u32[]{:S(2)}, u32[]{:S(2)}) collective-permute-start(f32[3,3,2,16,128]{4,3,2,1,0:T(8,128)S(1)} %get-tuple-element.30), channel_id=1, source_target_pairs={{0,16},{16,32},{32,48},{48,64},{64,80},{80,96},{96,112},{112,128},... | collective-permute-start | bytes 442376 | tf_op jit(solution)/shard_map/ppermute | solution.py:616
  75.7 2.4 %collective-permute-done.1.refs_4_ = f32[3,3,2,16,128]{4,3,2,1,0:T(8,128)S(1)} collective-permute-done((f32[3,3,2,16,128]{4,3,2,1,0:T(8,128)S(1)}, f32[3,3,2,16,128]{4,3,2,1,0:T(8,128)S(1)}, u32[]{:S(2)}, u32[]{:S(2)}) %collective-permute-start.1) | collective-permute-done | bytes 147488 | tf_op jit(solution)/shard_map/ppermute | solution.py:617
  78.1 2.1 %collective-permute-done.refs_3_ = f32[3,3,2,16,128]{4,3,2,1,0:T(8,128)S(1)} collective-permute-done((f32[3,3,2,16,128]{4,3,2,1,0:T(8,128)S(1)}, f32[3,3,2,16,128]{4,3,2,1,0:T(8,128)S(1)}, u32[]{:S(2)}, u32[]{:S(2)}) %collective-permute-start) | collective-permute-done | bytes 147488 | tf_op jit(solution)/shard_map/ppermute | solution.py:616
  80.2 0.0 copy-done
  80.2 0.0 copy-done.4
  80.2 0.7 copy-done.5
  80.9 12.3 %krylov_stage.1 = (f32[3,336,256]{2,1,0:T(8,128)}, f32[3,336,256]{2,1,0:T(8,128)}, f32[3,336,256]{2,1,0:T(8,128)}, f32[32,8,128]{2,1,0:T(8,128)}) custom-call(s32[2]{0:T(128)} %pad_add_fusion.ints.refs_0_, f32[2]{0:T(128)} %refs_1_.1, f32[16,3,2,16,128]{4,3,2,1,0:T(8,128)} %copy-done, f32[3,3,2,16,128]{4,3,2,1,0:T(8,128)} %copy-done.5, ...), custom_call_target="tpu_custom_call" | custom-call | tf_op jit(solution)/shard_map/krylov_stage/pallas_call | solution.py:427
  93.2 11.4 %all-to-all-start.2 = ((f32[32,8,128]{2,1,0:T(8,128)}), f32[32,8,128]{2,1,0:T(8,128)S(1)}, u32[]{:S(2)}, u32[]{:S(2)}) async-start(f32[32,8,128]{2,1,0:T(8,128)} %get-tuple-element.22), calls=%async_computation.2 | async-start | bytes 262144 | tf_op jit(solution)/shard_map/all_to_all | solution.py:622
  104.6 5.0 %unpack.1 = (f32[3,11,2,2816]{3,2,1,0:T(2,128)}, f32[3,11,2,2816]{3,2,1,0:T(2,128)}, f32[3,11,2,2816]{3,2,1,0:T(2,128)}) custom-call(f32[3,336,256]{2,1,0:T(8,128)} %get-tuple-element.23.v0_ref, f32[3,336,256]{2,1,0:T(8,128)} %get-tuple-element.24.v1_ref, f32[3,336,256]{2,1,0:T(8,128)} %get-tuple-element.25.v2_ref), custom_call_target="tpu_custom_call" | custom-call | tf_op jit(solution)/shard_map/unpack/pallas_call | solution.py:480
  109.6 4.7 %all-to-all-done.2.mom_ref = f32[32,8,128]{2,1,0:T(8,128)S(1)} async-done(((f32[32,8,128]{2,1,0:T(8,128)}), f32[32,8,128]{2,1,0:T(8,128)S(1)}, u32[]{:S(2)}, u32[]{:S(2)}) %all-to-all-start.2) | async-done | bytes 131104 | tf_op jit(solution)/shard_map/all_to_all | solution.py:622
  114.3 0.7 copy-done.2
  114.9 4.1 %finish.1 = f32[3,11,2,2816]{3,2,1,0:T(2,128)} custom-call(f32[32,8,128]{2,1,0:T(8,128)} %copy-done.2, f32[3,11,2,2816]{3,2,1,0:T(2,128)} %get-tuple-element.26.u0_ref, f32[3,11,2,2816]{3,2,1,0:T(2,128)} %get-tuple-element.27.u1_ref, f32[3,11,2,2816]{3,2,1,0:T(2,128)} %get-tuple-element.28.u2_ref), custom_call_target="tpu_custom_call" | custom-call | tf_op jit(solution)/shard_map/finish/pallas_call | solution.py:547
  (6 shorter events, 0.0 us)
Async XLA Ops:
  0.0 15.2 %copy-start.3 = (bf16[3,2,11,2816]{3,1,2,0:T(2,128)(2,1)S(1)}, bf16[3,2,11,2816]{3,1,2,0:T(2,128)(2,1)}, u32[]{:S(2)}) copy-start(bf16[3,2,11,2816]{3,1,2,0:T(2,128)(2,1)} %param.16) | copy-start | bytes 1115140
  4.1 31.1 %all-to-all-start = ((f32[16,3,2,16,128]{4,3,2,1,0:T(8,128)}), f32[16,3,2,16,128]{4,3,2,1,0:T(8,128)S(1)}, u32[]{:S(2)}, u32[]{:S(2)}) async-start(f32[16,3,2,16,128]{4,3,2,1,0:T(8,128)} %pack.1), calls=%async_computation | async-start | bytes 1572864 | tf_op jit(solution)/shard_map/all_to_all | solution.py:605
  35.2 0.9 copy-start.1
  69.8 10.4 %copy-start = (f32[16,3,2,16,128]{4,3,2,1,0:T(8,128)}, f32[16,3,2,16,128]{4,3,2,1,0:T(8,128)S(1)}, u32[]{:S(2)}) copy-start(f32[16,3,2,16,128]{4,3,2,1,0:T(8,128)S(1)} %all_to_all.15.refs_2_) | copy-start | bytes 2359300
  69.8 8.3 %collective-permute-start.1 = (f32[3,3,2,16,128]{4,3,2,1,0:T(8,128)S(1)}, f32[3,3,2,16,128]{4,3,2,1,0:T(8,128)S(1)}, u32[]{:S(2)}, u32[]{:S(2)}) collective-permute-start(f32[3,3,2,16,128]{4,3,2,1,0:T(8,128)S(1)} %get-tuple-element.29), channel_id=1, source_target_pairs={{16,0},{32,16},{48,32},{64,48},{80,64},{96,80},{112,96},{128,112},... | collective-permute-start | bytes 442376 | tf_op jit(solution)/shard_map/ppermute | solution.py:617
  72.2 8.0 %collective-permute-start = (f32[3,3,2,16,128]{4,3,2,1,0:T(8,128)S(1)}, f32[3,3,2,16,128]{4,3,2,1,0:T(8,128)S(1)}, u32[]{:S(2)}, u32[]{:S(2)}) collective-permute-start(f32[3,3,2,16,128]{4,3,2,1,0:T(8,128)S(1)} %get-tuple-element.30), channel_id=1, source_target_pairs={{0,16},{16,32},{32,48},{48,64},{64,80},{80,96},{96,112},{112,128},... | collective-permute-start | bytes 442376 | tf_op jit(solution)/shard_map/ppermute | solution.py:616
  78.1 2.1 %copy-start.4 = (f32[3,3,2,16,128]{4,3,2,1,0:T(8,128)}, f32[3,3,2,16,128]{4,3,2,1,0:T(8,128)S(1)}, u32[]{:S(2)}) copy-start(f32[3,3,2,16,128]{4,3,2,1,0:T(8,128)S(1)} %collective-permute-done.1.refs_4_) | copy-start | bytes 442372
  80.2 0.7 copy-start.5
  93.2 21.1 %all-to-all-start.2 = ((f32[32,8,128]{2,1,0:T(8,128)}), f32[32,8,128]{2,1,0:T(8,128)S(1)}, u32[]{:S(2)}, u32[]{:S(2)}) async-start(f32[32,8,128]{2,1,0:T(8,128)} %get-tuple-element.22), calls=%async_computation.2 | async-start | bytes 262144 | tf_op jit(solution)/shard_map/all_to_all | solution.py:622
  114.3 0.7 copy-start.2

commit v3 on v2

--- a/solution.py
+++ b/solution.py
@@ -276,8 +276,67 @@
     )(ints, widths, heights, arrived, fields, *tables, d_high, d_low, mass)
 
 
-def krylov_body(stiff_y, weights, ints, heights, own_ref, left_ref, right_ref, kb_ref, join_ref, wx_ref,
-                v0_ref, v1_ref, v2_ref, mom_ref, loc, kxs, kbs, vec, prod, tmp):
+def join_columns(chunks):
+    lane = lane_ids(chunks[0].shape)
+    place = lane - Q * ((lane * 5958) >> 16)
+    at_first = (place == 0) & (lane < NODES)
+    at_last = (place == Q - 1) & (lane < NODES)
+    results = []
+    for k, chunk in enumerate(chunks):
+        if chunk is None:
+            results.append(None)
+            continue
+        extra = 0.0
+        if k > 0 and chunks[k - 1] is not None:
+            extra = jnp.where(at_first, turn(chunks[k - 1], -(Q - 1)), extra)
+        if k + 1 < len(chunks) and chunks[k + 1] is not None:
+            extra = jnp.where(at_last, turn(chunks[k + 1], Q - 1), extra)
+        results.append(chunk + extra)
+    return results
+
+
+def split3(value):
+    high = value.astype(BF16)
+    rest = value - high.astype(F32)
+    mid = rest.astype(BF16)
+    return high, mid, (rest - mid.astype(F32)).astype(BF16)
+
+
+def dot_split(value, parts):
+    high, mid, low = split3(value)
+    total = dot(low, parts[0]) + dot(high, parts[2])
+    total = total + dot(mid, parts[1])
+    total = total + dot(mid, parts[0]) + dot(high, parts[1])
+    return total + dot(high, parts[0])
+
+
+def stiff_rows(stiff, values):
+    middle = Q // 2
+    even = [values[m] + values[Q - 1 - m] for m in range(middle)] + [values[middle]]
+    odd = [values[m] - values[Q - 1 - m] for m in range(middle)]
+    results = [None] * Q
+    for row in range(middle + 1):
+        total = None
+        for m in range(middle + 1):
+            factor = stiff[row][m] if m == middle or row == middle else (
+                0.5 * (stiff[row][m] + stiff[row][Q - 1 - m])
+            )
+            term = factor * even[m]
+            total = term if total is None else total + term
+        if row == middle:
+            results[row] = total
+            continue
+        other = None
+        for m in range(middle):
+            term = (0.5 * (stiff[row][m] - stiff[row][Q - 1 - m])) * odd[m]
+            other = term if other is None else other + term
+        results[row] = total + other
+        results[Q - 1 - row] = total - other
+    return results
+
+
+def krylov_body(stiff_y, weights, ints, heights, own_ref, left_ref, right_ref, kb_ref, kn_ref, wx_ref,
+                v0_ref, v1_ref, v2_ref, mom_ref, kxs, kbs, vec, prod, tmp):
     comp = pl.program_id(0)
     column_refs = (
         [left_ref.at[k] for k in range(GHOST)]
@@ -288,120 +347,115 @@
     @pl.when(comp == 0)
     def _():
         lane = lane_ids((8, LANES))
+        widths = [ref[0, 0, 0:8, NODES : NODES + 1] for ref in column_refs]
+        zero = jnp.zeros((8, 1), F32)
+        widths = [zero] + widths + [zero]
         for t in range(2):
             here = jnp.zeros((8, LANES), F32)
+            near = here
             for place in range(Q):
-                width = column_refs[Q * t + place][0, 0, 0:8, NODES : NODES + 1]
-                inside = (lane >= Q * place) & (lane < Q * place + Q)
-                here = jnp.where(inside, width, here)
+                k = Q * t + place + 1
+                low, high = Q * place, Q * place + Q - 1
+                here = jnp.where((lane >= low) & (lane <= high), widths[k], here)
+                near = jnp.where(lane == low, widths[k - 1], near)
+                near = jnp.where(lane == high, widths[k + 1], near)
             vec[0, :, t * LANES : (t + 1) * LANES] = here
-        here = vec[0]
-        inverse = jnp.where(here > 0.0, 1.0 / jnp.where(here > 0.0, here, 1.0), 0.0)
+            vec[1, :, t * LANES : (t + 1) * LANES] = near
+        here, near = vec[0], vec[1]
         line = lane_ids((8, 2 * LANES))
         own = ((line >= GHOST * Q) & (line < NODES)) | (
             (line >= LANES) & (line < LANES + (Q - GHOST) * Q)
         )
         own = own.astype(F32)
         mass_x = here * wx_ref[...]
-        vec[1] = dot_full(mass_x, join_ref[...])
         vec[2] = mass_x * own
-        place = jnp.where(line >= LANES, line - LANES, line)
-        place = place - Q * ((place * 5958) >> 16)
-        edge = (place == 0) | (place == Q - 1)
-        left_end = (line == GHOST * Q) & (pltpu.roll(here, 1, 1) == 0.0)
-        right_end = (line == LANES + (Q - GHOST) * Q - 1) & (
-            pltpu.roll(here, 2 * LANES - 1, 1) == 0.0
+        vec[1] = mass_x + near * wx_ref[...]
+        vec[3] = own * jnp.where(near > 0.0, 0.5, 1.0)
+        inverse, inverse_near = (
+            jnp.where(value > 0.0, 1.0 / jnp.where(value > 0.0, value, 1.0), 0.0)[0:1]
+            for value in (here, near)
         )
-        shared = edge & jnp.logical_not(left_end | right_end)
-        vec[3] = own * jnp.where(shared, 0.5, 1.0)
-        scaled = kb_ref[...] * inverse[0:1]
-        kxs[...] = dot_full(scaled, join_ref[...])
-        kbs[...] = scaled * own[0:1]
-
-    for t in range(2):
-        before = None
-        for ey in range(2):
-            chunks = [column_refs[Q * t + place][0, ey] for place in range(Q)]
-            placed = block_transpose(chunks, Q)
+        scaled = kb_ref[...] * inverse
+        for k, part in enumerate(split3(scaled + kn_ref[...] * inverse_near)):
+            kxs[k] = part
+        for k, part in enumerate(split3(scaled * own[0:1])):
+            kbs[k] = part
+
+    first, second, third = v0_ref.at[0], v1_ref.at[0], v2_ref.at[0]
+    before = [None, None]
+    for ey in range(2):
+        chunks = join_columns([ref[0, ey] for ref in column_refs])
+        for t in range(2):
+            placed = block_transpose(chunks[Q * t : Q * t + Q], Q)
             for qy in range(Q):
                 value = placed[qy]
                 y = qy + (Q - 1) * ey
                 if ey == 0 and qy == Q - 1:
-                    before = value
+                    before[t] = value
                     continue
                 if ey == 1 and qy == 0:
-                    value = value + before
-                loc[y * LOCAL : (y + 1) * LOCAL, t * LANES : (t + 1) * LANES] = value
+                    value = value + before[t]
+                first[y * LOCAL : (y + 1) * LOCAL, t * LANES : (t + 1) * LANES] = value
 
     h0, h1 = heights[0], heights[1]
-    inv0, inv1 = 1.0 / h0, 1.0 / h1
+    inverse_y = (1.0 / h0, 1.0 / h1)
     mass_y = []
     for y in range(ROWS):
         if y < Q - 1:
             mass_y.append(h0 * weights[y])
         elif y == Q - 1:
-            mass_y.append(h0 * weights[y] + h1 * weights[0])
+            mass_y.append((h0 + h1) * weights[0])
         else:
             mass_y.append(h1 * weights[y - Q + 1])
 
-    def products(source_ref, body):
+    def apply(source, target, operator, mass_row, low_key):
+        tmp[...] = dot_split(source[...], [operator[k] for k in range(3)])
+        sums = [[], []]
         for half in range(2):
             plane = ints[0] * LOCAL + half * 8 + lax.broadcasted_iota(jnp.int32, (8, LANES), 0)
             kappa = jnp.where(plane == 1, PLANES // 2, plane >> 1).astype(F32)
             beta = kappa * (2.0 * np.pi / (PLANES / 64.0))
             lam = (beta * beta + SIGMA) * 0.25
+            square = cross = None
             for t in range(2):
-                rows = [pl.ds(y * LOCAL + half * 8, 8) for y in range(ROWS)]
-                lanes = pl.ds(t * LANES, LANES)
-                values = [source_ref[r, lanes] for r in rows]
-                for y in range(ROWS):
-                    total = (lam * mass_y[y]) * values[y]
-                    if y <= Q - 1:
-                        inner = stiff_y[y][0] * values[0]
-                        for m in range(1, Q):
-                            inner = inner + stiff_y[y][m] * values[m]
-                        total = total + inv0 * inner
-                    if y >= Q - 1:
-                        inner = stiff_y[y - Q + 1][0] * values[Q - 1]
-                        for m in range(1, Q):
-                            inner = inner + stiff_y[y - Q + 1][m] * values[Q - 1 + m]
-                        total = total + inv1 * inner
-                    body(half, t, y, rows[y], lanes, values[y], total)
-
-    first, second, third = v0_ref.at[0], v1_ref.at[0], v2_ref.at[0]
-    first[...] = dot_full(loc[...], join_ref[...])
-    sums = {}
-
-    def add(key, half, t, value):
-        key = (key, half, t)
-        sums[key] = value if key not in sums else sums[key] + value
-
-    def step(target, low_key, previous):
-        def body(half, t, y, r, lanes, value, total):
-            image = mass_y[y] * tmp[r, lanes] + vec[1, :, lanes] * total
-            target[r, lanes] = image
-            weighted = value * vec[3, :, lanes]
-            add(low_key, half, t, weighted * value)
-            add(low_key + 1, half, t, weighted * image)
-        return body
-
-    def last(half, t, y, r, lanes, value, total):
-        image = mass_y[y] * tmp[r, lanes] + vec[2, :, lanes] * total
-        add(4, half, t, value * vec[3, :, lanes] * value)
-        add(5, half, t, value * image)
-
-    tmp[...] = dot_full(first[...], kxs[...])
-    products(first, step(second, 0, None))
-    tmp[...] = dot_full(second[...], kxs[...])
-    products(second, step(third, 2, None))
-    tmp[...] = dot_full(third[...], kbs[...])
-    products(third, last)
-    prod[...] = jnp.zeros_like(prod)
-    for key in range(6):
-        for half in range(2):
-            prod[key * LOCAL + half * 8 : key * LOCAL + half * 8 + 8, :] = (
-                sums[(key, half, 0)] + sums[(key, half, 1)]
-            )
+                lanes = slice(t * LANES, (t + 1) * LANES)
+                mass_x = vec[mass_row, :, lanes]
+                shift = lam * mass_x
+                weight = vec[3, :, lanes]
+                here_square = here_cross = None
+                shared = None
+                for ey in range(2):
+                    rows = [
+                        slice(y * LOCAL + half * 8, y * LOCAL + half * 8 + 8)
+                        for y in range((Q - 1) * ey, (Q - 1) * ey + Q)
+                    ]
+                    values = [source[r, lanes] for r in rows]
+                    scale = mass_x * inverse_y[ey]
+                    stiff = [scale * value for value in stiff_rows(stiff_y, values)]
+                    if ey == 0:
+                        shared = stiff.pop()
+                    else:
+                        stiff[0] = stiff[0] + shared
+                    for k, part in enumerate(stiff):
+                        y, value = (Q - 1) * ey + k, values[k]
+                        image = mass_y[y] * (tmp[rows[k], lanes] + shift * value) + part
+                        if target is not None:
+                            target[rows[k], lanes] = image
+                        one, two = value * value, value * image
+                        here_square = one if here_square is None else here_square + one
+                        here_cross = two if here_cross is None else here_cross + two
+                here_square = here_square * weight
+                if target is not None:
+                    here_cross = here_cross * weight
+                square = here_square if square is None else square + here_square
+                cross = here_cross if cross is None else cross + here_cross
+            prod[low_key * LOCAL + half * 8 : low_key * LOCAL + half * 8 + 8, :] = square
+            prod[(low_key + 1) * LOCAL + half * 8 : (low_key + 1) * LOCAL + half * 8 + 8, :] = cross
+
+    prod[6 * LOCAL :, :] = jnp.zeros((LANES - 6 * LOCAL, LANES), F32)
+    apply(first, second, kxs, 1, 0)
+    apply(second, third, kxs, 1, 2)
+    apply(third, None, kbs, 2, 4)
     row = lax.dot_general(
         jnp.ones((8, LANES), F32), prod[...], (((1,), (1,)), ((), ())),
         precision=HIGHEST, preferred_element_type=F32,
@@ -409,7 +463,7 @@
     mom_ref[:, pl.ds(comp, 1), :] = jnp.broadcast_to(row[0:1][None], (mom_ref.shape[0], 1, LANES))
 
 
-def krylov_stage(stiff_y, weights, ints, heights, own, left, right, kb, join, wx, peers):
+def krylov_stage(stiff_y, weights, ints, heights, own, left, right, kb, near, wx, peers):
     smem = pl.BlockSpec(memory_space=pltpu.SMEM)
 
     def whole(array):
@@ -427,19 +481,18 @@
     return pl.pallas_call(
         body,
         grid=(3,),
-        in_specs=[smem, smem, chunk(COLUMNS), chunk(GHOST), chunk(GHOST), whole(kb), whole(join), whole(wx)],
+        in_specs=[smem, smem, chunk(COLUMNS), chunk(GHOST), chunk(GHOST), whole(kb), whole(near), whole(wx)],
         out_specs=[vector, vector, vector, pl.BlockSpec((peers, 8, LANES), lambda i: (0, 0, 0))],
         out_shape=[shape, shape, shape, jax.ShapeDtypeStruct((peers, 8, LANES), F32)],
         scratch_shapes=[
-            pltpu.VMEM((ROWS * LOCAL, 2 * LANES), F32),
-            pltpu.VMEM((2 * LANES, 2 * LANES), F32),
-            pltpu.VMEM((2 * LANES, 2 * LANES), F32),
+            pltpu.VMEM((3, 2 * LANES, 2 * LANES), BF16),
+            pltpu.VMEM((3, 2 * LANES, 2 * LANES), BF16),
             pltpu.VMEM((4, 8, 2 * LANES), F32),
             pltpu.VMEM((LANES, LANES), F32),
             pltpu.VMEM((ROWS * LOCAL, 2 * LANES), F32),
         ],
         name="krylov_stage",
-    )(ints, heights, own, left, right, kb, join, wx)
+    )(ints, heights, own, left, right, kb, near, wx)
 
 
 def unpack_body(v0_ref, v1_ref, v2_ref, u0_ref, u1_ref, u2_ref, scr, flat):
@@ -588,11 +641,9 @@
     for left, right in zip(ends[:-1], ends[1:]):
         join[left + Q - 1, right] = 1.0
         join[right, left + Q - 1] = 1.0
-    for t in range(2):
-        join[t * LANES + NODES : (t + 1) * LANES] = 0.0
     return dict(
         table=table, stack=stack, dz=halves(span_slope), plane=halves(plane), mass=mass,
-        kb=kb.astype(np.float32), join=join.astype(np.float32), wx=wx,
+        kb=kb.astype(np.float32), near=(kb @ join - kb).astype(np.float32), wx=wx,
         stiff=stiff.tolist(), weights=weights.tolist(),
     )
 
@@ -617,7 +668,7 @@
     right = lax.ppermute(own[:GHOST], "elem", [(j, i) for i, j in up])
     v0, v1, v2, moments = krylov_stage(
         tables["stiff"], tables["weights"], ints, row_heights, own, left, right,
-        jnp.asarray(tables["kb"]), jnp.asarray(tables["join"]), jnp.asarray(tables["wx"]), elem_count,
+        jnp.asarray(tables["kb"]), jnp.asarray(tables["near"]), jnp.asarray(tables["wx"]), elem_count,
     )
     moments = lax.all_to_all(moments, "elem", split_axis=0, concat_axis=0, tiled=True)
     return finish(moments, *unpack(v0, v1, v2))

time: 120 us -> 117 us (0.975)
  Pallas kernels: 38.3 us -> 35.5 us
    pallas_call x1, Pallas kernels: 12.3 us -> 9.44 us  [krylov_stage(): pl.pallas_call(body, grid=(3,), in_specs=[smem, smem, chunk(COLUMNS), chu...]
where the time goes in v3:
time: 117 us; the launch traced here: 116 us
  Pallas kernels  35.5 us (30%)
  blocking collectives  27.8 us (24%)
  starting transfers between devices  27.7 us (24%)
  waiting for transfers between devices  20.7 us (18%)
  local copies, waits for them, and re-layouts  3.11 us (3%)
    all_to_all x1, blocking collectives, local(): lax.all_to_all(source, 'four', split_axis=0, concat_axis=0, tiled=True)  27.8 us
    all_to_all x1, waiting for transfers between devices, local(): lax.all_to_all(send, 'four', split_axis=0, concat_axis=0, tiled=True)  11.5 us
    all_to_all x1, starting transfers between devices, local(): lax.all_to_all(moments, 'elem', split_axis=0, concat_axis=0, tiled=True)  11.4 us
    all_to_all x1, starting transfers between devices, local(): lax.all_to_all(send, 'four', split_axis=0, concat_axis=0, tiled=True)  10.4 us
    pallas_call x1, Pallas kernels, krylov_stage(): pl.pallas_call(body, grid=(3,), in_specs=[smem, smem, chunk(COLUMNS), chu...  9.44 us
    pallas_call x1, Pallas kernels, base_stage(): pl.pallas_call(base_body, grid=(6,), in_specs=[smem, smem, smem, pl.Block...  6.97 us
    pallas_call x1, Pallas kernels, lines_stage(): pl.pallas_call(lines_body, grid=(2,), in_specs=[smem, smem, smem, block,...  5.88 us
    pallas_call x1, Pallas kernels, unpack(): pl.pallas_call(unpack_body, grid=(3,), in_specs=[vector] * 3, out_specs=[...  4.99 us
  transfers between devices with their start and end apart: 4, of which 4 were waited for; matrix products, arithmetic and copies ran while one was open for 1% of the time, Pallas kernels for 10%

profile of v3, /device:TPU:8, one launch (start us, length us, event | category | flops | bytes accessed | tf_op | source)
XLA Modules:
  0.0 116.1 jit_solution(1650156140046364622)
XLA Ops:
  0.0 0.0 copy-start.3
  0.0 4.1 %pack.1 = f32[16,3,2,16,128]{4,3,2,1,0:T(8,128)} custom-call(f32[3,11,2,2816]{3,2,1,0:T(2,128)} %bitcast.3), custom_call_target="tpu_custom_call" | custom-call | tf_op jit(solution)/shard_map/pack/pallas_call | solution.py:150
  4.1 10.4 %all-to-all-start = ((f32[16,3,2,16,128]{4,3,2,1,0:T(8,128)}), f32[16,3,2,16,128]{4,3,2,1,0:T(8,128)S(1)}, u32[]{:S(2)}, u32[]{:S(2)}) async-start(f32[16,3,2,16,128]{4,3,2,1,0:T(8,128)} %pack.1), calls=%async_computation | async-start | bytes 1572864 | tf_op jit(solution)/shard_map/all_to_all | solution.py:656
  15.2 0.0 copy-done.3
  15.2 0.9 copy.16.base_ref
  16.1 0.7 pad_add_fusion.ints.refs_0_
  16.7 7.0 %base_stage.1 = (f32[4,3,2,256,128]{4,3,2,1,0:T(8,128)}, bf16[512,256]{1,0:T(8,128)(2,1)}, bf16[512,256]{1,0:T(8,128)(2,1)}, bf16[256,256]{1,0:T(8,128)(2,1)}, bf16[256,256]{1,0:T(8,128)(2,1)}) custom-call(s32[2]{0:T(128)} %pad_add_fusion.ints.refs_0_, f32[16]{0:T(128)} %widths.3, f32[2]{0:T(128)} %refs_1_.1, bf16[3,2,11,2816]{3,2,1,0:T(8,128)(2,1)} %copy.16.base_ref, ...), custom_call_target="tpu_custom_call" | custom-call | tf_op jit(solution)/shard_map/base_stage/pallas_call | solution.py:202
  23.7 11.5 %all-to-all-done.in_ref = f32[16,3,2,16,128]{4,3,2,1,0:T(8,128)S(1)} async-done(((f32[16,3,2,16,128]{4,3,2,1,0:T(8,128)}), f32[16,3,2,16,128]{4,3,2,1,0:T(8,128)S(1)}, u32[]{:S(2)}, u32[]{:S(2)}) %all-to-all-start) | async-done | bytes 786464 | tf_op jit(solution)/shard_map/all_to_all | solution.py:656
  35.3 0.9 copy-done.1
  36.2 5.9 %lines_stage.1 = f32[16,3,2,16,128]{4,3,2,1,0:T(8,128)} custom-call(s32[2]{0:T(128)} %pad_add_fusion.ints.refs_0_, f32[16]{0:T(128)} %widths.3, f32[2]{0:T(128)} %refs_1_.1, f32[16,3,2,16,128]{4,3,2,1,0:T(8,128)} %copy-done.1, f32[4,3,2,256,128]{4,3,2,1,0:T(8,128)} %get-tuple-element.17.field_ref, bf16[512,256]{1,0:T(8,128)(2,1)} %get-tuple-element.18.fgh_ref, ...), custom_call_target="tpu_custom_call" | custom-call | tf_op jit(solution)/shard_map/lines_stage/pallas_call | solution.py:266
  42.0 27.8 %all_to_all.15.refs_2_ = f32[16,3,2,16,128]{4,3,2,1,0:T(8,128)S(1)} all-to-all(f32[16,3,2,16,128]{4,3,2,1,0:T(8,128)} %lines_stage.1), channel_id=1, replica_groups=mesh['elem'=32,'four'=16] {'four'}, dimensions={0} | all-to-all | bytes 1572864 | tf_op jit(solution)/shard_map/all_to_all | solution.py:665
  69.8 2.4 %collective-permute-start.1 = (f32[3,3,2,16,128]{4,3,2,1,0:T(8,128)S(1)}, f32[3,3,2,16,128]{4,3,2,1,0:T(8,128)S(1)}, u32[]{:S(2)}, u32[]{:S(2)}) collective-permute-start(f32[3,3,2,16,128]{4,3,2,1,0:T(8,128)S(1)} %get-tuple-element.29), channel_id=1, source_target_pairs={{16,0},{32,16},{48,32},{64,48},{80,64},{96,80},{112,96},{128,112},... | collective-permute-start | bytes 442376 | tf_op jit(solution)/shard_map/ppermute | solution.py:668
  72.2 3.5 %collective-permute-start = (f32[3,3,2,16,128]{4,3,2,1,0:T(8,128)S(1)}, f32[3,3,2,16,128]{4,3,2,1,0:T(8,128)S(1)}, u32[]{:S(2)}, u32[]{:S(2)}) collective-permute-start(f32[3,3,2,16,128]{4,3,2,1,0:T(8,128)S(1)} %get-tuple-element.30), channel_id=1, source_target_pairs={{0,16},{16,32},{32,48},{48,64},{64,80},{80,96},{96,112},{112,128},... | collective-permute-start | bytes 442376 | tf_op jit(solution)/shard_map/ppermute | solution.py:667
  75.7 2.4 %collective-permute-done.1.refs_4_ = f32[3,3,2,16,128]{4,3,2,1,0:T(8,128)S(1)} collective-permute-done((f32[3,3,2,16,128]{4,3,2,1,0:T(8,128)S(1)}, f32[3,3,2,16,128]{4,3,2,1,0:T(8,128)S(1)}, u32[]{:S(2)}, u32[]{:S(2)}) %collective-permute-start.1) | collective-permute-done | bytes 147488 | tf_op jit(solution)/shard_map/ppermute | solution.py:668
  78.1 2.1 %collective-permute-done.refs_3_ = f32[3,3,2,16,128]{4,3,2,1,0:T(8,128)S(1)} collective-permute-done((f32[3,3,2,16,128]{4,3,2,1,0:T(8,128)S(1)}, f32[3,3,2,16,128]{4,3,2,1,0:T(8,128)S(1)}, u32[]{:S(2)}, u32[]{:S(2)}) %collective-permute-start) | collective-permute-done | bytes 147488 | tf_op jit(solution)/shard_map/ppermute | solution.py:667
  80.2 0.0 copy-done
  80.2 0.0 copy-done.4
  80.2 0.7 copy-done.5
  80.9 9.4 %krylov_stage.1 = (f32[3,336,256]{2,1,0:T(8,128)}, f32[3,336,256]{2,1,0:T(8,128)}, f32[3,336,256]{2,1,0:T(8,128)}, f32[32,8,128]{2,1,0:T(8,128)}) custom-call(s32[2]{0:T(128)} %pad_add_fusion.ints.refs_0_, f32[2]{0:T(128)} %refs_1_.1, f32[16,3,2,16,128]{4,3,2,1,0:T(8,128)} %copy-done, f32[3,3,2,16,128]{4,3,2,1,0:T(8,128)} %copy-done.5, ...), custom_call_target="tpu_custom_call" | custom-call | tf_op jit(solution)/shard_map/krylov_stage/pallas_call | solution.py:481
  90.3 11.4 %all-to-all-start.2 = ((f32[32,8,128]{2,1,0:T(8,128)}), f32[32,8,128]{2,1,0:T(8,128)S(1)}, u32[]{:S(2)}, u32[]{:S(2)}) async-start(f32[32,8,128]{2,1,0:T(8,128)} %get-tuple-element.22), calls=%async_computation.2 | async-start | bytes 262144 | tf_op jit(solution)/shard_map/all_to_all | solution.py:673
  101.7 5.0 %unpack.1 = (f32[3,11,2,2816]{3,2,1,0:T(2,128)}, f32[3,11,2,2816]{3,2,1,0:T(2,128)}, f32[3,11,2,2816]{3,2,1,0:T(2,128)}) custom-call(f32[3,336,256]{2,1,0:T(8,128)} %get-tuple-element.23.v0_ref, f32[3,336,256]{2,1,0:T(8,128)} %get-tuple-element.24.v1_ref, f32[3,336,256]{2,1,0:T(8,128)} %get-tuple-element.25.v2_ref), custom_call_target="tpu_custom_call" | custom-call | tf_op jit(solution)/shard_map/unpack/pallas_call | solution.py:533
  106.7 4.7 %all-to-all-done.2.mom_ref = f32[32,8,128]{2,1,0:T(8,128)S(1)} async-done(((f32[32,8,128]{2,1,0:T(8,128)}), f32[32,8,128]{2,1,0:T(8,128)S(1)}, u32[]{:S(2)}, u32[]{:S(2)}) %all-to-all-start.2) | async-done | bytes 131104 | tf_op jit(solution)/shard_map/all_to_all | solution.py:673
  111.4 0.7 copy-done.2
  112.0 4.1 %finish.1 = f32[3,11,2,2816]{3,2,1,0:T(2,128)} custom-call(f32[32,8,128]{2,1,0:T(8,128)} %copy-done.2, f32[3,11,2,2816]{3,2,1,0:T(2,128)} %get-tuple-element.26.u0_ref, f32[3,11,2,2816]{3,2,1,0:T(2,128)} %get-tuple-element.27.u1_ref, f32[3,11,2,2816]{3,2,1,0:T(2,128)} %get-tuple-element.28.u2_ref), custom_call_target="tpu_custom_call" | custom-call | tf_op jit(solution)/shard_map/finish/pallas_call | solution.py:600
  (6 shorter events, 0.0 us)
Async XLA Ops:
  0.0 15.2 %copy-start.3 = (bf16[3,2,11,2816]{3,1,2,0:T(2,128)(2,1)S(1)}, bf16[3,2,11,2816]{3,1,2,0:T(2,128)(2,1)}, u32[]{:S(2)}) copy-start(bf16[3,2,11,2816]{3,1,2,0:T(2,128)(2,1)} %param.16) | copy-start | bytes 1115140
  4.1 31.1 %all-to-all-start = ((f32[16,3,2,16,128]{4,3,2,1,0:T(8,128)}), f32[16,3,2,16,128]{4,3,2,1,0:T(8,128)S(1)}, u32[]{:S(2)}, u32[]{:S(2)}) async-start(f32[16,3,2,16,128]{4,3,2,1,0:T(8,128)} %pack.1), calls=%async_computation | async-start | bytes 1572864 | tf_op jit(solution)/shard_map/all_to_all | solution.py:656
  35.2 0.9 copy-start.1
  69.8 10.4 %copy-start = (f32[16,3,2,16,128]{4,3,2,1,0:T(8,128)}, f32[16,3,2,16,128]{4,3,2,1,0:T(8,128)S(1)}, u32[]{:S(2)}) copy-start(f32[16,3,2,16,128]{4,3,2,1,0:T(8,128)S(1)} %all_to_all.15.refs_2_) | copy-start | bytes 2359300
  69.8 8.3 %collective-permute-start.1 = (f32[3,3,2,16,128]{4,3,2,1,0:T(8,128)S(1)}, f32[3,3,2,16,128]{4,3,2,1,0:T(8,128)S(1)}, u32[]{:S(2)}, u32[]{:S(2)}) collective-permute-start(f32[3,3,2,16,128]{4,3,2,1,0:T(8,128)S(1)} %get-tuple-element.29), channel_id=1, source_target_pairs={{16,0},{32,16},{48,32},{64,48},{80,64},{96,80},{112,96},{128,112},... | collective-permute-start | bytes 442376 | tf_op jit(solution)/shard_map/ppermute | solution.py:668
  72.2 8.0 %collective-permute-start = (f32[3,3,2,16,128]{4,3,2,1,0:T(8,128)S(1)}, f32[3,3,2,16,128]{4,3,2,1,0:T(8,128)S(1)}, u32[]{:S(2)}, u32[]{:S(2)}) collective-permute-start(f32[3,3,2,16,128]{4,3,2,1,0:T(8,128)S(1)} %get-tuple-element.30), channel_id=1, source_target_pairs={{0,16},{16,32},{32,48},{48,64},{64,80},{80,96},{96,112},{112,128},... | collective-permute-start | bytes 442376 | tf_op jit(solution)/shard_map/ppermute | solution.py:667
  78.1 2.1 %copy-start.4 = (f32[3,3,2,16,128]{4,3,2,1,0:T(8,128)}, f32[3,3,2,16,128]{4,3,2,1,0:T(8,128)S(1)}, u32[]{:S(2)}) copy-start(f32[3,3,2,16,128]{4,3,2,1,0:T(8,128)S(1)} %collective-permute-done.1.refs_4_) | copy-start | bytes 442372
  80.2 0.7 copy-start.5
  90.3 21.1 %all-to-all-start.2 = ((f32[32,8,128]{2,1,0:T(8,128)}), f32[32,8,128]{2,1,0:T(8,128)S(1)}, u32[]{:S(2)}, u32[]{:S(2)}) async-start(f32[32,8,128]{2,1,0:T(8,128)} %get-tuple-element.22), calls=%async_computation.2 | async-start | bytes 262144 | tf_op jit(solution)/shard_map/all_to_all | solution.py:673
  111.4 0.7 copy-start.2

commit v4 on v3

--- a/solution.py
+++ b/solution.py
@@ -95,8 +95,20 @@
     return jnp.dot(left, right, preferred_element_type=F32)
 
 
+def dot3(left_high, left_low, high, low):
+    half = left_high.shape[0] // 2
+    parts = [slice(0, half), slice(half, None)]
+    totals = [dot(left_high[p], low) for p in parts]
+    totals = [t + dot(left_low[p], high) for t, p in zip(totals, parts)]
+    return [t + dot(left_high[p], high) for t, p in zip(totals, parts)]
+
+
 def dot_full(left, right):
     return jnp.dot(left, right, precision=HIGHEST, preferred_element_type=F32)
+
+
+def in_hbm(array):
+    return pltpu.with_memory_space_constraint(array, pltpu.HBM)
 
 
 def lane_ids(shape):
@@ -224,36 +236,54 @@
     )(ints, widths, heights, base, table, stack, dz_high, dz_low)
 
 
-def lines_body(ints, widths, heights, in_ref, field_ref, fgh_ref, fgl_ref, fh_ref, fl_ref,
-               dh_ref, dl_ref, mass_ref, out_ref):
-    ey = pl.program_id(0)
-    width, height = widths[ints[0]], heights[ey]
-    coeffs = [in_ref[:, c, 0].reshape(PLANES, LANES) for c in range(3)]
-    high, low = split(jnp.concatenate(coeffs, axis=1))
-    both = dot(fgh_ref[...], high) + dot(fgh_ref[...], low) + dot(fgl_ref[...], high)
-    lines = [both[:PLANES, c * LANES : (c + 1) * LANES] for c in range(3)]
-    slopes = [None, None, [both[PLANES:, c * LANES : (c + 1) * LANES] for c in range(3)]]
-    high, low = split(jnp.concatenate(lines, axis=0))
-    plane = dot(high, dh_ref[...]) + dot(low, dh_ref[...]) + dot(high, dl_ref[...])
-    per_c = [plane[c * PLANES : (c + 1) * PLANES] for c in range(3)]
-    slopes[0] = [part[:, :LANES] * (2.0 / width) for part in per_c]
-    slopes[1] = [part[:, LANES:] * (2.0 / height) for part in per_c]
-    pieces = []
-    for c in range(3):
-        total = field_ref[0, 0, 0] * slopes[0][c]
-        for d in range(1, 3):
-            total = total + field_ref[0, d, 0] * slopes[d][c]
-        for d in range(3):
-            total = total - lines[d] * field_ref[1 + c, d, 0]
-        pieces.append(total)
-    high, low = split(jnp.concatenate(pieces, axis=1))
-    hat = dot(fh_ref[...], high) + dot(fh_ref[...], low) + dot(fl_ref[...], high)
-    mass = mass_ref[...] * (width * height * 0.25)
+def lines_body(ints, widths, heights, in_ref, field_hbm, fgh_ref, fgl_ref, fh_ref, fl_ref,
+               dh_ref, dl_ref, mass_ref, out_ref, fields, lines, slopes, sems):
+    copies = [
+        pltpu.make_async_copy(field_hbm.at[k], fields.at[k], sems.at[k]) for k in range(4)
+    ]
+    for copy in copies:
+        copy.start()
+    width = widths[ints[0]]
+    pairs = [((2 * p) // 2, (2 * p) % 2, (2 * p + 1) % 2) for p in range(3)]
+    double_dh = jnp.concatenate([dh_ref[...], dh_ref[...]], axis=0)
+
+    def coeffs(c, ey):
+        return in_ref[:, c, ey].reshape(PLANES, LANES)
+
+    for c, _, _ in pairs:
+        high, low = split(jnp.concatenate([coeffs(c, 0), coeffs(c, 1)], axis=1))
+        both = dot3(fgh_ref[...], fgl_ref[...], high, low)
+        for ey in range(2):
+            line = both[0][:, ey * LANES : (ey + 1) * LANES]
+            lines[c, ey] = line
+            slopes[2, c, ey] = both[1][:, ey * LANES : (ey + 1) * LANES]
+            high_line, low_line = split(line)
+            wide = jnp.concatenate([high_line, low_line], axis=1)
+            parts = [slice(0, LANES), slice(LANES, PLANES)]
+            planes = [dot(wide[p], double_dh) for p in parts]
+            planes = [v + dot(high_line[p], dl_ref[...]) for v, p in zip(planes, parts)]
+            for plane, p in zip(planes, parts):
+                slopes[0, c, ey, p] = plane[:, :LANES] * (2.0 / width)
+                slopes[1, c, ey, p] = plane[:, LANES:] * (2.0 / heights[ey])
+    for copy in copies:
+        copy.wait()
     lane = lane_ids((PLANES, LANES))
     for c in range(3):
-        source = SIGMA * coeffs[c] + hat[:, c * LANES : (c + 1) * LANES] * (1.0 / NU)
-        value = jnp.where(lane < NODES, mass * source, width)
-        out_ref[:, c, 0] = value.reshape(PEERS, LOCAL, LANES)
+        pieces = []
+        for ey in range(2):
+            total = fields[0, 0, ey] * slopes[0, c, ey]
+            for d in range(1, 3):
+                total = total + fields[0, d, ey] * slopes[d, c, ey]
+            for d in range(3):
+                total = total - lines[d, ey] * fields[1 + c, d, ey]
+            pieces.append(total)
+        high, low = split(jnp.concatenate(pieces, axis=1))
+        hat = jnp.concatenate(dot3(fh_ref[...], fl_ref[...], high, low), axis=0)
+        for ey in range(2):
+            mass = mass_ref[...] * (width * heights[ey] * 0.25)
+            source = SIGMA * coeffs(c, ey) + hat[:, ey * LANES : (ey + 1) * LANES] * (1.0 / NU)
+            value = jnp.where(lane < NODES, mass * source, width)
+            out_ref[:, c, ey] = value.reshape(PEERS, LOCAL, LANES)
 
 
 def lines_stage(ints, widths, heights, arrived, fields, tables, d_high, d_low, mass):
@@ -262,18 +292,22 @@
     def whole(array):
         return pl.BlockSpec(array.shape, lambda i: (0,) * array.ndim)
 
-    block = pl.BlockSpec((PEERS, 3, 1, LOCAL, LANES), lambda i: (0, 0, i, 0, 0))
     return pl.pallas_call(
         lines_body,
-        grid=(2,),
-        in_specs=[
-            smem, smem, smem, block,
-            pl.BlockSpec((4, 3, 1, PLANES, LANES), lambda i: (0, 0, i, 0, 0)),
-        ] + [whole(a) for a in tables] + [whole(d_high), whole(d_low), whole(mass)],
-        out_specs=block,
+        grid=(1,),
+        in_specs=[smem, smem, smem, whole(arrived), pl.BlockSpec(memory_space=pl.ANY)]
+        + [whole(a) for a in tables] + [whole(d_high), whole(d_low), whole(mass)],
+        out_specs=whole(arrived),
         out_shape=jax.ShapeDtypeStruct((PEERS, 3, 2, LOCAL, LANES), F32),
+        scratch_shapes=[
+            pltpu.VMEM((4, 3, 2, PLANES, LANES), F32),
+            pltpu.VMEM((3, 2, PLANES, LANES), F32),
+            pltpu.VMEM((3, 3, 2, PLANES, LANES), F32),
+            pltpu.SemaphoreType.DMA((4,)),
+        ],
+        compiler_params=pltpu.CompilerParams(vmem_limit_bytes=24 * 2**20),
         name="lines_stage",
-    )(ints, widths, heights, arrived, fields, *tables, d_high, d_low, mass)
+    )(*map(in_hbm, (ints, widths, heights)), arrived, in_hbm(fields), *map(in_hbm, tables), d_high, d_low, mass)
 
 
 def join_columns(chunks):
@@ -302,12 +336,17 @@
     return high, mid, (rest - mid.astype(F32)).astype(BF16)
 
 
-def dot_split(value, parts):
-    high, mid, low = split3(value)
-    total = dot(low, parts[0]) + dot(high, parts[2])
-    total = total + dot(mid, parts[1])
-    total = total + dot(mid, parts[0]) + dot(high, parts[1])
-    return total + dot(high, parts[0])
+def dot_split(source, target, operator):
+    cut = 176
+    parts = [slice(0, cut), slice(cut, ROWS * LOCAL)]
+    pieces = [split3(source[p, :]) for p in parts]
+    totals = [None, None]
+    for left, right in ((2, 0), (0, 2), (1, 1), (1, 0), (0, 1), (0, 0)):
+        for k in range(2):
+            value = dot(pieces[k][left], operator[right])
+            totals[k] = value if totals[k] is None else totals[k] + value
+    for k in range(2):
+        target[parts[k], :] = totals[k]
 
 
 def stiff_rows(stiff, values):
@@ -409,7 +448,7 @@
             mass_y.append(h1 * weights[y - Q + 1])
 
     def apply(source, target, operator, mass_row, low_key):
-        tmp[...] = dot_split(source[...], [operator[k] for k in range(3)])
+        dot_split(source, tmp, operator)
         sums = [[], []]
         for half in range(2):
             plane = ints[0] * LOCAL + half * 8 + lax.broadcasted_iota(jnp.int32, (8, LANES), 0)
@@ -491,8 +530,9 @@
             pltpu.VMEM((LANES, LANES), F32),
             pltpu.VMEM((ROWS * LOCAL, 2 * LANES), F32),
         ],
+        compiler_params=pltpu.CompilerParams(vmem_limit_bytes=24 * 2**20),
         name="krylov_stage",
-    )(ints, heights, own, left, right, kb, near, wx)
+    )(in_hbm(ints), in_hbm(heights), own, left, right, kb, near, wx)
 
 
 def unpack_body(v0_ref, v1_ref, v2_ref, u0_ref, u1_ref, u2_ref, scr, flat):
@@ -529,7 +569,7 @@
 def unpack(v0, v1, v2):
     vector = pl.BlockSpec((1, ROWS * LOCAL, 2 * LANES), lambda i: (i, 0, 0))
     target = pl.BlockSpec((1, Q, 2, COLUMNS * Q * LOCAL), lambda i: (i, 0, 0, 0))
-    shape = jax.ShapeDtypeStruct((3, Q, 2, COLUMNS * Q * LOCAL), F32)
+    shape = pltpu.HBM((3, Q, 2, COLUMNS * Q * LOCAL), F32)
     return pl.pallas_call(
         unpack_body,
         grid=(3,),
@@ -540,6 +580,7 @@
             pltpu.VMEM((2, 2, 256, LANES), F32),
             pltpu.VMEM((COLUMNS * Q * LOCAL // LANES, 32, LANES), F32),
         ],
+        compiler_params=pltpu.CompilerParams(vmem_limit_bytes=24 * 2**20),
         name="unpack",
     )(v0, v1, v2)
 
@@ -604,8 +645,9 @@
         out_specs=target,
         out_shape=jax.ShapeDtypeStruct((3, Q, 2, COLUMNS * Q * LOCAL), F32),
         scratch_shapes=[pltpu.VMEM((3, COLUMNS * Q * LOCAL // LANES, 8, LANES), F32)],
+        compiler_params=pltpu.CompilerParams(vmem_limit_bytes=24 * 2**20),
         name="finish",
-    )(moments, u0, u1, u2)
+    )(moments, in_hbm(u0), in_hbm(u1), in_hbm(u2))
     return jnp.transpose(out, (0, 2, 1, 3))
 
 

time: 117 us -> 112 us (0.957)
  Pallas kernels: 35.5 us -> 31 us
  local copies, waits for them, and re-layouts: 3.11 us -> 0.91 us
  waiting for transfers between devices: 20.7 us -> 22.9 us
    unnamed x13 -> x15, local copies, waits for them, and re-layouts: 3.09 us -> 0.89 us
    all_to_all x1, waiting for transfers between devices: 4.68 us -> 6.48 us  [local(): lax.all_to_all(moments, 'elem', split_axis=0, concat_axis=0, tiled=True)]
    pallas_call x1, Pallas kernels: 4.99 us -> 3.29 us  [unpack(): pl.pallas_call(unpack_body, grid=(3,), in_specs=[vector] * 3, out_specs=[...]
    pallas_call x1, Pallas kernels: 9.44 us -> 7.97 us  [krylov_stage(): pl.pallas_call(body, grid=(3,), in_specs=[smem, smem, chunk(COLUMNS), chu...]
  transfers between devices with their start and end apart: 4 -> 4, of which waited for: 4 -> 4; matrix products, arithmetic and copies ran while one was open for 1% -> 1% of each run, Pallas kernels for 10% -> 9%
where the time goes in v4:
time: 112 us; the launch traced here: 111 us
  Pallas kernels  31 us (28%)
  starting transfers between devices  27.6 us (25%)
  blocking collectives  27.3 us (24%)
  waiting for transfers between devices  22.9 us (20%)
    all_to_all x1, blocking collectives, local(): lax.all_to_all(source, 'four', split_axis=0, concat_axis=0, tiled=True)  27.3 us
    all_to_all x1, waiting for transfers between devices, local(): lax.all_to_all(send, 'four', split_axis=0, concat_axis=0, tiled=True)  11.6 us
    all_to_all x1, starting transfers between devices, local(): lax.all_to_all(moments, 'elem', split_axis=0, concat_axis=0, tiled=True)  11.4 us
    all_to_all x1, starting transfers between devices, local(): lax.all_to_all(send, 'four', split_axis=0, concat_axis=0, tiled=True)  10.4 us
    pallas_call x1, Pallas kernels, krylov_stage(): pl.pallas_call(body, grid=(3,), in_specs=[smem, smem, chunk(COLUMNS), chu...  7.97 us
    pallas_call x1, Pallas kernels, base_stage(): pl.pallas_call(base_body, grid=(6,), in_specs=[smem, smem, smem, pl.Block...  6.98 us
    all_to_all x1, waiting for transfers between devices, local(): lax.all_to_all(moments, 'elem', split_axis=0, concat_axis=0, tiled=True)  6.48 us
    pallas_call x1, Pallas kernels, lines_stage(): pl.pallas_call(lines_body, grid=(1,), in_specs=[smem, smem, smem, whole(a...  4.72 us
  transfers between devices with their start and end apart: 4, of which 4 were waited for; matrix products, arithmetic and copies ran while one was open for 1% of the time, Pallas kernels for 9%

profile of v4, /device:TPU:8, one launch (start us, length us, event | category | flops | bytes accessed | tf_op | source)
XLA Modules:
  0.0 111.2 jit_solution(13722635362865698049)
XLA Ops:
  0.0 0.0 copy-start.6
  0.0 4.1 %pack.1 = f32[16,3,2,16,128]{4,3,2,1,0:T(8,128)} custom-call(f32[3,11,2,2816]{3,2,1,0:T(2,128)} %bitcast.3), custom_call_target="tpu_custom_call" | custom-call | tf_op jit(solution)/shard_map/pack/pallas_call | solution.py:162
  4.2 10.4 %all-to-all-start = ((f32[16,3,2,16,128]{4,3,2,1,0:T(8,128)}), f32[16,3,2,16,128]{4,3,2,1,0:T(8,128)S(1)}, u32[]{:S(2)}, u32[]{:S(2)}) async-start(f32[16,3,2,16,128]{4,3,2,1,0:T(8,128)} %pack.1), calls=%async_computation | async-start | bytes 1572864 | tf_op jit(solution)/shard_map/all_to_all | solution.py:698
  15.2 0.0 copy-done.6
  15.2 0.9 copy.16.base_ref
  16.1 0.6 pad_add_fusion.ints.refs_0_
  16.7 7.0 %base_stage.1 = (f32[4,3,2,256,128]{4,3,2,1,0:T(8,128)}, bf16[512,256]{1,0:T(8,128)(2,1)}, bf16[512,256]{1,0:T(8,128)(2,1)}, bf16[256,256]{1,0:T(8,128)(2,1)}, bf16[256,256]{1,0:T(8,128)(2,1)}) custom-call(s32[2]{0:T(128)} %pad_add_fusion.ints.refs_0_, f32[16]{0:T(128)} %widths.3, f32[2]{0:T(128)} %refs_1_.1, bf16[3,2,11,2816]{3,2,1,0:T(8,128)(2,1)} %copy.16.base_ref, ...), custom_call_target="tpu_custom_call" | custom-call | tf_op jit(solution)/shard_map/base_stage/pallas_call | solution.py:214
  23.7 11.6 %all-to-all-done.in_ref = f32[16,3,2,16,128]{4,3,2,1,0:T(8,128)S(1)} async-done(((f32[16,3,2,16,128]{4,3,2,1,0:T(8,128)}), f32[16,3,2,16,128]{4,3,2,1,0:T(8,128)S(1)}, u32[]{:S(2)}, u32[]{:S(2)}) %all-to-all-start) | async-done | bytes 786464 | tf_op jit(solution)/shard_map/all_to_all | solution.py:698
  35.3 0.0 copy-done.3
  35.3 0.0 copy-start
  35.3 0.0 copy-start.1
  35.3 0.0 copy-start.4
  35.3 4.7 %lines_stage.1 = f32[16,3,2,16,128]{4,3,2,1,0:T(8,128)S(1)} custom-call(s32[2]{0:T(128)} %pad_add_fusion.ints.refs_0_, f32[16]{0:T(128)} %widths.3, f32[2]{0:T(128)} %refs_1_.1, f32[16,3,2,16,128]{4,3,2,1,0:T(8,128)S(1)} %all-to-all-done.in_ref, f32[4,3,2,256,128]{4,3,2,1,0:T(8,128)} %get-tuple-element.17.field_hbm, ...), custom_call_target="tpu_custom_call" | custom-call | tf_op jit(solution)/shard_map/lines_stage/pallas_call | solution.py:295
  40.0 27.3 %all_to_all.15.refs_2_ = f32[16,3,2,16,128]{4,3,2,1,0:T(8,128)S(1)} all-to-all(f32[16,3,2,16,128]{4,3,2,1,0:T(8,128)S(1)} %lines_stage.1), channel_id=1, replica_groups=mesh['elem'=32,'four'=16] {'four'}, dimensions={0} | all-to-all | bytes 1572864 | tf_op jit(solution)/shard_map/all_to_all | solution.py:707
  67.4 2.4 %collective-permute-start.1 = (f32[3,3,2,16,128]{4,3,2,1,0:T(8,128)S(1)}, f32[3,3,2,16,128]{4,3,2,1,0:T(8,128)S(1)}, u32[]{:S(2)}, u32[]{:S(2)}) collective-permute-start(f32[3,3,2,16,128]{4,3,2,1,0:T(8,128)S(1)} %get-tuple-element.29), channel_id=1, source_target_pairs={{16,0},{32,16},{48,32},{64,48},{80,64},{96,80},{112,96},{128,112},... | collective-permute-start | bytes 442376 | tf_op jit(solution)/shard_map/ppermute | solution.py:710
  69.8 3.5 %collective-permute-start = (f32[3,3,2,16,128]{4,3,2,1,0:T(8,128)S(1)}, f32[3,3,2,16,128]{4,3,2,1,0:T(8,128)S(1)}, u32[]{:S(2)}, u32[]{:S(2)}) collective-permute-start(f32[3,3,2,16,128]{4,3,2,1,0:T(8,128)S(1)} %get-tuple-element.30), channel_id=1, source_target_pairs={{0,16},{16,32},{32,48},{48,64},{64,80},{80,96},{96,112},{112,128},... | collective-permute-start | bytes 442376 | tf_op jit(solution)/shard_map/ppermute | solution.py:709
  73.3 2.7 %collective-permute-done.1.refs_4_ = f32[3,3,2,16,128]{4,3,2,1,0:T(8,128)S(1)} collective-permute-done((f32[3,3,2,16,128]{4,3,2,1,0:T(8,128)S(1)}, f32[3,3,2,16,128]{4,3,2,1,0:T(8,128)S(1)}, u32[]{:S(2)}, u32[]{:S(2)}) %collective-permute-start.1) | collective-permute-done | bytes 147488 | tf_op jit(solution)/shard_map/ppermute | solution.py:710
  76.0 2.1 %collective-permute-done.refs_3_ = f32[3,3,2,16,128]{4,3,2,1,0:T(8,128)S(1)} collective-permute-done((f32[3,3,2,16,128]{4,3,2,1,0:T(8,128)S(1)}, f32[3,3,2,16,128]{4,3,2,1,0:T(8,128)S(1)}, u32[]{:S(2)}, u32[]{:S(2)}) %collective-permute-start) | collective-permute-done | bytes 147488 | tf_op jit(solution)/shard_map/ppermute | solution.py:709
  78.1 0.0 copy-done.4
  78.1 8.0 %krylov_stage.1 = (f32[3,336,256]{2,1,0:T(8,128)S(1)}, f32[3,336,256]{2,1,0:T(8,128)S(1)}, f32[3,336,256]{2,1,0:T(8,128)S(1)}, f32[32,8,128]{2,1,0:T(8,128)}) custom-call(s32[2]{0:T(128)} %pad_add_fusion.ints.refs_0_, f32[2]{0:T(128)} %refs_1_.1, f32[16,3,2,16,128]{4,3,2,1,0:T(8,128)S(1)} %all_to_all.15.refs_2_, ...), custom_call_target="tpu_custom_call" | custom-call | tf_op jit(solution)/shard_map/krylov_stage/pallas_call | solution.py:520
  86.1 11.4 %all-to-all-start.2 = ((f32[32,8,128]{2,1,0:T(8,128)}), f32[32,8,128]{2,1,0:T(8,128)S(1)}, u32[]{:S(2)}, u32[]{:S(2)}) async-start(f32[32,8,128]{2,1,0:T(8,128)} %get-tuple-element.22), calls=%async_computation.2 | async-start | bytes 262144 | tf_op jit(solution)/shard_map/all_to_all | solution.py:715
  97.5 3.3 %unpack.1 = (f32[3,11,2,2816]{3,2,1,0:T(2,128)}, f32[3,11,2,2816]{3,2,1,0:T(2,128)}, f32[3,11,2,2816]{3,2,1,0:T(2,128)}) custom-call(f32[3,336,256]{2,1,0:T(8,128)S(1)} %get-tuple-element.23.v0_ref, f32[3,336,256]{2,1,0:T(8,128)S(1)} %get-tuple-element.24.v1_ref, f32[3,336,256]{2,1,0:T(8,128)S(1)} %get-tuple-element.25.v2_ref), custom_call_target="tpu_custom_call" | custom-call | tf_op jit(solution)/shard_map/unpack/pallas_call | solution.py:573
  100.8 6.5 %all-to-all-done.2.mom_ref = f32[32,8,128]{2,1,0:T(8,128)S(1)} async-done(((f32[32,8,128]{2,1,0:T(8,128)}), f32[32,8,128]{2,1,0:T(8,128)S(1)}, u32[]{:S(2)}, u32[]{:S(2)}) %all-to-all-start.2) | async-done | bytes 131104 | tf_op jit(solution)/shard_map/all_to_all | solution.py:715
  107.2 3.9 %finish.1 = f32[3,11,2,2816]{3,2,1,0:T(2,128)} custom-call(f32[32,8,128]{2,1,0:T(8,128)S(1)} %all-to-all-done.2.mom_ref, f32[3,11,2,2816]{3,2,1,0:T(2,128)} %get-tuple-element.26.u0_ref, f32[3,11,2,2816]{3,2,1,0:T(2,128)} %get-tuple-element.27.u1_ref, f32[3,11,2,2816]{3,2,1,0:T(2,128)} %get-tuple-element.28.u2_ref), custom_call_target="tpu_custom_call" | custom-call | tf_op jit(solution)/shard_map/finish/pallas_call | solution.py:641
  (8 shorter events, 0.0 us)
Async XLA Ops:
  0.0 35.3 %copy-start.5 = (f32[1,128]{1,0:T(1,128)S(1)}, f32[1,128]{1,0:T(1,128)}, u32[]{:S(2)}) copy-start(f32[1,128]{1,0:T(1,128)} %constant.30.clone.mass_ref) | copy-start | bytes 1540
  0.0 35.3 %copy-start.2 = (bf16[128,256]{1,0:T(8,128)(2,1)S(1)}, bf16[128,256]{1,0:T(8,128)(2,1)}, u32[]{:S(2)}) copy-start(bf16[128,256]{1,0:T(8,128)(2,1)} %constant.29.clone.dl_ref) | copy-start | bytes 196612
  0.0 35.3 %copy-start.3 = (bf16[128,256]{1,0:T(8,128)(2,1)S(1)}, bf16[128,256]{1,0:T(8,128)(2,1)}, u32[]{:S(2)}) copy-start(bf16[128,256]{1,0:T(8,128)(2,1)} %constant.28.clone.dh_ref) | copy-start | bytes 196612
  0.0 15.2 %copy-start.6 = (bf16[3,2,11,2816]{3,1,2,0:T(2,128)(2,1)S(1)}, bf16[3,2,11,2816]{3,1,2,0:T(2,128)(2,1)}, u32[]{:S(2)}) copy-start(bf16[3,2,11,2816]{3,1,2,0:T(2,128)(2,1)} %param.16) | copy-start | bytes 1115140
  4.2 31.1 %all-to-all-start = ((f32[16,3,2,16,128]{4,3,2,1,0:T(8,128)}), f32[16,3,2,16,128]{4,3,2,1,0:T(8,128)S(1)}, u32[]{:S(2)}, u32[]{:S(2)}) async-start(f32[16,3,2,16,128]{4,3,2,1,0:T(8,128)} %pack.1), calls=%async_computation | async-start | bytes 1572864 | tf_op jit(solution)/shard_map/all_to_all | solution.py:698
  35.3 42.8 %copy-start = (f32[256,256]{1,0:T(8,128)S(1)}, f32[256,256]{1,0:T(8,128)}, u32[]{:S(2)}) copy-start(f32[256,256]{1,0:T(8,128)} %constant.32.clone.refs_6_) | copy-start | bytes 786436
  35.3 42.8 %copy-start.1 = (f32[256,256]{1,0:T(8,128)S(1)}, f32[256,256]{1,0:T(8,128)}, u32[]{:S(2)}) copy-start(f32[256,256]{1,0:T(8,128)} %constant.31.clone.refs_5_) | copy-start | bytes 786436
  35.3 42.8 %copy-start.4 = (f32[1,256]{1,0:T(1,128)S(1)}, f32[1,256]{1,0:T(1,128)}, u32[]{:S(2)}) copy-start(f32[1,256]{1,0:T(1,128)} %constant.33.clone.refs_7_) | copy-start | bytes 3076
  67.4 8.6 %collective-permute-start.1 = (f32[3,3,2,16,128]{4,3,2,1,0:T(8,128)S(1)}, f32[3,3,2,16,128]{4,3,2,1,0:T(8,128)S(1)}, u32[]{:S(2)}, u32[]{:S(2)}) collective-permute-start(f32[3,3,2,16,128]{4,3,2,1,0:T(8,128)S(1)} %get-tuple-element.29), channel_id=1, source_target_pairs={{16,0},{32,16},{48,32},{64,48},{80,64},{96,80},{112,96},{128,112},... | collective-permute-start | bytes 442376 | tf_op jit(solution)/shard_map/ppermute | solution.py:710
  69.8 8.3 %collective-permute-start = (f32[3,3,2,16,128]{4,3,2,1,0:T(8,128)S(1)}, f32[3,3,2,16,128]{4,3,2,1,0:T(8,128)S(1)}, u32[]{:S(2)}, u32[]{:S(2)}) collective-permute-start(f32[3,3,2,16,128]{4,3,2,1,0:T(8,128)S(1)} %get-tuple-element.30), channel_id=1, source_target_pairs={{0,16},{16,32},{32,48},{48,64},{64,80},{80,96},{96,112},{112,128},... | collective-permute-start | bytes 442376 | tf_op jit(solution)/shard_map/ppermute | solution.py:709
  86.1 21.1 %all-to-all-start.2 = ((f32[32,8,128]{2,1,0:T(8,128)}), f32[32,8,128]{2,1,0:T(8,128)S(1)}, u32[]{:S(2)}, u32[]{:S(2)}) async-start(f32[32,8,128]{2,1,0:T(8,128)} %get-tuple-element.22), calls=%async_computation.2 | async-start | bytes 262144 | tf_op jit(solution)/shard_map/all_to_all | solution.py:715

commit v5 on v4

--- a/solution.py
+++ b/solution.py
@@ -15,6 +15,9 @@
 ROWS = 21
 NODES = Q * Q
 LANES = 128
+PITCH = 17
+FACE = ROWS * Q
+TILES = 11
 NU = 0.005
 DT = 0.01
 SIGMA = 1.0 / (NU * DT)
@@ -120,11 +123,11 @@
     return value if shift == 0 else pltpu.roll(value, shift, value.ndim - 1)
 
 
-def block_transpose(arrays, count):
+def block_transpose(arrays, places, offset=0):
     lane = lane_ids(arrays[0].shape)
-    turned = [turn(array, Q * k) for k, array in enumerate(arrays)]
+    turned = [turn(array, Q * k - offset) for k, array in enumerate(arrays)]
     results = []
-    for place in range(count):
+    for place in places:
         distance = (lane - Q * place) & (LANES - 1)
         chosen = turned[0]
         for k in range(1, len(turned)):
@@ -150,11 +153,11 @@
                 first = flat[tile, rows, :]
                 if shift and tile + 1 < tiles:
                     first = jnp.where(lane >= shift, first, flat[tile + 1, rows, :])
-                scratches[t][ey, j * 16 : j * 16 + 16, :] = turn(first, -shift)
+                scratches[t][ey, j * PITCH : j * PITCH + 16, :] = turn(first, -shift)
     for ey in range(2):
         for t in range(2):
-            rows = [scratches[t][ey, pl.ds(qy, LOCAL, stride=16), :] for qy in range(Q)]
-            for place, value in enumerate(block_transpose(rows, Q if t == 0 else COLUMNS - Q)):
+            rows = [scratches[t][ey, pl.ds(qy, LOCAL, stride=PITCH), :] for qy in range(Q)]
+            for place, value in enumerate(block_transpose(rows, range(Q if t == 0 else COLUMNS - Q))):
                 out_ref[Q * t + place, 0, ey] = value
 
 
@@ -167,11 +170,12 @@
         out_shape=jax.ShapeDtypeStruct((PEERS, 3, 2, LOCAL, LANES), F32),
         scratch_shapes=[
             pltpu.VMEM((COLUMNS * Q * LOCAL // LANES, 32, LANES), F32),
-            pltpu.VMEM((2, 256, LANES), F32),
-            pltpu.VMEM((2, 256, LANES), F32),
+            pltpu.VMEM((2, LOCAL * PITCH, LANES), F32),
+            pltpu.VMEM((2, LOCAL * PITCH, LANES), F32),
         ],
+        compiler_params=pltpu.CompilerParams(vmem_limit_bytes=24 * 2**20),
         name="pack",
-    )(jnp.transpose(adjoint, (0, 2, 1, 3)))
+    )(in_hbm(jnp.transpose(adjoint, (0, 2, 1, 3))))
 
 
 def base_body(ints, widths, heights, base_ref, table_ref, stack_ref, dzh_ref, dzl_ref,
@@ -237,7 +241,7 @@
 
 
 def lines_body(ints, widths, heights, in_ref, field_hbm, fgh_ref, fgl_ref, fh_ref, fl_ref,
-               dh_ref, dl_ref, mass_ref, out_ref, fields, lines, slopes, sems):
+               dh_ref, dl_ref, mass_ref, out_ref, fields, lines, slopes, packed, sems):
     copies = [
         pltpu.make_async_copy(field_hbm.at[k], fields.at[k], sems.at[k]) for k in range(4)
     ]
@@ -279,11 +283,31 @@
             pieces.append(total)
         high, low = split(jnp.concatenate(pieces, axis=1))
         hat = jnp.concatenate(dot3(fh_ref[...], fl_ref[...], high, low), axis=0)
+        values = []
         for ey in range(2):
             mass = mass_ref[...] * (width * heights[ey] * 0.25)
             source = SIGMA * coeffs(c, ey) + hat[:, ey * LANES : (ey + 1) * LANES] * (1.0 / NU)
-            value = jnp.where(lane < NODES, mass * source, width)
-            out_ref[:, c, ey] = value.reshape(PEERS, LOCAL, LANES)
+            values.append(mass * source)
+        values[0] = values[0] + jnp.where(lane >= NODES - Q, turn(values[1], NODES - Q), 0.0)
+        for ey in range(2):
+            packed[c, ey] = values[ey]
+    lane = lane_ids((PEERS, 8, LANES))
+    pieces = []
+    for half in range(2):
+        for c in range(3):
+            base = (half * 3 + c) * FACE
+            for ey in range(2):
+                value = packed[c, ey].reshape(PEERS, 2, 8, LANES)[:, half]
+                pieces.append((base + NODES * ey, turn(value, base + (NODES - Q) * ey)))
+    pieces.append((6 * FACE, jnp.full((PEERS, 8, LANES), width, F32)))
+    starts = [start for start, _ in pieces] + [TILES * LANES]
+    for tile in range(TILES):
+        low, high = tile * LANES, (tile + 1) * LANES
+        chosen = None
+        for k, (start, value) in enumerate(pieces):
+            if start < high and starts[k + 1] > low:
+                chosen = value if chosen is None else jnp.where(lane >= start - low, value, chosen)
+        out_ref[:, tile] = chosen
 
 
 def lines_stage(ints, widths, heights, arrived, fields, tables, d_high, d_low, mass):
@@ -297,12 +321,13 @@
         grid=(1,),
         in_specs=[smem, smem, smem, whole(arrived), pl.BlockSpec(memory_space=pl.ANY)]
         + [whole(a) for a in tables] + [whole(d_high), whole(d_low), whole(mass)],
-        out_specs=whole(arrived),
-        out_shape=jax.ShapeDtypeStruct((PEERS, 3, 2, LOCAL, LANES), F32),
+        out_specs=pl.BlockSpec((PEERS, TILES, 8, LANES), lambda i: (0, 0, 0, 0)),
+        out_shape=jax.ShapeDtypeStruct((PEERS, TILES, 8, LANES), F32),
         scratch_shapes=[
             pltpu.VMEM((4, 3, 2, PLANES, LANES), F32),
             pltpu.VMEM((3, 2, PLANES, LANES), F32),
             pltpu.VMEM((3, 3, 2, PLANES, LANES), F32),
+            pltpu.VMEM((3, 2, PLANES, LANES), F32),
             pltpu.SemaphoreType.DMA((4,)),
         ],
         compiler_params=pltpu.CompilerParams(vmem_limit_bytes=24 * 2**20),
@@ -310,20 +335,17 @@
     )(*map(in_hbm, (ints, widths, heights)), arrived, in_hbm(fields), *map(in_hbm, tables), d_high, d_low, mass)
 
 
-def join_columns(chunks):
-    lane = lane_ids(chunks[0].shape)
+def join_columns(chunks, offset):
+    lane = (lane_ids(chunks[0].shape) - offset) & (LANES - 1)
     place = lane - Q * ((lane * 5958) >> 16)
     at_first = (place == 0) & (lane < NODES)
     at_last = (place == Q - 1) & (lane < NODES)
     results = []
     for k, chunk in enumerate(chunks):
-        if chunk is None:
-            results.append(None)
-            continue
         extra = 0.0
-        if k > 0 and chunks[k - 1] is not None:
+        if k > 0:
             extra = jnp.where(at_first, turn(chunks[k - 1], -(Q - 1)), extra)
-        if k + 1 < len(chunks) and chunks[k + 1] is not None:
+        if k + 1 < len(chunks):
             extra = jnp.where(at_last, turn(chunks[k + 1], Q - 1), extra)
         results.append(chunk + extra)
     return results
@@ -376,65 +398,46 @@
 
 def krylov_body(stiff_y, weights, ints, heights, own_ref, left_ref, right_ref, kb_ref, kn_ref, wx_ref,
                 v0_ref, v1_ref, v2_ref, mom_ref, kxs, kbs, vec, prod, tmp):
-    comp = pl.program_id(0)
     column_refs = (
         [left_ref.at[k] for k in range(GHOST)]
         + [own_ref.at[k] for k in range(COLUMNS)]
         + [right_ref.at[k] for k in range(GHOST)]
     )
 
-    @pl.when(comp == 0)
-    def _():
-        lane = lane_ids((8, LANES))
-        widths = [ref[0, 0, 0:8, NODES : NODES + 1] for ref in column_refs]
-        zero = jnp.zeros((8, 1), F32)
-        widths = [zero] + widths + [zero]
-        for t in range(2):
-            here = jnp.zeros((8, LANES), F32)
-            near = here
-            for place in range(Q):
-                k = Q * t + place + 1
-                low, high = Q * place, Q * place + Q - 1
-                here = jnp.where((lane >= low) & (lane <= high), widths[k], here)
-                near = jnp.where(lane == low, widths[k - 1], near)
-                near = jnp.where(lane == high, widths[k + 1], near)
-            vec[0, :, t * LANES : (t + 1) * LANES] = here
-            vec[1, :, t * LANES : (t + 1) * LANES] = near
-        here, near = vec[0], vec[1]
-        line = lane_ids((8, 2 * LANES))
-        own = ((line >= GHOST * Q) & (line < NODES)) | (
-            (line >= LANES) & (line < LANES + (Q - GHOST) * Q)
-        )
-        own = own.astype(F32)
-        mass_x = here * wx_ref[...]
-        vec[2] = mass_x * own
-        vec[1] = mass_x + near * wx_ref[...]
-        vec[3] = own * jnp.where(near > 0.0, 0.5, 1.0)
-        inverse, inverse_near = (
-            jnp.where(value > 0.0, 1.0 / jnp.where(value > 0.0, value, 1.0), 0.0)[0:1]
-            for value in (here, near)
-        )
-        scaled = kb_ref[...] * inverse
-        for k, part in enumerate(split3(scaled + kn_ref[...] * inverse_near)):
-            kxs[k] = part
-        for k, part in enumerate(split3(scaled * own[0:1])):
-            kbs[k] = part
-
-    first, second, third = v0_ref.at[0], v1_ref.at[0], v2_ref.at[0]
-    before = [None, None]
-    for ey in range(2):
-        chunks = join_columns([ref[0, ey] for ref in column_refs])
-        for t in range(2):
-            placed = block_transpose(chunks[Q * t : Q * t + Q], Q)
-            for qy in range(Q):
-                value = placed[qy]
-                y = qy + (Q - 1) * ey
-                if ey == 0 and qy == Q - 1:
-                    before[t] = value
-                    continue
-                if ey == 1 and qy == 0:
-                    value = value + before[t]
-                first[y * LOCAL : (y + 1) * LOCAL, t * LANES : (t + 1) * LANES] = value
+    lane = lane_ids((8, LANES))
+    widths = [ref[TILES - 1, :, LANES - 1 :] for ref in column_refs]
+    zero = jnp.zeros((8, 1), F32)
+    widths = [zero] + widths + [zero]
+    for t in range(2):
+        here = jnp.zeros((8, LANES), F32)
+        near = here
+        for place in range(Q):
+            k = Q * t + place + 1
+            low, high = Q * place, Q * place + Q - 1
+            here = jnp.where((lane >= low) & (lane <= high), widths[k], here)
+            near = jnp.where(lane == low, widths[k - 1], near)
+            near = jnp.where(lane == high, widths[k + 1], near)
+        vec[0, :, t * LANES : (t + 1) * LANES] = here
+        vec[1, :, t * LANES : (t + 1) * LANES] = near
+    here, near = vec[0], vec[1]
+    line = lane_ids((8, 2 * LANES))
+    own = ((line >= GHOST * Q) & (line < NODES)) | (
+        (line >= LANES) & (line < LANES + (Q - GHOST) * Q)
+    )
+    own = own.astype(F32)
+    mass_x = here * wx_ref[...]
+    vec[2] = mass_x * own
+    vec[1] = mass_x + near * wx_ref[...]
+    vec[3] = own * jnp.where(near > 0.0, 0.5, 1.0)
+    inverse, inverse_near = (
+        jnp.where(value > 0.0, 1.0 / jnp.where(value > 0.0, value, 1.0), 0.0)[0:1]
+        for value in (here, near)
+    )
+    scaled = kb_ref[...] * inverse
+    for k, part in enumerate(split3(scaled + kn_ref[...] * inverse_near)):
+        kxs[k] = part
+    for k, part in enumerate(split3(scaled * own[0:1])):
+        kbs[k] = part
 
     h0, h1 = heights[0], heights[1]
     inverse_y = (1.0 / h0, 1.0 / h1)
@@ -491,15 +494,38 @@
             prod[low_key * LOCAL + half * 8 : low_key * LOCAL + half * 8 + 8, :] = square
             prod[(low_key + 1) * LOCAL + half * 8 : (low_key + 1) * LOCAL + half * 8 + 8, :] = cross
 
-    prod[6 * LOCAL :, :] = jnp.zeros((LANES - 6 * LOCAL, LANES), F32)
-    apply(first, second, kxs, 1, 0)
-    apply(second, third, kxs, 1, 2)
-    apply(third, None, kbs, 2, 4)
-    row = lax.dot_general(
-        jnp.ones((8, LANES), F32), prod[...], (((1,), (1,)), ((), ())),
-        precision=HIGHEST, preferred_element_type=F32,
-    )
-    mom_ref[:, pl.ds(comp, 1), :] = jnp.broadcast_to(row[0:1][None], (mom_ref.shape[0], 1, LANES))
+    lane = lane_ids((8, LANES))
+    for comp in range(3):
+        first, second, third = v0_ref.at[comp], v1_ref.at[comp], v2_ref.at[comp]
+        for half in range(2):
+            for ey in range(2):
+                start = (half * 3 + comp) * FACE + (NODES - Q) * ey
+                tile, offset = start // LANES, start % LANES
+                chunks = [ref[tile] for ref in column_refs]
+                if offset:
+                    chunks = [
+                        jnp.where(lane >= offset, chunk, ref[tile + 1])
+                        for chunk, ref in zip(chunks, column_refs)
+                    ]
+                chunks = join_columns(chunks, offset)
+                places = range(ey, Q)
+                for t in range(2):
+                    for qy, value in zip(
+                        places, block_transpose(chunks[Q * t : Q * t + Q], places, offset)
+                    ):
+                        row = (qy + (Q - 1) * ey) * LOCAL + half * 8
+                        first[row : row + 8, t * LANES : (t + 1) * LANES] = value
+        prod[6 * LOCAL :, :] = jnp.zeros((LANES - 6 * LOCAL, LANES), F32)
+        apply(first, second, kxs, 1, 0)
+        apply(second, third, kxs, 1, 2)
+        apply(third, None, kbs, 2, 4)
+        row = lax.dot_general(
+            jnp.ones((8, LANES), F32), prod[...], (((1,), (1,)), ((), ())),
+            precision=HIGHEST, preferred_element_type=F32,
+        )
+        mom_ref[:, comp : comp + 1, :] = jnp.broadcast_to(
+            row[0:1][None], (mom_ref.shape[0], 1, LANES)
+        )
 
 
 def krylov_stage(stiff_y, weights, ints, heights, own, left, right, kb, near, wx, peers):
@@ -509,9 +535,9 @@
         return pl.BlockSpec(array.shape, lambda i: (0,) * array.ndim)
 
     def chunk(count):
-        return pl.BlockSpec((count, 1, 2, LOCAL, LANES), lambda i: (0, i, 0, 0, 0))
-
-    vector = pl.BlockSpec((1, ROWS * LOCAL, 2 * LANES), lambda i: (i, 0, 0))
+        return pl.BlockSpec((count, TILES, 8, LANES), lambda i: (0, 0, 0, 0))
+
+    vector = pl.BlockSpec((3, ROWS * LOCAL, 2 * LANES), lambda i: (0, 0, 0))
     shape = jax.ShapeDtypeStruct((3, ROWS * LOCAL, 2 * LANES), F32)
 
     def body(*refs):
@@ -519,7 +545,7 @@
 
     return pl.pallas_call(
         body,
-        grid=(3,),
+        grid=(1,),
         in_specs=[smem, smem, chunk(COLUMNS), chunk(GHOST), chunk(GHOST), whole(kb), whole(near), whole(wx)],
         out_specs=[vector, vector, vector, pl.BlockSpec((peers, 8, LANES), lambda i: (0, 0, 0))],
         out_shape=[shape, shape, shape, jax.ShapeDtypeStruct((peers, 8, LANES), F32)],
@@ -535,23 +561,23 @@
     )(in_hbm(ints), in_hbm(heights), own, left, right, kb, near, wx)
 
 
-def unpack_body(v0_ref, v1_ref, v2_ref, u0_ref, u1_ref, u2_ref, scr, flat):
+def unpack_body(v0_ref, v1_ref, v2_ref, out_ref, scr, flat):
     lane = lane_ids((16, LANES))
     run = COLUMNS * Q // 2
-    for vector, target in ((v0_ref, u0_ref), (v1_ref, u1_ref), (v2_ref, u2_ref)):
+    for k, vector in enumerate((v0_ref, v1_ref, v2_ref)):
         for y in range(ROWS):
             rows = slice(y * LOCAL, (y + 1) * LOCAL)
             for t in range(2):
                 value = vector[0, rows, t * LANES : (t + 1) * LANES]
                 if y <= Q - 1:
-                    scr[0, t, pl.ds(y, LOCAL, stride=16), :] = value
+                    scr[0, t, pl.ds(y, LOCAL, stride=PITCH), :] = value
                 if y >= Q - 1:
-                    scr[1, t, pl.ds(y - Q + 1, LOCAL, stride=16), :] = value
+                    scr[1, t, pl.ds(y - Q + 1, LOCAL, stride=PITCH), :] = value
         for ey in range(2):
             turned = []
             for r in range(2 * LOCAL):
                 start = GHOST * Q if r % 2 == 0 else 0
-                value = scr[ey, r % 2, (r // 2) * 16 : (r // 2) * 16 + 16, :]
+                value = scr[ey, r % 2, (r // 2) * PITCH : (r // 2) * PITCH + 16, :]
                 turned.append(turn(value, run * r - start))
             for tile in range(COLUMNS * Q * LOCAL // LANES):
                 low, high = tile * LANES // run, (tile * LANES + LANES - 1) // run
@@ -561,23 +587,23 @@
                 flat[tile, ey * 16 : ey * 16 + 16, :] = value
         for qy in range(Q):
             for tile in range(COLUMNS * Q * LOCAL // LANES):
-                target[0, qy, :, tile * LANES : (tile + 1) * LANES] = flat[
+                out_ref[0, k, qy, :, tile * LANES : (tile + 1) * LANES] = flat[
                     tile, pl.ds(qy, 2, stride=16), :
                 ]
 
 
 def unpack(v0, v1, v2):
     vector = pl.BlockSpec((1, ROWS * LOCAL, 2 * LANES), lambda i: (i, 0, 0))
-    target = pl.BlockSpec((1, Q, 2, COLUMNS * Q * LOCAL), lambda i: (i, 0, 0, 0))
-    shape = pltpu.HBM((3, Q, 2, COLUMNS * Q * LOCAL), F32)
+    target = pl.BlockSpec((1, 3, Q, 2, COLUMNS * Q * LOCAL), lambda i: (i, 0, 0, 0, 0))
+    shape = pltpu.HBM((3, 3, Q, 2, COLUMNS * Q * LOCAL), F32)
     return pl.pallas_call(
         unpack_body,
         grid=(3,),
         in_specs=[vector] * 3,
-        out_specs=[target] * 3,
-        out_shape=[shape] * 3,
+        out_specs=target,
+        out_shape=shape,
         scratch_shapes=[
-            pltpu.VMEM((2, 2, 256, LANES), F32),
+            pltpu.VMEM((2, 2, LOCAL * PITCH, LANES), F32),
             pltpu.VMEM((COLUMNS * Q * LOCAL // LANES, 32, LANES), F32),
         ],
         compiler_params=pltpu.CompilerParams(vmem_limit_bytes=24 * 2**20),
@@ -585,7 +611,7 @@
     )(v0, v1, v2)
 
 
-def finish_body(mom_ref, u0_ref, u1_ref, u2_ref, out_ref, coef):
+def finish_body(mom_ref, u_ref, out_ref, coef):
     comp = pl.program_id(0)
     tiles = COLUMNS * Q * LOCAL // LANES
 
@@ -630,24 +656,27 @@
         )
         for qy in range(Q):
             out_ref[0, qy, :, lanes] = (
-                c0 * u0_ref[0, qy, :, lanes]
-                + c1 * u1_ref[0, qy, :, lanes]
-                + c2 * u2_ref[0, qy, :, lanes]
+                c0 * u_ref[0, 0, qy, :, lanes]
+                + c1 * u_ref[0, 1, qy, :, lanes]
+                + c2 * u_ref[0, 2, qy, :, lanes]
             )
 
 
-def finish(moments, u0, u1, u2):
+def finish(moments, vectors):
     target = pl.BlockSpec((1, Q, 2, COLUMNS * Q * LOCAL), lambda i: (i, 0, 0, 0))
     out = pl.pallas_call(
         finish_body,
         grid=(3,),
-        in_specs=[pl.BlockSpec(moments.shape, lambda i: (0, 0, 0)), target, target, target],
+        in_specs=[
+            pl.BlockSpec(moments.shape, lambda i: (0, 0, 0)),
+            pl.BlockSpec((1, 3, Q, 2, COLUMNS * Q * LOCAL), lambda i: (i, 0, 0, 0, 0)),
+        ],
         out_specs=target,
         out_shape=jax.ShapeDtypeStruct((3, Q, 2, COLUMNS * Q * LOCAL), F32),
         scratch_shapes=[pltpu.VMEM((3, COLUMNS * Q * LOCAL // LANES, 8, LANES), F32)],
         compiler_params=pltpu.CompilerParams(vmem_limit_bytes=24 * 2**20),
         name="finish",
-    )(moments, in_hbm(u0), in_hbm(u1), in_hbm(u2))
+    )(moments, in_hbm(vectors))
     return jnp.transpose(out, (0, 2, 1, 3))
 
 
@@ -713,7 +742,7 @@
         jnp.asarray(tables["kb"]), jnp.asarray(tables["near"]), jnp.asarray(tables["wx"]), elem_count,
     )
     moments = lax.all_to_all(moments, "elem", split_axis=0, concat_axis=0, tiled=True)
-    return finish(moments, *unpack(v0, v1, v2))
+    return finish(moments, unpack(v0, v1, v2))
 
 
 def solution(mesh):

time: 112 us -> 110 us (0.982)
  blocking collectives: 27.3 us -> 26 us
    all_to_all x1, blocking collectives: 27.3 us -> 26 us  [local(): lax.all_to_all(source, 'four', split_axis=0, concat_axis=0, tiled=True)]
where the time goes in v5:
time: 110 us
  Pallas kernels  30.8 us (28%)
  starting transfers between devices  27.6 us (25%)
  blocking collectives  26 us (24%)
  waiting for transfers between devices  22.8 us (21%)
    all_to_all x1, blocking collectives, local(): lax.all_to_all(source, 'four', split_axis=0, concat_axis=0, tiled=True)  26 us
    all_to_all x1, waiting for transfers between devices, local(): lax.all_to_all(send, 'four', split_axis=0, concat_axis=0, tiled=True)  11.6 us
    all_to_all x1, starting transfers between devices, local(): lax.all_to_all(moments, 'elem', split_axis=0, concat_axis=0, tiled=True)  11.4 us
    all_to_all x1, starting transfers between devices, local(): lax.all_to_all(send, 'four', split_axis=0, concat_axis=0, tiled=True)  10.4 us
    pallas_call x1, Pallas kernels, krylov_stage(): pl.pallas_call(body, grid=(1,), in_specs=[smem, smem, chunk(COLUMNS), chu...  7.99 us
    pallas_call x1, Pallas kernels, base_stage(): pl.pallas_call(base_body, grid=(6,), in_specs=[smem, smem, smem, pl.Block...  6.97 us
    all_to_all x1, waiting for transfers between devices, local(): lax.all_to_all(moments, 'elem', split_axis=0, concat_axis=0, tiled=True)  6.68 us
    pallas_call x1, Pallas kernels, lines_stage(): pl.pallas_call(lines_body, grid=(1,), in_specs=[smem, smem, smem, whole(a...  4.91 us
  transfers between devices with their start and end apart: 4, of which 4 were waited for; matrix products, arithmetic and copies ran while one was open for 1% of the time, Pallas kernels for 9%

profile of v5, /device:TPU:8, one launch (start us, length us, event | category | flops | bytes accessed | tf_op | source)
XLA Modules:
  0.0 109.5 jit_solution(13738327695072988163)
XLA Ops:
  0.0 0.0 copy-start.6
  0.0 4.1 %pack.1 = f32[16,3,2,16,128]{4,3,2,1,0:T(8,128)} custom-call(f32[3,11,2,2816]{3,2,1,0:T(2,128)} %bitcast.3), custom_call_target="tpu_custom_call" | custom-call | tf_op jit(solution)/shard_map/pack/pallas_call | solution.py:165
  4.1 10.4 %all-to-all-start = ((f32[16,3,2,16,128]{4,3,2,1,0:T(8,128)}), f32[16,3,2,16,128]{4,3,2,1,0:T(8,128)S(1)}, u32[]{:S(2)}, u32[]{:S(2)}) async-start(f32[16,3,2,16,128]{4,3,2,1,0:T(8,128)} %pack.1), calls=%async_computation | async-start | bytes 1572864 | tf_op jit(solution)/shard_map/all_to_all | solution.py:727
  15.2 0.0 copy-done.6
  15.2 0.9 copy.16.base_ref
  16.1 0.6 pad_add_fusion.ints.refs_0_
  16.7 7.0 %base_stage.1 = (f32[4,3,2,256,128]{4,3,2,1,0:T(8,128)}, bf16[512,256]{1,0:T(8,128)(2,1)}, bf16[512,256]{1,0:T(8,128)(2,1)}, bf16[256,256]{1,0:T(8,128)(2,1)}, bf16[256,256]{1,0:T(8,128)(2,1)}) custom-call(s32[2]{0:T(128)} %pad_add_fusion.ints.refs_0_, f32[16]{0:T(128)} %widths.3, f32[2]{0:T(128)} %refs_1_.1, bf16[3,2,11,2816]{3,2,1,0:T(8,128)(2,1)} %copy.16.base_ref, ...), custom_call_target="tpu_custom_call" | custom-call | tf_op jit(solution)/shard_map/base_stage/pallas_call | solution.py:218
  23.7 11.6 %all-to-all-done.in_ref = f32[16,3,2,16,128]{4,3,2,1,0:T(8,128)S(1)} async-done(((f32[16,3,2,16,128]{4,3,2,1,0:T(8,128)}), f32[16,3,2,16,128]{4,3,2,1,0:T(8,128)S(1)}, u32[]{:S(2)}, u32[]{:S(2)}) %all-to-all-start) | async-done | bytes 786464 | tf_op jit(solution)/shard_map/all_to_all | solution.py:727
  35.3 0.0 copy-done.2
  35.3 0.0 copy-start
  35.3 0.0 copy-start.1
  35.3 0.0 copy-start.4
  35.3 4.9 %lines_stage.1 = f32[16,11,8,128]{3,2,1,0:T(8,128)S(1)} custom-call(s32[2]{0:T(128)} %pad_add_fusion.ints.refs_0_, f32[16]{0:T(128)} %widths.3, f32[2]{0:T(128)} %refs_1_.1, f32[16,3,2,16,128]{4,3,2,1,0:T(8,128)S(1)} %all-to-all-done.in_ref, f32[4,3,2,256,128]{4,3,2,1,0:T(8,128)} %get-tuple-element.14.field_hbm, bf16[512,256]{1,0:T(8,128)(2,1)} %get-tuple-element.15.fgh_ref, ...), custom_call_target="tpu_custom_call" | custom-call | tf_op jit(solution)/shard_map/lines_stage/pallas_call | solution.py:319
  40.2 26.0 %all_to_all.15.refs_2_ = f32[16,11,8,128]{3,2,1,0:T(8,128)S(1)} all-to-all(f32[16,11,8,128]{3,2,1,0:T(8,128)S(1)} %lines_stage.1), channel_id=1, replica_groups=mesh['elem'=32,'four'=16] {'four'}, dimensions={0} | all-to-all | bytes 1441792 | tf_op jit(solution)/shard_map/all_to_all | solution.py:736
  66.2 2.3 %collective-permute-start.1 = (f32[3,11,8,128]{3,2,1,0:T(8,128)S(1)}, f32[3,11,8,128]{3,2,1,0:T(8,128)S(1)}, u32[]{:S(2)}, u32[]{:S(2)}) collective-permute-start(f32[3,11,8,128]{3,2,1,0:T(8,128)S(1)} %get-tuple-element.23), channel_id=1, source_target_pairs={{16,0},{32,16},{48,32},{64,48},{80,64},{96,80},{112,96},{128,112},... | collective-permute-start | bytes 405512 | tf_op jit(solution)/shard_map/ppermute | solution.py:739
  68.6 3.5 %collective-permute-start = (f32[3,11,8,128]{3,2,1,0:T(8,128)S(1)}, f32[3,11,8,128]{3,2,1,0:T(8,128)S(1)}, u32[]{:S(2)}, u32[]{:S(2)}) collective-permute-start(f32[3,11,8,128]{3,2,1,0:T(8,128)S(1)} %get-tuple-element.24), channel_id=1, source_target_pairs={{0,16},{16,32},{32,48},{48,64},{64,80},{80,96},{96,112},{112,128},... | collective-permute-start | bytes 405512 | tf_op jit(solution)/shard_map/ppermute | solution.py:738
  72.1 2.4 %collective-permute-done.1.refs_4_ = f32[3,11,8,128]{3,2,1,0:T(8,128)S(1)} collective-permute-done((f32[3,11,8,128]{3,2,1,0:T(8,128)S(1)}, f32[3,11,8,128]{3,2,1,0:T(8,128)S(1)}, u32[]{:S(2)}, u32[]{:S(2)}) %collective-permute-start.1) | collective-permute-done | bytes 135200 | tf_op jit(solution)/shard_map/ppermute | solution.py:739
  74.5 2.1 %collective-permute-done.refs_3_ = f32[3,11,8,128]{3,2,1,0:T(8,128)S(1)} collective-permute-done((f32[3,11,8,128]{3,2,1,0:T(8,128)S(1)}, f32[3,11,8,128]{3,2,1,0:T(8,128)S(1)}, u32[]{:S(2)}, u32[]{:S(2)}) %collective-permute-start) | collective-permute-done | bytes 135200 | tf_op jit(solution)/shard_map/ppermute | solution.py:738
  76.6 0.0 copy-done
  76.6 8.0 %krylov_stage.1 = (f32[3,336,256]{2,1,0:T(8,128)S(1)}, f32[3,336,256]{2,1,0:T(8,128)S(1)}, f32[3,336,256]{2,1,0:T(8,128)S(1)}, f32[32,8,128]{2,1,0:T(8,128)}) custom-call(s32[2]{0:T(128)} %pad_add_fusion.ints.refs_0_, f32[2]{0:T(128)} %refs_1_.1, f32[16,11,8,128]{3,2,1,0:T(8,128)S(1)} %all_to_all.15.refs_2_, ...), custom_call_target="tpu_custom_call" | custom-call | tf_op jit(solution)/shard_map/krylov_stage/pallas_call | solution.py:546
  84.6 11.4 %all-to-all-start.2 = ((f32[32,8,128]{2,1,0:T(8,128)}), f32[32,8,128]{2,1,0:T(8,128)S(1)}, u32[]{:S(2)}, u32[]{:S(2)}) async-start(f32[32,8,128]{2,1,0:T(8,128)} %get-tuple-element.19), calls=%async_computation.2 | async-start | bytes 262144 | tf_op jit(solution)/shard_map/all_to_all | solution.py:744
  96.0 3.1 %unpack.1.u_ref = f32[3,3,11,2,2816]{4,3,2,1,0:T(2,128)} custom-call(f32[3,336,256]{2,1,0:T(8,128)S(1)} %get-tuple-element.20.v0_ref, f32[3,336,256]{2,1,0:T(8,128)S(1)} %get-tuple-element.21.v1_ref, f32[3,336,256]{2,1,0:T(8,128)S(1)} %get-tuple-element.22.v2_ref), custom_call_target="tpu_custom_call" | custom-call | tf_op jit(solution)/shard_map/unpack/pallas_call | solution.py:599
  99.1 6.7 %all-to-all-done.2.mom_ref = f32[32,8,128]{2,1,0:T(8,128)S(1)} async-done(((f32[32,8,128]{2,1,0:T(8,128)}), f32[32,8,128]{2,1,0:T(8,128)S(1)}, u32[]{:S(2)}, u32[]{:S(2)}) %all-to-all-start.2) | async-done | bytes 131104 | tf_op jit(solution)/shard_map/all_to_all | solution.py:744
  105.7 3.8 %finish.1 = f32[3,11,2,2816]{3,2,1,0:T(2,128)} custom-call(f32[32,8,128]{2,1,0:T(8,128)S(1)} %all-to-all-done.2.mom_ref, f32[3,3,11,2,2816]{4,3,2,1,0:T(2,128)} %unpack.1.u_ref), custom_call_target="tpu_custom_call" | custom-call | tf_op jit(solution)/shard_map/finish/pallas_call | solution.py:667
  (8 shorter events, 0.0 us)
Async XLA Ops:
  0.0 35.3 %copy-start.5 = (f32[1,128]{1,0:T(1,128)S(1)}, f32[1,128]{1,0:T(1,128)}, u32[]{:S(2)}) copy-start(f32[1,128]{1,0:T(1,128)} %constant.30.clone.mass_ref) | copy-start | bytes 1540
  0.0 35.3 %copy-start.2 = (bf16[128,256]{1,0:T(8,128)(2,1)S(1)}, bf16[128,256]{1,0:T(8,128)(2,1)}, u32[]{:S(2)}) copy-start(bf16[128,256]{1,0:T(8,128)(2,1)} %constant.29.clone.dl_ref) | copy-start | bytes 196612
  0.0 35.3 %copy-start.3 = (bf16[128,256]{1,0:T(8,128)(2,1)S(1)}, bf16[128,256]{1,0:T(8,128)(2,1)}, u32[]{:S(2)}) copy-start(bf16[128,256]{1,0:T(8,128)(2,1)} %constant.28.clone.dh_ref) | copy-start | bytes 196612
  0.0 15.2 %copy-start.6 = (bf16[3,2,11,2816]{3,1,2,0:T(2,128)(2,1)S(1)}, bf16[3,2,11,2816]{3,1,2,0:T(2,128)(2,1)}, u32[]{:S(2)}) copy-start(bf16[3,2,11,2816]{3,1,2,0:T(2,128)(2,1)} %param.16) | copy-start | bytes 1115140
  4.1 31.1 %all-to-all-start = ((f32[16,3,2,16,128]{4,3,2,1,0:T(8,128)}), f32[16,3,2,16,128]{4,3,2,1,0:T(8,128)S(1)}, u32[]{:S(2)}, u32[]{:S(2)}) async-start(f32[16,3,2,16,128]{4,3,2,1,0:T(8,128)} %pack.1), calls=%async_computation | async-start | bytes 1572864 | tf_op jit(solution)/shard_map/all_to_all | solution.py:727
  35.3 41.3 %copy-start = (f32[256,256]{1,0:T(8,128)S(1)}, f32[256,256]{1,0:T(8,128)}, u32[]{:S(2)}) copy-start(f32[256,256]{1,0:T(8,128)} %constant.32.clone.refs_6_) | copy-start | bytes 786436
  35.3 41.3 %copy-start.1 = (f32[256,256]{1,0:T(8,128)S(1)}, f32[256,256]{1,0:T(8,128)}, u32[]{:S(2)}) copy-start(f32[256,256]{1,0:T(8,128)} %constant.31.clone.refs_5_) | copy-start | bytes 786436
  35.3 41.3 %copy-start.4 = (f32[1,256]{1,0:T(1,128)S(1)}, f32[1,256]{1,0:T(1,128)}, u32[]{:S(2)}) copy-start(f32[1,256]{1,0:T(1,128)} %constant.33.clone.refs_7_) | copy-start | bytes 3076
  66.2 8.3 %collective-permute-start.1 = (f32[3,11,8,128]{3,2,1,0:T(8,128)S(1)}, f32[3,11,8,128]{3,2,1,0:T(8,128)S(1)}, u32[]{:S(2)}, u32[]{:S(2)}) collective-permute-start(f32[3,11,8,128]{3,2,1,0:T(8,128)S(1)} %get-tuple-element.23), channel_id=1, source_target_pairs={{16,0},{32,16},{48,32},{64,48},{80,64},{96,80},{112,96},{128,112},... | collective-permute-start | bytes 405512 | tf_op jit(solution)/shard_map/ppermute | solution.py:739
  68.6 8.0 %collective-permute-start = (f32[3,11,8,128]{3,2,1,0:T(8,128)S(1)}, f32[3,11,8,128]{3,2,1,0:T(8,128)S(1)}, u32[]{:S(2)}, u32[]{:S(2)}) collective-permute-start(f32[3,11,8,128]{3,2,1,0:T(8,128)S(1)} %get-tuple-element.24), channel_id=1, source_target_pairs={{0,16},{16,32},{32,48},{48,64},{64,80},{80,96},{96,112},{112,128},... | collective-permute-start | bytes 405512 | tf_op jit(solution)/shard_map/ppermute | solution.py:738
  84.6 21.1 %all-to-all-start.2 = ((f32[32,8,128]{2,1,0:T(8,128)}), f32[32,8,128]{2,1,0:T(8,128)S(1)}, u32[]{:S(2)}, u32[]{:S(2)}) async-start(f32[32,8,128]{2,1,0:T(8,128)} %get-tuple-element.19), calls=%async_computation.2 | async-start | bytes 262144 | tf_op jit(solution)/shard_map/all_to_all | solution.py:744

commit v6 on v5

--- a/solution.py
+++ b/solution.py
@@ -114,6 +114,16 @@
     return pltpu.with_memory_space_constraint(array, pltpu.HBM)
 
 
+def to_groups(array):
+    array = jnp.transpose(array, (0, 2, 1, 3)).reshape(3, Q, 2, Q, 2, LANES)
+    return jnp.transpose(array, (0, 1, 3, 4, 2, 5)).reshape(3, NODES, 4, LANES)
+
+
+def from_groups(array):
+    array = jnp.transpose(array.reshape(3, Q, Q, 2, 2, LANES), (0, 1, 4, 2, 3, 5))
+    return jnp.transpose(array.reshape(3, Q, 2, COLUMNS * Q * LOCAL), (0, 2, 1, 3))
+
+
 def lane_ids(shape):
     return lax.broadcasted_iota(jnp.int32, shape, len(shape) - 1)
 
@@ -123,16 +133,19 @@
     return value if shift == 0 else pltpu.roll(value, shift, value.ndim - 1)
 
 
-def block_transpose(arrays, places, offset=0):
+def block_transpose(arrays, places, offset=0, first=0):
     lane = lane_ids(arrays[0].shape)
-    turned = [turn(array, Q * k - offset) for k, array in enumerate(arrays)]
+    turned = [turn(array, Q * (first + k) - offset) for k, array in enumerate(arrays)]
     results = []
     for place in places:
         distance = (lane - Q * place) & (LANES - 1)
         chosen = turned[0]
         for k in range(1, len(turned)):
-            chosen = jnp.where(distance >= Q * k, turned[k], chosen)
-        chosen = jnp.where(distance < NODES, chosen, 0.0)
+            chosen = jnp.where(distance >= Q * (first + k), turned[k], chosen)
+        inside = distance < Q * (first + len(turned))
+        if first:
+            inside = inside & (distance >= Q * first)
+        chosen = jnp.where(inside, chosen, 0.0)
         results.append(turn(chosen, -Q * place))
     return results
 
@@ -142,17 +155,20 @@
     scratches = (scr0, scr1)
     tiles = COLUMNS * Q * LOCAL // LANES
     for qy in range(Q):
-        for tile in range(tiles):
-            flat[tile, pl.ds(qy, 2, stride=16), :] = in_ref[0, qy, :, tile * LANES : (tile + 1) * LANES]
+        for pair in range(Q):
+            flat[pair, pl.ds(qy, 4, stride=16), :] = in_ref[0, qy * Q + pair]
     for ey in range(2):
-        rows = slice(ey * 16, ey * 16 + 16)
+        def read(tile):
+            low = (tile % 2) * 32 + ey * 16
+            return flat[tile // 2, low : low + 16, :]
+
         for j in range(LOCAL):
             for t in range(2):
                 offset = j * COLUMNS * Q + NODES * t
                 tile, shift = offset // LANES, offset % LANES
-                first = flat[tile, rows, :]
+                first = read(tile)
                 if shift and tile + 1 < tiles:
-                    first = jnp.where(lane >= shift, first, flat[tile + 1, rows, :])
+                    first = jnp.where(lane >= shift, first, read(tile + 1))
                 scratches[t][ey, j * PITCH : j * PITCH + 16, :] = turn(first, -shift)
     for ey in range(2):
         for t in range(2):
@@ -165,17 +181,17 @@
     return pl.pallas_call(
         pack_body,
         grid=(3,),
-        in_specs=[pl.BlockSpec((1, Q, 2, COLUMNS * Q * LOCAL), lambda i: (i, 0, 0, 0))],
+        in_specs=[pl.BlockSpec((1, NODES, 4, LANES), lambda i: (i, 0, 0, 0))],
         out_specs=pl.BlockSpec((PEERS, 1, 2, LOCAL, LANES), lambda i: (0, i, 0, 0, 0)),
         out_shape=jax.ShapeDtypeStruct((PEERS, 3, 2, LOCAL, LANES), F32),
         scratch_shapes=[
-            pltpu.VMEM((COLUMNS * Q * LOCAL // LANES, 32, LANES), F32),
+            pltpu.VMEM((Q, 64, LANES), F32),
             pltpu.VMEM((2, LOCAL * PITCH, LANES), F32),
             pltpu.VMEM((2, LOCAL * PITCH, LANES), F32),
         ],
         compiler_params=pltpu.CompilerParams(vmem_limit_bytes=24 * 2**20),
         name="pack",
-    )(in_hbm(jnp.transpose(adjoint, (0, 2, 1, 3))))
+    )(in_hbm(to_groups(adjoint)))
 
 
 def base_body(ints, widths, heights, base_ref, table_ref, stack_ref, dzh_ref, dzl_ref,
@@ -335,7 +351,7 @@
     )(*map(in_hbm, (ints, widths, heights)), arrived, in_hbm(fields), *map(in_hbm, tables), d_high, d_low, mass)
 
 
-def join_columns(chunks, offset):
+def join_columns(chunks, offset, partial=()):
     lane = (lane_ids(chunks[0].shape) - offset) & (LANES - 1)
     place = lane - Q * ((lane * 5958) >> 16)
     at_first = (place == 0) & (lane < NODES)
@@ -347,8 +363,55 @@
             extra = jnp.where(at_first, turn(chunks[k - 1], -(Q - 1)), extra)
         if k + 1 < len(chunks):
             extra = jnp.where(at_last, turn(chunks[k + 1], Q - 1), extra)
-        results.append(chunk + extra)
+        results.append(extra if k in partial else chunk + extra)
     return results
+
+
+def windows(refs, start):
+    tile, offset = start // LANES, start % LANES
+    chunks = [ref[tile] for ref in refs]
+    if offset:
+        lane = lane_ids((8, LANES))
+        chunks = [
+            jnp.where(lane >= offset, chunk, ref[tile + 1]) for chunk, ref in zip(chunks, refs)
+        ]
+    return chunks, offset
+
+
+def face_parts():
+    for comp in range(3):
+        for half in range(2):
+            for ey in range(2):
+                start = (half * 3 + comp) * FACE + (NODES - Q) * ey
+                yield comp, start, range(ey, Q), (Q - 1) * ey * LOCAL + half * 8
+
+
+def place_body(own_ref, out_ref):
+    refs = [own_ref.at[k] for k in range(COLUMNS)]
+    cut = Q - GHOST
+    for comp, start, places, base in face_parts():
+        chunks, offset = windows(refs, start)
+        chunks = join_columns(chunks, offset)
+        sides = [
+            block_transpose(chunks[:cut], places, offset, GHOST),
+            block_transpose(chunks[cut:], places, offset),
+        ]
+        for t, values in enumerate(sides):
+            for qy, value in zip(places, values):
+                row = base + qy * LOCAL
+                out_ref[comp, row : row + 8, t * LANES : (t + 1) * LANES] = value
+
+
+def place_stage(own):
+    return pl.pallas_call(
+        place_body,
+        grid=(1,),
+        in_specs=[pl.BlockSpec(own.shape, lambda i: (0, 0, 0, 0))],
+        out_specs=pl.BlockSpec((3, ROWS * LOCAL, 2 * LANES), lambda i: (0, 0, 0)),
+        out_shape=jax.ShapeDtypeStruct((3, ROWS * LOCAL, 2 * LANES), F32),
+        compiler_params=pltpu.CompilerParams(vmem_limit_bytes=24 * 2**20),
+        name="place_stage",
+    )(own)
 
 
 def split3(value):
@@ -396,7 +459,7 @@
     return results
 
 
-def krylov_body(stiff_y, weights, ints, heights, own_ref, left_ref, right_ref, kb_ref, kn_ref, wx_ref,
+def krylov_body(stiff_y, weights, ints, heights, placed_ref, own_ref, left_ref, right_ref, kb_ref, kn_ref, wx_ref,
                 v0_ref, v1_ref, v2_ref, mom_ref, kxs, kbs, vec, prod, tmp):
     column_refs = (
         [left_ref.at[k] for k in range(GHOST)]
@@ -494,27 +557,21 @@
             prod[low_key * LOCAL + half * 8 : low_key * LOCAL + half * 8 + 8, :] = square
             prod[(low_key + 1) * LOCAL + half * 8 : (low_key + 1) * LOCAL + half * 8 + 8, :] = cross
 
-    lane = lane_ids((8, LANES))
+    cut = Q - GHOST - 1
+    for comp, start, places, base in face_parts():
+        left, offset = windows(column_refs[: GHOST + 1], start)
+        right, _ = windows(column_refs[-GHOST - 1 :], start)
+        sides = [
+            block_transpose(join_columns(left, offset, (GHOST,)), places, offset),
+            block_transpose(join_columns(right, offset, (0,)), places, offset, cut),
+        ]
+        for t, values in enumerate(sides):
+            lanes = slice(t * LANES, (t + 1) * LANES)
+            for qy, value in zip(places, values):
+                rows = slice(base + qy * LOCAL, base + qy * LOCAL + 8)
+                v0_ref[comp, rows, lanes] = placed_ref[comp, rows, lanes] + value
     for comp in range(3):
         first, second, third = v0_ref.at[comp], v1_ref.at[comp], v2_ref.at[comp]
-        for half in range(2):
-            for ey in range(2):
-                start = (half * 3 + comp) * FACE + (NODES - Q) * ey
-                tile, offset = start // LANES, start % LANES
-                chunks = [ref[tile] for ref in column_refs]
-                if offset:
-                    chunks = [
-                        jnp.where(lane >= offset, chunk, ref[tile + 1])
-                        for chunk, ref in zip(chunks, column_refs)
-                    ]
-                chunks = join_columns(chunks, offset)
-                places = range(ey, Q)
-                for t in range(2):
-                    for qy, value in zip(
-                        places, block_transpose(chunks[Q * t : Q * t + Q], places, offset)
-                    ):
-                        row = (qy + (Q - 1) * ey) * LOCAL + half * 8
-                        first[row : row + 8, t * LANES : (t + 1) * LANES] = value
         prod[6 * LOCAL :, :] = jnp.zeros((LANES - 6 * LOCAL, LANES), F32)
         apply(first, second, kxs, 1, 0)
         apply(second, third, kxs, 1, 2)
@@ -528,7 +585,7 @@
         )
 
 
-def krylov_stage(stiff_y, weights, ints, heights, own, left, right, kb, near, wx, peers):
+def krylov_stage(stiff_y, weights, ints, heights, placed, own, left, right, kb, near, wx, peers):
     smem = pl.BlockSpec(memory_space=pltpu.SMEM)
 
     def whole(array):
@@ -546,7 +603,7 @@
     return pl.pallas_call(
         body,
         grid=(1,),
-        in_specs=[smem, smem, chunk(COLUMNS), chunk(GHOST), chunk(GHOST), whole(kb), whole(near), whole(wx)],
+        in_specs=[smem, smem, vector, chunk(COLUMNS), chunk(GHOST), chunk(GHOST), whole(kb), whole(near), whole(wx)],
         out_specs=[vector, vector, vector, pl.BlockSpec((peers, 8, LANES), lambda i: (0, 0, 0))],
         out_shape=[shape, shape, shape, jax.ShapeDtypeStruct((peers, 8, LANES), F32)],
         scratch_shapes=[
@@ -558,7 +615,7 @@
         ],
         compiler_params=pltpu.CompilerParams(vmem_limit_bytes=24 * 2**20),
         name="krylov_stage",
-    )(in_hbm(ints), in_hbm(heights), own, left, right, kb, near, wx)
+    )(in_hbm(ints), in_hbm(heights), placed, own, left, right, kb, near, wx)
 
 
 def unpack_body(v0_ref, v1_ref, v2_ref, out_ref, scr, flat):
@@ -584,18 +641,17 @@
                 value = turned[low]
                 for r in range(low + 1, high + 1):
                     value = jnp.where(lane >= run * r - LANES * tile, turned[r], value)
-                flat[tile, ey * 16 : ey * 16 + 16, :] = value
+                place = (tile % 2) * 32 + ey * 16
+                flat[tile // 2, place : place + 16, :] = value
         for qy in range(Q):
-            for tile in range(COLUMNS * Q * LOCAL // LANES):
-                out_ref[0, k, qy, :, tile * LANES : (tile + 1) * LANES] = flat[
-                    tile, pl.ds(qy, 2, stride=16), :
-                ]
+            for pair in range(Q):
+                out_ref[0, k, qy * Q + pair] = flat[pair, pl.ds(qy, 4, stride=16), :]
 
 
 def unpack(v0, v1, v2):
     vector = pl.BlockSpec((1, ROWS * LOCAL, 2 * LANES), lambda i: (i, 0, 0))
-    target = pl.BlockSpec((1, 3, Q, 2, COLUMNS * Q * LOCAL), lambda i: (i, 0, 0, 0, 0))
-    shape = pltpu.HBM((3, 3, Q, 2, COLUMNS * Q * LOCAL), F32)
+    target = pl.BlockSpec((1, 3, NODES, 4, LANES), lambda i: (i, 0, 0, 0, 0))
+    shape = pltpu.HBM((3, 3, NODES, 4, LANES), F32)
     return pl.pallas_call(
         unpack_body,
         grid=(3,),
@@ -604,7 +660,7 @@
         out_shape=shape,
         scratch_shapes=[
             pltpu.VMEM((2, 2, LOCAL * PITCH, LANES), F32),
-            pltpu.VMEM((COLUMNS * Q * LOCAL // LANES, 32, LANES), F32),
+            pltpu.VMEM((Q, 64, LANES), F32),
         ],
         compiler_params=pltpu.CompilerParams(vmem_limit_bytes=24 * 2**20),
         name="unpack",
@@ -649,35 +705,39 @@
                     chosen = jnp.where(lane >= COLUMNS * Q * high - LANES * tile, wide[high], chosen)
                 coef[k, tile] = chosen
 
-    for tile in range(tiles):
-        lanes = slice(tile * LANES, (tile + 1) * LANES)
-        c0, c1, c2 = (
-            jnp.broadcast_to(coef[k, tile, pl.ds(comp, 1), :], (2, LANES)) for k in range(3)
-        )
+    upper = lax.broadcasted_iota(jnp.int32, (4, LANES), 0) >= 2
+    for pair in range(Q):
+        factors = []
+        for k in range(3):
+            one, two = (
+                jnp.broadcast_to(coef[k, 2 * pair + side, pl.ds(comp, 1), :], (4, LANES))
+                for side in range(2)
+            )
+            factors.append(jnp.where(upper, two, one))
         for qy in range(Q):
-            out_ref[0, qy, :, lanes] = (
-                c0 * u_ref[0, 0, qy, :, lanes]
-                + c1 * u_ref[0, 1, qy, :, lanes]
-                + c2 * u_ref[0, 2, qy, :, lanes]
+            group = qy * Q + pair
+            out_ref[0, group] = (
+                factors[0] * u_ref[0, 0, group]
+                + factors[1] * u_ref[0, 1, group]
+                + factors[2] * u_ref[0, 2, group]
             )
 
 
 def finish(moments, vectors):
-    target = pl.BlockSpec((1, Q, 2, COLUMNS * Q * LOCAL), lambda i: (i, 0, 0, 0))
     out = pl.pallas_call(
         finish_body,
         grid=(3,),
         in_specs=[
             pl.BlockSpec(moments.shape, lambda i: (0, 0, 0)),
-            pl.BlockSpec((1, 3, Q, 2, COLUMNS * Q * LOCAL), lambda i: (i, 0, 0, 0, 0)),
+            pl.BlockSpec((1, 3, NODES, 4, LANES), lambda i: (i, 0, 0, 0, 0)),
         ],
-        out_specs=target,
-        out_shape=jax.ShapeDtypeStruct((3, Q, 2, COLUMNS * Q * LOCAL), F32),
+        out_specs=pl.BlockSpec((1, NODES, 4, LANES), lambda i: (i, 0, 0, 0)),
+        out_shape=jax.ShapeDtypeStruct((3, NODES, 4, LANES), F32),
         scratch_shapes=[pltpu.VMEM((3, COLUMNS * Q * LOCAL // LANES, 8, LANES), F32)],
         compiler_params=pltpu.CompilerParams(vmem_limit_bytes=24 * 2**20),
         name="finish",
     )(moments, in_hbm(vectors))
-    return jnp.transpose(out, (0, 2, 1, 3))
+    return from_groups(out)
 
 
 def make_tables():
@@ -738,7 +798,7 @@
     left = lax.ppermute(own[COLUMNS - GHOST :], "elem", up)
     right = lax.ppermute(own[:GHOST], "elem", [(j, i) for i, j in up])
     v0, v1, v2, moments = krylov_stage(
-        tables["stiff"], tables["weights"], ints, row_heights, own, left, right,
+        tables["stiff"], tables["weights"], ints, row_heights, place_stage(own), own, left, right,
         jnp.asarray(tables["kb"]), jnp.asarray(tables["near"]), jnp.asarray(tables["wx"]), elem_count,
     )
     moments = lax.all_to_all(moments, "elem", split_axis=0, concat_axis=0, tiled=True)

time: 110 us -> 110 us (level)
  waiting for transfers between devices: 22.8 us -> 20.3 us
  Pallas kernels: 30.8 us -> 32.6 us
    ppermute x1, waiting for transfers between devices: 2.45 us -> 0.01 us  [local(): right = lax.ppermute(own[:GHOST], 'elem', [(j, i) for i, j in up])]
    pallas_call x2 -> x3, Pallas kernels: 12.1 us -> 14.2 us  [the longest x1 7.44 us: krylov_stage(): pl.pallas_call(body, grid=(1,), in_specs=[smem, smem, vector, chunk(COLUM...]
  transfers between devices with their start and end apart: 4 -> 4, of which waited for: 4 -> 3; matrix products, arithmetic and copies ran while one was open for 1% -> 1% of each run, Pallas kernels for 9% -> 12%
where the time goes in v6:
time: 110 us; the launch traced here: 109 us
  Pallas kernels  32.6 us (30%)
  starting transfers between devices  27.6 us (25%)
  blocking collectives  26.1 us (24%)
  waiting for transfers between devices  20.3 us (18%)
    all_to_all x1, blocking collectives, local(): lax.all_to_all(source, 'four', split_axis=0, concat_axis=0, tiled=True)  26.1 us
    all_to_all x1, waiting for transfers between devices, local(): lax.all_to_all(send, 'four', split_axis=0, concat_axis=0, tiled=True)  11.6 us
    all_to_all x1, starting transfers between devices, local(): lax.all_to_all(moments, 'elem', split_axis=0, concat_axis=0, tiled=True)  11.4 us
    all_to_all x1, starting transfers between devices, local(): lax.all_to_all(send, 'four', split_axis=0, concat_axis=0, tiled=True)  10.4 us
    pallas_call x1, Pallas kernels, krylov_stage(): pl.pallas_call(body, grid=(1,), in_specs=[smem, smem, vector, chunk(COLUM...  7.44 us
    pallas_call x1, Pallas kernels, base_stage(): pl.pallas_call(base_body, grid=(6,), in_specs=[smem, smem, smem, pl.Block...  6.97 us
    all_to_all x1, waiting for transfers between devices, local(): lax.all_to_all(moments, 'elem', split_axis=0, concat_axis=0, tiled=True)  6.8 us
    pallas_call x1, Pallas kernels, lines_stage(): pl.pallas_call(lines_body, grid=(1,), in_specs=[smem, smem, smem, whole(a...  4.84 us
  transfers between devices with their start and end apart: 4, of which 3 were waited for; matrix products, arithmetic and copies ran while one was open for 1% of the time, Pallas kernels for 12%

profile of v6, /device:TPU:8, one launch (start us, length us, event | category | flops | bytes accessed | tf_op | source)
XLA Modules:
  0.0 108.9 jit_solution(15130989370418885821)
XLA Ops:
  0.0 4.1 %pack.1 = f32[16,3,2,16,128]{4,3,2,1,0:T(8,128)} custom-call(f32[3,121,4,128]{3,2,1,0:T(4,128)} %bitcast.15), custom_call_target="tpu_custom_call" | custom-call | tf_op jit(solution)/shard_map/pack/pallas_call | solution.py:181
  4.1 10.4 %all-to-all-start = ((f32[16,3,2,16,128]{4,3,2,1,0:T(8,128)}), f32[16,3,2,16,128]{4,3,2,1,0:T(8,128)S(1)}, u32[]{:S(2)}, u32[]{:S(2)}) async-start(f32[16,3,2,16,128]{4,3,2,1,0:T(8,128)} %pack.1), calls=%async_computation | async-start | bytes 1572864 | tf_op jit(solution)/shard_map/all_to_all | solution.py:787
  15.2 0.0 copy-done.6
  15.2 0.9 copy.17.base_ref
  16.1 0.6 pad_add_fusion.ints.refs_0_
  16.7 7.0 %base_stage.1 = (f32[4,3,2,256,128]{4,3,2,1,0:T(8,128)}, bf16[512,256]{1,0:T(8,128)(2,1)}, bf16[512,256]{1,0:T(8,128)(2,1)}, bf16[256,256]{1,0:T(8,128)(2,1)}, bf16[256,256]{1,0:T(8,128)(2,1)}) custom-call(s32[2]{0:T(128)} %pad_add_fusion.ints.refs_0_, f32[16]{0:T(128)} %widths.3, f32[2]{0:T(128)} %refs_1_.1, bf16[3,2,11,2816]{3,2,1,0:T(8,128)(2,1)} %copy.17.base_ref, ...), custom_call_target="tpu_custom_call" | custom-call | tf_op jit(solution)/shard_map/base_stage/pallas_call | solution.py:234
  23.6 11.6 %all-to-all-done.in_ref = f32[16,3,2,16,128]{4,3,2,1,0:T(8,128)S(1)} async-done(((f32[16,3,2,16,128]{4,3,2,1,0:T(8,128)}), f32[16,3,2,16,128]{4,3,2,1,0:T(8,128)S(1)}, u32[]{:S(2)}, u32[]{:S(2)}) %all-to-all-start) | async-done | bytes 786464 | tf_op jit(solution)/shard_map/all_to_all | solution.py:787
  35.3 0.0 copy-done.3
  35.3 4.8 %lines_stage.1 = f32[16,11,8,128]{3,2,1,0:T(8,128)S(1)} custom-call(s32[2]{0:T(128)} %pad_add_fusion.ints.refs_0_, f32[16]{0:T(128)} %widths.3, f32[2]{0:T(128)} %refs_1_.1, f32[16,3,2,16,128]{4,3,2,1,0:T(8,128)S(1)} %all-to-all-done.in_ref, f32[4,3,2,256,128]{4,3,2,1,0:T(8,128)} %get-tuple-element.14.field_hbm, bf16[512,256]{1,0:T(8,128)(2,1)} %get-tuple-element.15.fgh_ref, ...), custom_call_target="tpu_custom_call" | custom-call | tf_op jit(solution)/shard_map/lines_stage/pallas_call | solution.py:335
  40.1 0.0 copy-start
  40.1 0.0 copy-start.1
  40.1 0.0 copy-start.4
  40.1 26.1 %all_to_all.15.own_ref.refs_3_ = f32[16,11,8,128]{3,2,1,0:T(8,128)S(1)} all-to-all(f32[16,11,8,128]{3,2,1,0:T(8,128)S(1)} %lines_stage.1), channel_id=1, replica_groups=mesh['elem'=32,'four'=16] {'four'}, dimensions={0} | all-to-all | bytes 1441792 | tf_op jit(solution)/shard_map/all_to_all | solution.py:796
  66.3 2.4 %collective-permute-start.1 = (f32[3,11,8,128]{3,2,1,0:T(8,128)S(1)}, f32[3,11,8,128]{3,2,1,0:T(8,128)S(1)}, u32[]{:S(2)}, u32[]{:S(2)}) collective-permute-start(f32[3,11,8,128]{3,2,1,0:T(8,128)S(1)} %get-tuple-element.23), channel_id=1, source_target_pairs={{16,0},{32,16},{48,32},{64,48},{80,64},{96,80},{112,96},{128,112},... | collective-permute-start | bytes 405512 | tf_op jit(solution)/shard_map/ppermute | solution.py:799
  68.6 3.5 %collective-permute-start = (f32[3,11,8,128]{3,2,1,0:T(8,128)S(1)}, f32[3,11,8,128]{3,2,1,0:T(8,128)S(1)}, u32[]{:S(2)}, u32[]{:S(2)}) collective-permute-start(f32[3,11,8,128]{3,2,1,0:T(8,128)S(1)} %get-tuple-element.24), channel_id=1, source_target_pairs={{0,16},{16,32},{32,48},{48,64},{64,80},{80,96},{96,112},{112,128},... | collective-permute-start | bytes 405512 | tf_op jit(solution)/shard_map/ppermute | solution.py:798
  72.1 2.7 %place_stage.1.refs_2_ = f32[3,336,256]{2,1,0:T(8,128)S(1)} custom-call(f32[16,11,8,128]{3,2,1,0:T(8,128)S(1)} %all_to_all.15.own_ref.refs_3_), custom_call_target="tpu_custom_call" | custom-call | tf_op jit(solution)/shard_map/place_stage/pallas_call | solution.py:406
  74.8 0.0 collective-permute-done.1.refs_5_
  74.8 1.9 %collective-permute-done.refs_4_ = f32[3,11,8,128]{3,2,1,0:T(8,128)S(1)} collective-permute-done((f32[3,11,8,128]{3,2,1,0:T(8,128)S(1)}, f32[3,11,8,128]{3,2,1,0:T(8,128)S(1)}, u32[]{:S(2)}, u32[]{:S(2)}) %collective-permute-start) | collective-permute-done | bytes 135200 | tf_op jit(solution)/shard_map/ppermute | solution.py:798
  76.7 0.0 copy-done.4
  76.7 7.4 %krylov_stage.1 = (f32[3,336,256]{2,1,0:T(8,128)S(1)}, f32[3,336,256]{2,1,0:T(8,128)S(1)}, f32[3,336,256]{2,1,0:T(8,128)S(1)}, f32[32,8,128]{2,1,0:T(8,128)}) custom-call(s32[2]{0:T(128)} %pad_add_fusion.ints.refs_0_, f32[2]{0:T(128)} %refs_1_.1, f32[3,336,256]{2,1,0:T(8,128)S(1)} %place_stage.1.refs_2_, f32[16,11,8,128]{3,2,1,0:T(8,128)S(1)} %all_to_all.15.own_ref.refs_3_, ...), custom_call_target="tpu_custom_call" | custom-call | tf_op jit(solution)/shard_map/krylov_stage/pallas_call | solution.py:603
  84.1 11.4 %all-to-all-start.2 = ((f32[32,8,128]{2,1,0:T(8,128)}), f32[32,8,128]{2,1,0:T(8,128)S(1)}, u32[]{:S(2)}, u32[]{:S(2)}) async-start(f32[32,8,128]{2,1,0:T(8,128)} %get-tuple-element.19), calls=%async_computation.2 | async-start | bytes 262144 | tf_op jit(solution)/shard_map/all_to_all | solution.py:804
  95.5 2.9 %unpack.1.u_ref = f32[3,3,121,4,128]{4,3,2,1,0:T(4,128)} custom-call(f32[3,336,256]{2,1,0:T(8,128)S(1)} %get-tuple-element.20.v0_ref, f32[3,336,256]{2,1,0:T(8,128)S(1)} %get-tuple-element.21.v1_ref, f32[3,336,256]{2,1,0:T(8,128)S(1)} %get-tuple-element.22.v2_ref), custom_call_target="tpu_custom_call" | custom-call | tf_op jit(solution)/shard_map/unpack/pallas_call | solution.py:655
  98.5 6.8 %all-to-all-done.2.mom_ref = f32[32,8,128]{2,1,0:T(8,128)S(1)} async-done(((f32[32,8,128]{2,1,0:T(8,128)}), f32[32,8,128]{2,1,0:T(8,128)S(1)}, u32[]{:S(2)}, u32[]{:S(2)}) %all-to-all-start.2) | async-done | bytes 131104 | tf_op jit(solution)/shard_map/all_to_all | solution.py:804
  105.3 3.6 %finish.1 = f32[3,121,4,128]{3,2,1,0:T(4,128)} custom-call(f32[32,8,128]{2,1,0:T(8,128)S(1)} %all-to-all-done.2.mom_ref, f32[3,3,121,4,128]{4,3,2,1,0:T(4,128)} %unpack.1.u_ref), custom_call_target="tpu_custom_call" | custom-call | tf_op jit(solution)/shard_map/finish/pallas_call | solution.py:727
  (9 shorter events, 0.0 us)
Async XLA Ops:
  0.0 35.2 %copy-start.5 = (f32[1,128]{1,0:T(1,128)S(1)}, f32[1,128]{1,0:T(1,128)}, u32[]{:S(2)}) copy-start(f32[1,128]{1,0:T(1,128)} %constant.30.clone.mass_ref) | copy-start | bytes 1540
  0.0 35.2 %copy-start.2 = (bf16[128,256]{1,0:T(8,128)(2,1)S(1)}, bf16[128,256]{1,0:T(8,128)(2,1)}, u32[]{:S(2)}) copy-start(bf16[128,256]{1,0:T(8,128)(2,1)} %constant.29.clone.dl_ref) | copy-start | bytes 196612
  0.0 35.2 %copy-start.3 = (bf16[128,256]{1,0:T(8,128)(2,1)S(1)}, bf16[128,256]{1,0:T(8,128)(2,1)}, u32[]{:S(2)}) copy-start(bf16[128,256]{1,0:T(8,128)(2,1)} %constant.28.clone.dh_ref) | copy-start | bytes 196612
  0.0 15.2 %copy-start.6 = (bf16[3,2,11,2816]{3,1,2,0:T(2,128)(2,1)S(1)}, bf16[3,2,11,2816]{3,1,2,0:T(2,128)(2,1)}, u32[]{:S(2)}) copy-start(bf16[3,2,11,2816]{3,1,2,0:T(2,128)(2,1)} %param.16) | copy-start | bytes 1115140
  4.1 31.1 %all-to-all-start = ((f32[16,3,2,16,128]{4,3,2,1,0:T(8,128)}), f32[16,3,2,16,128]{4,3,2,1,0:T(8,128)S(1)}, u32[]{:S(2)}, u32[]{:S(2)}) async-start(f32[16,3,2,16,128]{4,3,2,1,0:T(8,128)} %pack.1), calls=%async_computation | async-start | bytes 1572864 | tf_op jit(solution)/shard_map/all_to_all | solution.py:787
  40.1 36.6 %copy-start = (f32[256,256]{1,0:T(8,128)S(1)}, f32[256,256]{1,0:T(8,128)}, u32[]{:S(2)}) copy-start(f32[256,256]{1,0:T(8,128)} %constant.32.clone.refs_7_) | copy-start | bytes 786436
  40.1 36.5 %copy-start.1 = (f32[256,256]{1,0:T(8,128)S(1)}, f32[256,256]{1,0:T(8,128)}, u32[]{:S(2)}) copy-start(f32[256,256]{1,0:T(8,128)} %constant.31.clone.refs_6_) | copy-start | bytes 786436
  40.1 36.5 %copy-start.4 = (f32[1,256]{1,0:T(1,128)S(1)}, f32[1,256]{1,0:T(1,128)}, u32[]{:S(2)}) copy-start(f32[1,256]{1,0:T(1,128)} %constant.33.clone.refs_8_) | copy-start | bytes 3076
  66.3 8.5 %collective-permute-start.1 = (f32[3,11,8,128]{3,2,1,0:T(8,128)S(1)}, f32[3,11,8,128]{3,2,1,0:T(8,128)S(1)}, u32[]{:S(2)}, u32[]{:S(2)}) collective-permute-start(f32[3,11,8,128]{3,2,1,0:T(8,128)S(1)} %get-tuple-element.23), channel_id=1, source_target_pairs={{16,0},{32,16},{48,32},{64,48},{80,64},{96,80},{112,96},{128,112},... | collective-permute-start | bytes 405512 | tf_op jit(solution)/shard_map/ppermute | solution.py:799
  68.6 8.0 %collective-permute-start = (f32[3,11,8,128]{3,2,1,0:T(8,128)S(1)}, f32[3,11,8,128]{3,2,1,0:T(8,128)S(1)}, u32[]{:S(2)}, u32[]{:S(2)}) collective-permute-start(f32[3,11,8,128]{3,2,1,0:T(8,128)S(1)} %get-tuple-element.24), channel_id=1, source_target_pairs={{0,16},{16,32},{32,48},{48,64},{64,80},{80,96},{96,112},{112,128},... | collective-permute-start | bytes 405512 | tf_op jit(solution)/shard_map/ppermute | solution.py:798
  84.1 21.1 %all-to-all-start.2 = ((f32[32,8,128]{2,1,0:T(8,128)}), f32[32,8,128]{2,1,0:T(8,128)S(1)}, u32[]{:S(2)}, u32[]{:S(2)}) async-start(f32[32,8,128]{2,1,0:T(8,128)} %get-tuple-element.19), calls=%async_computation.2 | async-start | bytes 262144 | tf_op jit(solution)/shard_map/all_to_all | solution.py:804

commit v7 on v6

--- a/solution.py
+++ b/solution.py
@@ -285,10 +285,10 @@
             for plane, p in zip(planes, parts):
                 slopes[0, c, ey, p] = plane[:, :LANES] * (2.0 / width)
                 slopes[1, c, ey, p] = plane[:, LANES:] * (2.0 / heights[ey])
-    for copy in copies:
-        copy.wait()
+    copies[0].wait()
     lane = lane_ids((PLANES, LANES))
     for c in range(3):
+        copies[1 + c].wait()
         pieces = []
         for ey in range(2):
             total = fields[0, 0, ey] * slopes[0, c, ey]
@@ -513,9 +513,7 @@
         else:
             mass_y.append(h1 * weights[y - Q + 1])
 
-    def apply(source, target, operator, mass_row, low_key):
-        dot_split(source, tmp, operator)
-        sums = [[], []]
+    def apply(source, target, tmp, prod, mass_row, low_key):
         for half in range(2):
             plane = ints[0] * LOCAL + half * 8 + lax.broadcasted_iota(jnp.int32, (8, LANES), 0)
             kappa = jnp.where(plane == 1, PLANES // 2, plane >> 1).astype(F32)
@@ -570,14 +568,23 @@
             for qy, value in zip(places, values):
                 rows = slice(base + qy * LOCAL, base + qy * LOCAL + 8)
                 v0_ref[comp, rows, lanes] = placed_ref[comp, rows, lanes] + value
+    vectors = (v0_ref, v1_ref, v2_ref)
+    tasks = [(stage, comp) for stage in range(3) for comp in range(3)]
+
+    def multiply(stage, comp):
+        dot_split(vectors[stage].at[comp], tmp.at[comp], kxs if stage < 2 else kbs)
+
+    multiply(*tasks[0])
+    for k, (stage, comp) in enumerate(tasks):
+        if k + 1 < len(tasks):
+            multiply(*tasks[k + 1])
+        target = vectors[stage + 1].at[comp] if stage < 2 else None
+        mass_row = 1 if stage < 2 else 2
+        apply(vectors[stage].at[comp], target, tmp.at[comp], prod.at[comp], mass_row, 2 * stage)
     for comp in range(3):
-        first, second, third = v0_ref.at[comp], v1_ref.at[comp], v2_ref.at[comp]
-        prod[6 * LOCAL :, :] = jnp.zeros((LANES - 6 * LOCAL, LANES), F32)
-        apply(first, second, kxs, 1, 0)
-        apply(second, third, kxs, 1, 2)
-        apply(third, None, kbs, 2, 4)
+        prod[comp, 6 * LOCAL :, :] = jnp.zeros((LANES - 6 * LOCAL, LANES), F32)
         row = lax.dot_general(
-            jnp.ones((8, LANES), F32), prod[...], (((1,), (1,)), ((), ())),
+            jnp.ones((8, LANES), F32), prod[comp], (((1,), (1,)), ((), ())),
             precision=HIGHEST, preferred_element_type=F32,
         )
         mom_ref[:, comp : comp + 1, :] = jnp.broadcast_to(
@@ -610,8 +617,8 @@
             pltpu.VMEM((3, 2 * LANES, 2 * LANES), BF16),
             pltpu.VMEM((3, 2 * LANES, 2 * LANES), BF16),
             pltpu.VMEM((4, 8, 2 * LANES), F32),
-            pltpu.VMEM((LANES, LANES), F32),
-            pltpu.VMEM((ROWS * LOCAL, 2 * LANES), F32),
+            pltpu.VMEM((3, LANES, LANES), F32),
+            pltpu.VMEM((3, ROWS * LOCAL, 2 * LANES), F32),
         ],
         compiler_params=pltpu.CompilerParams(vmem_limit_bytes=24 * 2**20),
         name="krylov_stage",

time: 110 us -> 108 us (0.982)
  Pallas kernels: 32.6 us -> 30.9 us
    pallas_call x1, Pallas kernels: 7.44 us -> 5.82 us  [krylov_stage(): pl.pallas_call(body, grid=(1,), in_specs=[smem, smem, vector, chunk(COLUM...]
where the time goes in v7:
time: 108 us; the launch traced here: 107 us
  Pallas kernels  30.9 us (29%)
  starting transfers between devices  27.6 us (26%)
  blocking collectives  26.1 us (24%)
  waiting for transfers between devices  20.3 us (19%)
    all_to_all x1, blocking collectives, local(): lax.all_to_all(source, 'four', split_axis=0, concat_axis=0, tiled=True)  26.1 us
    all_to_all x1, waiting for transfers between devices, local(): lax.all_to_all(send, 'four', split_axis=0, concat_axis=0, tiled=True)  11.6 us
    all_to_all x1, starting transfers between devices, local(): lax.all_to_all(moments, 'elem', split_axis=0, concat_axis=0, tiled=True)  11.4 us
    all_to_all x1, starting transfers between devices, local(): lax.all_to_all(send, 'four', split_axis=0, concat_axis=0, tiled=True)  10.4 us
    pallas_call x1, Pallas kernels, base_stage(): pl.pallas_call(base_body, grid=(6,), in_specs=[smem, smem, smem, pl.Block...  6.97 us
    all_to_all x1, waiting for transfers between devices, local(): lax.all_to_all(moments, 'elem', split_axis=0, concat_axis=0, tiled=True)  6.8 us
    pallas_call x1, Pallas kernels, krylov_stage(): pl.pallas_call(body, grid=(1,), in_specs=[smem, smem, vector, chunk(COLUM...  5.82 us
    pallas_call x1, Pallas kernels, lines_stage(): pl.pallas_call(lines_body, grid=(1,), in_specs=[smem, smem, smem, whole(a...  4.75 us
  transfers between devices with their start and end apart: 4, of which 3 were waited for; matrix products, arithmetic and copies ran while one was open for 1% of the time, Pallas kernels for 12%

profile of v7, /device:TPU:8, one launch (start us, length us, event | category | flops | bytes accessed | tf_op | source)
XLA Modules:
  0.0 107.2 jit_solution(13929353511904191543)
XLA Ops:
  0.0 0.0 copy-start.6
  0.0 4.1 %pack.1 = f32[16,3,2,16,128]{4,3,2,1,0:T(8,128)} custom-call(f32[3,121,4,128]{3,2,1,0:T(4,128)} %bitcast.15), custom_call_target="tpu_custom_call" | custom-call | tf_op jit(solution)/shard_map/pack/pallas_call | solution.py:181
  4.1 10.4 %all-to-all-start = ((f32[16,3,2,16,128]{4,3,2,1,0:T(8,128)}), f32[16,3,2,16,128]{4,3,2,1,0:T(8,128)S(1)}, u32[]{:S(2)}, u32[]{:S(2)}) async-start(f32[16,3,2,16,128]{4,3,2,1,0:T(8,128)} %pack.1), calls=%async_computation | async-start | bytes 1572864 | tf_op jit(solution)/shard_map/all_to_all | solution.py:794
  15.2 0.9 copy.17.base_ref
  16.1 0.6 pad_add_fusion.ints.refs_0_
  16.7 7.0 %base_stage.1 = (f32[4,3,2,256,128]{4,3,2,1,0:T(8,128)}, bf16[512,256]{1,0:T(8,128)(2,1)}, bf16[512,256]{1,0:T(8,128)(2,1)}, bf16[256,256]{1,0:T(8,128)(2,1)}, bf16[256,256]{1,0:T(8,128)(2,1)}) custom-call(s32[2]{0:T(128)} %pad_add_fusion.ints.refs_0_, f32[16]{0:T(128)} %widths.3, f32[2]{0:T(128)} %refs_1_.1, bf16[3,2,11,2816]{3,2,1,0:T(8,128)(2,1)} %copy.17.base_ref, ...), custom_call_target="tpu_custom_call" | custom-call | tf_op jit(solution)/shard_map/base_stage/pallas_call | solution.py:234
  23.6 11.6 %all-to-all-done.in_ref = f32[16,3,2,16,128]{4,3,2,1,0:T(8,128)S(1)} async-done(((f32[16,3,2,16,128]{4,3,2,1,0:T(8,128)}), f32[16,3,2,16,128]{4,3,2,1,0:T(8,128)S(1)}, u32[]{:S(2)}, u32[]{:S(2)}) %all-to-all-start) | async-done | bytes 786464 | tf_op jit(solution)/shard_map/all_to_all | solution.py:794
  35.2 0.0 copy-done.5
  35.3 0.0 copy-done.3
  35.3 4.8 %lines_stage.1 = f32[16,11,8,128]{3,2,1,0:T(8,128)S(1)} custom-call(s32[2]{0:T(128)} %pad_add_fusion.ints.refs_0_, f32[16]{0:T(128)} %widths.3, f32[2]{0:T(128)} %refs_1_.1, f32[16,3,2,16,128]{4,3,2,1,0:T(8,128)S(1)} %all-to-all-done.in_ref, f32[4,3,2,256,128]{4,3,2,1,0:T(8,128)} %get-tuple-element.14.field_hbm, bf16[512,256]{1,0:T(8,128)(2,1)} %get-tuple-element.15.fgh_ref, ...), custom_call_target="tpu_custom_call" | custom-call | tf_op jit(solution)/shard_map/lines_stage/pallas_call | solution.py:335
  40.0 0.0 copy-start
  40.0 0.0 copy-start.1
  40.0 0.0 copy-start.4
  40.1 26.1 %all_to_all.15.own_ref.refs_3_ = f32[16,11,8,128]{3,2,1,0:T(8,128)S(1)} all-to-all(f32[16,11,8,128]{3,2,1,0:T(8,128)S(1)} %lines_stage.1), channel_id=1, replica_groups=mesh['elem'=32,'four'=16] {'four'}, dimensions={0} | all-to-all | bytes 1441792 | tf_op jit(solution)/shard_map/all_to_all | solution.py:803
  66.2 2.3 %collective-permute-start.1 = (f32[3,11,8,128]{3,2,1,0:T(8,128)S(1)}, f32[3,11,8,128]{3,2,1,0:T(8,128)S(1)}, u32[]{:S(2)}, u32[]{:S(2)}) collective-permute-start(f32[3,11,8,128]{3,2,1,0:T(8,128)S(1)} %get-tuple-element.23), channel_id=1, source_target_pairs={{16,0},{32,16},{48,32},{64,48},{80,64},{96,80},{112,96},{128,112},... | collective-permute-start | bytes 405512 | tf_op jit(solution)/shard_map/ppermute | solution.py:806
  68.5 3.5 %collective-permute-start = (f32[3,11,8,128]{3,2,1,0:T(8,128)S(1)}, f32[3,11,8,128]{3,2,1,0:T(8,128)S(1)}, u32[]{:S(2)}, u32[]{:S(2)}) collective-permute-start(f32[3,11,8,128]{3,2,1,0:T(8,128)S(1)} %get-tuple-element.24), channel_id=1, source_target_pairs={{0,16},{16,32},{32,48},{48,64},{64,80},{80,96},{96,112},{112,128},... | collective-permute-start | bytes 405512 | tf_op jit(solution)/shard_map/ppermute | solution.py:805
  72.0 2.7 %place_stage.1.refs_2_ = f32[3,336,256]{2,1,0:T(8,128)S(1)} custom-call(f32[16,11,8,128]{3,2,1,0:T(8,128)S(1)} %all_to_all.15.own_ref.refs_3_), custom_call_target="tpu_custom_call" | custom-call | tf_op jit(solution)/shard_map/place_stage/pallas_call | solution.py:406
  74.7 0.0 collective-permute-done.1.refs_5_
  74.7 1.9 %collective-permute-done.refs_4_ = f32[3,11,8,128]{3,2,1,0:T(8,128)S(1)} collective-permute-done((f32[3,11,8,128]{3,2,1,0:T(8,128)S(1)}, f32[3,11,8,128]{3,2,1,0:T(8,128)S(1)}, u32[]{:S(2)}, u32[]{:S(2)}) %collective-permute-start) | collective-permute-done | bytes 135200 | tf_op jit(solution)/shard_map/ppermute | solution.py:805
  76.6 5.8 %krylov_stage.1 = (f32[3,336,256]{2,1,0:T(8,128)S(1)}, f32[3,336,256]{2,1,0:T(8,128)S(1)}, f32[3,336,256]{2,1,0:T(8,128)S(1)}, f32[32,8,128]{2,1,0:T(8,128)}) custom-call(s32[2]{0:T(128)} %pad_add_fusion.ints.refs_0_, f32[2]{0:T(128)} %refs_1_.1, f32[3,336,256]{2,1,0:T(8,128)S(1)} %place_stage.1.refs_2_, f32[16,11,8,128]{3,2,1,0:T(8,128)S(1)} %all_to_all.15.own_ref.refs_3_, ...), custom_call_target="tpu_custom_call" | custom-call | tf_op jit(solution)/shard_map/krylov_stage/pallas_call | solution.py:610
  82.4 11.4 %all-to-all-start.2 = ((f32[32,8,128]{2,1,0:T(8,128)}), f32[32,8,128]{2,1,0:T(8,128)S(1)}, u32[]{:S(2)}, u32[]{:S(2)}) async-start(f32[32,8,128]{2,1,0:T(8,128)} %get-tuple-element.19), calls=%async_computation.2 | async-start | bytes 262144 | tf_op jit(solution)/shard_map/all_to_all | solution.py:811
  93.8 2.9 %unpack.1.u_ref = f32[3,3,121,4,128]{4,3,2,1,0:T(4,128)} custom-call(f32[3,336,256]{2,1,0:T(8,128)S(1)} %get-tuple-element.20.v0_ref, f32[3,336,256]{2,1,0:T(8,128)S(1)} %get-tuple-element.21.v1_ref, f32[3,336,256]{2,1,0:T(8,128)S(1)} %get-tuple-element.22.v2_ref), custom_call_target="tpu_custom_call" | custom-call | tf_op jit(solution)/shard_map/unpack/pallas_call | solution.py:662
  96.7 6.8 %all-to-all-done.2.mom_ref = f32[32,8,128]{2,1,0:T(8,128)S(1)} async-done(((f32[32,8,128]{2,1,0:T(8,128)}), f32[32,8,128]{2,1,0:T(8,128)S(1)}, u32[]{:S(2)}, u32[]{:S(2)}) %all-to-all-start.2) | async-done | bytes 131104 | tf_op jit(solution)/shard_map/all_to_all | solution.py:811
  103.5 3.6 %finish.1 = f32[3,121,4,128]{3,2,1,0:T(4,128)} custom-call(f32[32,8,128]{2,1,0:T(8,128)S(1)} %all-to-all-done.2.mom_ref, f32[3,3,121,4,128]{4,3,2,1,0:T(4,128)} %unpack.1.u_ref), custom_call_target="tpu_custom_call" | custom-call | tf_op jit(solution)/shard_map/finish/pallas_call | solution.py:734
  (9 shorter events, 0.0 us)
Async XLA Ops:
  0.0 35.2 %copy-start.5 = (f32[1,128]{1,0:T(1,128)S(1)}, f32[1,128]{1,0:T(1,128)}, u32[]{:S(2)}) copy-start(f32[1,128]{1,0:T(1,128)} %constant.30.clone.mass_ref) | copy-start | bytes 1540
  0.0 35.2 %copy-start.2 = (bf16[128,256]{1,0:T(8,128)(2,1)S(1)}, bf16[128,256]{1,0:T(8,128)(2,1)}, u32[]{:S(2)}) copy-start(bf16[128,256]{1,0:T(8,128)(2,1)} %constant.29.clone.dl_ref) | copy-start | bytes 196612
  0.0 35.2 %copy-start.3 = (bf16[128,256]{1,0:T(8,128)(2,1)S(1)}, bf16[128,256]{1,0:T(8,128)(2,1)}, u32[]{:S(2)}) copy-start(bf16[128,256]{1,0:T(8,128)(2,1)} %constant.28.clone.dh_ref) | copy-start | bytes 196612
  0.0 15.2 %copy-start.6 = (bf16[3,2,11,2816]{3,1,2,0:T(2,128)(2,1)S(1)}, bf16[3,2,11,2816]{3,1,2,0:T(2,128)(2,1)}, u32[]{:S(2)}) copy-start(bf16[3,2,11,2816]{3,1,2,0:T(2,128)(2,1)} %param.16) | copy-start | bytes 1115140
  4.1 31.1 %all-to-all-start = ((f32[16,3,2,16,128]{4,3,2,1,0:T(8,128)}), f32[16,3,2,16,128]{4,3,2,1,0:T(8,128)S(1)}, u32[]{:S(2)}, u32[]{:S(2)}) async-start(f32[16,3,2,16,128]{4,3,2,1,0:T(8,128)} %pack.1), calls=%async_computation | async-start | bytes 1572864 | tf_op jit(solution)/shard_map/all_to_all | solution.py:794
  40.0 36.6 %copy-start = (f32[256,256]{1,0:T(8,128)S(1)}, f32[256,256]{1,0:T(8,128)}, u32[]{:S(2)}) copy-start(f32[256,256]{1,0:T(8,128)} %constant.32.clone.refs_7_) | copy-start | bytes 786436
  40.0 36.5 %copy-start.1 = (f32[256,256]{1,0:T(8,128)S(1)}, f32[256,256]{1,0:T(8,128)}, u32[]{:S(2)}) copy-start(f32[256,256]{1,0:T(8,128)} %constant.31.clone.refs_6_) | copy-start | bytes 786436
  40.0 36.5 %copy-start.4 = (f32[1,256]{1,0:T(1,128)S(1)}, f32[1,256]{1,0:T(1,128)}, u32[]{:S(2)}) copy-start(f32[1,256]{1,0:T(1,128)} %constant.33.clone.refs_8_) | copy-start | bytes 3076
  66.2 8.5 %collective-permute-start.1 = (f32[3,11,8,128]{3,2,1,0:T(8,128)S(1)}, f32[3,11,8,128]{3,2,1,0:T(8,128)S(1)}, u32[]{:S(2)}, u32[]{:S(2)}) collective-permute-start(f32[3,11,8,128]{3,2,1,0:T(8,128)S(1)} %get-tuple-element.23), channel_id=1, source_target_pairs={{16,0},{32,16},{48,32},{64,48},{80,64},{96,80},{112,96},{128,112},... | collective-permute-start | bytes 405512 | tf_op jit(solution)/shard_map/ppermute | solution.py:806
  68.5 8.0 %collective-permute-start = (f32[3,11,8,128]{3,2,1,0:T(8,128)S(1)}, f32[3,11,8,128]{3,2,1,0:T(8,128)S(1)}, u32[]{:S(2)}, u32[]{:S(2)}) collective-permute-start(f32[3,11,8,128]{3,2,1,0:T(8,128)S(1)} %get-tuple-element.24), channel_id=1, source_target_pairs={{0,16},{16,32},{32,48},{48,64},{64,80},{80,96},{96,112},{112,128},... | collective-permute-start | bytes 405512 | tf_op jit(solution)/shard_map/ppermute | solution.py:805
  82.4 21.1 %all-to-all-start.2 = ((f32[32,8,128]{2,1,0:T(8,128)}), f32[32,8,128]{2,1,0:T(8,128)S(1)}, u32[]{:S(2)}, u32[]{:S(2)}) async-start(f32[32,8,128]{2,1,0:T(8,128)} %get-tuple-element.19), calls=%async_computation.2 | async-start | bytes 262144 | tf_op jit(solution)/shard_map/all_to_all | solution.py:811

commit v8 on v7

--- a/solution.py
+++ b/solution.py
@@ -286,9 +286,12 @@
                 slopes[0, c, ey, p] = plane[:, :LANES] * (2.0 / width)
                 slopes[1, c, ey, p] = plane[:, LANES:] * (2.0 / heights[ey])
     copies[0].wait()
+    copies[1].wait()
     lane = lane_ids((PLANES, LANES))
     for c in range(3):
-        copies[1 + c].wait()
+        if c == 1:
+            copies[2].wait()
+            copies[3].wait()
         pieces = []
         for ey in range(2):
             total = fields[0, 0, ey] * slopes[0, c, ey]

time: 108 us -> 108 us (level)
  no operation moved by 1% of the time
where the time goes in v8:
time: 108 us; the launch traced here: 107 us
  Pallas kernels  30.7 us (28%)
  starting transfers between devices  27.6 us (26%)
  blocking collectives  26.1 us (24%)
  waiting for transfers between devices  20.3 us (19%)
    all_to_all x1, blocking collectives, local(): lax.all_to_all(source, 'four', split_axis=0, concat_axis=0, tiled=True)  26.1 us
    all_to_all x1, waiting for transfers between devices, local(): lax.all_to_all(send, 'four', split_axis=0, concat_axis=0, tiled=True)  11.6 us
    all_to_all x1, starting transfers between devices, local(): lax.all_to_all(moments, 'elem', split_axis=0, concat_axis=0, tiled=True)  11.4 us
    all_to_all x1, starting transfers between devices, local(): lax.all_to_all(send, 'four', split_axis=0, concat_axis=0, tiled=True)  10.4 us
    pallas_call x1, Pallas kernels, base_stage(): pl.pallas_call(base_body, grid=(6,), in_specs=[smem, smem, smem, pl.Block...  6.97 us
    all_to_all x1, waiting for transfers between devices, local(): lax.all_to_all(moments, 'elem', split_axis=0, concat_axis=0, tiled=True)  6.8 us
    pallas_call x1, Pallas kernels, krylov_stage(): pl.pallas_call(body, grid=(1,), in_specs=[smem, smem, vector, chunk(COLUM...  5.82 us
    pallas_call x1, Pallas kernels, lines_stage(): pl.pallas_call(lines_body, grid=(1,), in_specs=[smem, smem, smem, whole(a...  4.61 us
  transfers between devices with their start and end apart: 4, of which 3 were waited for; matrix products, arithmetic and copies ran while one was open for 1% of the time, Pallas kernels for 12%

profile of v8, /device:TPU:8, one launch (start us, length us, event | category | flops | bytes accessed | tf_op | source)
XLA Modules:
  0.0 107.0 jit_solution(4691680359400661849)
XLA Ops:
  0.0 4.1 %pack.1 = f32[16,3,2,16,128]{4,3,2,1,0:T(8,128)} custom-call(f32[3,121,4,128]{3,2,1,0:T(4,128)} %bitcast.15), custom_call_target="tpu_custom_call" | custom-call | tf_op jit(solution)/shard_map/pack/pallas_call | solution.py:181
  4.1 10.4 %all-to-all-start = ((f32[16,3,2,16,128]{4,3,2,1,0:T(8,128)}), f32[16,3,2,16,128]{4,3,2,1,0:T(8,128)S(1)}, u32[]{:S(2)}, u32[]{:S(2)}) async-start(f32[16,3,2,16,128]{4,3,2,1,0:T(8,128)} %pack.1), calls=%async_computation | async-start | bytes 1572864 | tf_op jit(solution)/shard_map/all_to_all | solution.py:797
  15.2 0.9 copy.17.base_ref
  16.1 0.6 pad_add_fusion.ints.refs_0_
  16.7 7.0 %base_stage.1 = (f32[4,3,2,256,128]{4,3,2,1,0:T(8,128)}, bf16[512,256]{1,0:T(8,128)(2,1)}, bf16[512,256]{1,0:T(8,128)(2,1)}, bf16[256,256]{1,0:T(8,128)(2,1)}, bf16[256,256]{1,0:T(8,128)(2,1)}) custom-call(s32[2]{0:T(128)} %pad_add_fusion.ints.refs_0_, f32[16]{0:T(128)} %widths.3, f32[2]{0:T(128)} %refs_1_.1, bf16[3,2,11,2816]{3,2,1,0:T(8,128)(2,1)} %copy.17.base_ref, ...), custom_call_target="tpu_custom_call" | custom-call | tf_op jit(solution)/shard_map/base_stage/pallas_call | solution.py:234
  23.6 11.6 %all-to-all-done.in_ref = f32[16,3,2,16,128]{4,3,2,1,0:T(8,128)S(1)} async-done(((f32[16,3,2,16,128]{4,3,2,1,0:T(8,128)}), f32[16,3,2,16,128]{4,3,2,1,0:T(8,128)S(1)}, u32[]{:S(2)}, u32[]{:S(2)}) %all-to-all-start) | async-done | bytes 786464 | tf_op jit(solution)/shard_map/all_to_all | solution.py:797
  35.2 0.0 copy-done.5
  35.3 0.0 copy-done.3
  35.3 4.6 %lines_stage.1 = f32[16,11,8,128]{3,2,1,0:T(8,128)S(1)} custom-call(s32[2]{0:T(128)} %pad_add_fusion.ints.refs_0_, f32[16]{0:T(128)} %widths.3, f32[2]{0:T(128)} %refs_1_.1, f32[16,3,2,16,128]{4,3,2,1,0:T(8,128)S(1)} %all-to-all-done.in_ref, f32[4,3,2,256,128]{4,3,2,1,0:T(8,128)} %get-tuple-element.14.field_hbm, bf16[512,256]{1,0:T(8,128)(2,1)} %get-tuple-element.15.fgh_ref, ...), custom_call_target="tpu_custom_call" | custom-call | tf_op jit(solution)/shard_map/lines_stage/pallas_call | solution.py:338
  39.9 0.0 copy-start
  39.9 0.0 copy-start.1
  39.9 0.0 copy-start.4
  39.9 26.1 %all_to_all.15.own_ref.refs_3_ = f32[16,11,8,128]{3,2,1,0:T(8,128)S(1)} all-to-all(f32[16,11,8,128]{3,2,1,0:T(8,128)S(1)} %lines_stage.1), channel_id=1, replica_groups=mesh['elem'=32,'four'=16] {'four'}, dimensions={0} | all-to-all | bytes 1441792 | tf_op jit(solution)/shard_map/all_to_all | solution.py:806
  66.0 2.3 %collective-permute-start.1 = (f32[3,11,8,128]{3,2,1,0:T(8,128)S(1)}, f32[3,11,8,128]{3,2,1,0:T(8,128)S(1)}, u32[]{:S(2)}, u32[]{:S(2)}) collective-permute-start(f32[3,11,8,128]{3,2,1,0:T(8,128)S(1)} %get-tuple-element.23), channel_id=1, source_target_pairs={{16,0},{32,16},{48,32},{64,48},{80,64},{96,80},{112,96},{128,112},... | collective-permute-start | bytes 405512 | tf_op jit(solution)/shard_map/ppermute | solution.py:809
  68.4 3.5 %collective-permute-start = (f32[3,11,8,128]{3,2,1,0:T(8,128)S(1)}, f32[3,11,8,128]{3,2,1,0:T(8,128)S(1)}, u32[]{:S(2)}, u32[]{:S(2)}) collective-permute-start(f32[3,11,8,128]{3,2,1,0:T(8,128)S(1)} %get-tuple-element.24), channel_id=1, source_target_pairs={{0,16},{16,32},{32,48},{48,64},{64,80},{80,96},{96,112},{112,128},... | collective-permute-start | bytes 405512 | tf_op jit(solution)/shard_map/ppermute | solution.py:808
  71.9 2.7 %place_stage.1.refs_2_ = f32[3,336,256]{2,1,0:T(8,128)S(1)} custom-call(f32[16,11,8,128]{3,2,1,0:T(8,128)S(1)} %all_to_all.15.own_ref.refs_3_), custom_call_target="tpu_custom_call" | custom-call | tf_op jit(solution)/shard_map/place_stage/pallas_call | solution.py:409
  74.6 0.0 collective-permute-done.1.refs_5_
  74.6 1.8 %collective-permute-done.refs_4_ = f32[3,11,8,128]{3,2,1,0:T(8,128)S(1)} collective-permute-done((f32[3,11,8,128]{3,2,1,0:T(8,128)S(1)}, f32[3,11,8,128]{3,2,1,0:T(8,128)S(1)}, u32[]{:S(2)}, u32[]{:S(2)}) %collective-permute-start) | collective-permute-done | bytes 135200 | tf_op jit(solution)/shard_map/ppermute | solution.py:808
  76.4 0.0 copy-done.4
  76.4 5.8 %krylov_stage.1 = (f32[3,336,256]{2,1,0:T(8,128)S(1)}, f32[3,336,256]{2,1,0:T(8,128)S(1)}, f32[3,336,256]{2,1,0:T(8,128)S(1)}, f32[32,8,128]{2,1,0:T(8,128)}) custom-call(s32[2]{0:T(128)} %pad_add_fusion.ints.refs_0_, f32[2]{0:T(128)} %refs_1_.1, f32[3,336,256]{2,1,0:T(8,128)S(1)} %place_stage.1.refs_2_, f32[16,11,8,128]{3,2,1,0:T(8,128)S(1)} %all_to_all.15.own_ref.refs_3_, ...), custom_call_target="tpu_custom_call" | custom-call | tf_op jit(solution)/shard_map/krylov_stage/pallas_call | solution.py:613
  82.3 11.4 %all-to-all-start.2 = ((f32[32,8,128]{2,1,0:T(8,128)}), f32[32,8,128]{2,1,0:T(8,128)S(1)}, u32[]{:S(2)}, u32[]{:S(2)}) async-start(f32[32,8,128]{2,1,0:T(8,128)} %get-tuple-element.19), calls=%async_computation.2 | async-start | bytes 262144 | tf_op jit(solution)/shard_map/all_to_all | solution.py:814
  93.6 2.9 %unpack.1.u_ref = f32[3,3,121,4,128]{4,3,2,1,0:T(4,128)} custom-call(f32[3,336,256]{2,1,0:T(8,128)S(1)} %get-tuple-element.20.v0_ref, f32[3,336,256]{2,1,0:T(8,128)S(1)} %get-tuple-element.21.v1_ref, f32[3,336,256]{2,1,0:T(8,128)S(1)} %get-tuple-element.22.v2_ref), custom_call_target="tpu_custom_call" | custom-call | tf_op jit(solution)/shard_map/unpack/pallas_call | solution.py:665
  96.6 6.8 %all-to-all-done.2.mom_ref = f32[32,8,128]{2,1,0:T(8,128)S(1)} async-done(((f32[32,8,128]{2,1,0:T(8,128)}), f32[32,8,128]{2,1,0:T(8,128)S(1)}, u32[]{:S(2)}, u32[]{:S(2)}) %all-to-all-start.2) | async-done | bytes 131104 | tf_op jit(solution)/shard_map/all_to_all | solution.py:814
  103.4 3.6 %finish.1 = f32[3,121,4,128]{3,2,1,0:T(4,128)} custom-call(f32[32,8,128]{2,1,0:T(8,128)S(1)} %all-to-all-done.2.mom_ref, f32[3,3,121,4,128]{4,3,2,1,0:T(4,128)} %unpack.1.u_ref), custom_call_target="tpu_custom_call" | custom-call | tf_op jit(solution)/shard_map/finish/pallas_call | solution.py:737
  (9 shorter events, 0.0 us)
Async XLA Ops:
  0.0 35.2 %copy-start.5 = (f32[1,128]{1,0:T(1,128)S(1)}, f32[1,128]{1,0:T(1,128)}, u32[]{:S(2)}) copy-start(f32[1,128]{1,0:T(1,128)} %constant.30.clone.mass_ref) | copy-start | bytes 1540
  0.0 35.2 %copy-start.2 = (bf16[128,256]{1,0:T(8,128)(2,1)S(1)}, bf16[128,256]{1,0:T(8,128)(2,1)}, u32[]{:S(2)}) copy-start(bf16[128,256]{1,0:T(8,128)(2,1)} %constant.29.clone.dl_ref) | copy-start | bytes 196612
  0.0 35.2 %copy-start.3 = (bf16[128,256]{1,0:T(8,128)(2,1)S(1)}, bf16[128,256]{1,0:T(8,128)(2,1)}, u32[]{:S(2)}) copy-start(bf16[128,256]{1,0:T(8,128)(2,1)} %constant.28.clone.dh_ref) | copy-start | bytes 196612
  0.0 15.2 %copy-start.6 = (bf16[3,2,11,2816]{3,1,2,0:T(2,128)(2,1)S(1)}, bf16[3,2,11,2816]{3,1,2,0:T(2,128)(2,1)}, u32[]{:S(2)}) copy-start(bf16[3,2,11,2816]{3,1,2,0:T(2,128)(2,1)} %param.16) | copy-start | bytes 1115140
  4.1 31.1 %all-to-all-start = ((f32[16,3,2,16,128]{4,3,2,1,0:T(8,128)}), f32[16,3,2,16,128]{4,3,2,1,0:T(8,128)S(1)}, u32[]{:S(2)}, u32[]{:S(2)}) async-start(f32[16,3,2,16,128]{4,3,2,1,0:T(8,128)} %pack.1), calls=%async_computation | async-start | bytes 1572864 | tf_op jit(solution)/shard_map/all_to_all | solution.py:797
  39.9 36.5 %copy-start = (f32[256,256]{1,0:T(8,128)S(1)}, f32[256,256]{1,0:T(8,128)}, u32[]{:S(2)}) copy-start(f32[256,256]{1,0:T(8,128)} %constant.32.clone.refs_7_) | copy-start | bytes 786436
  39.9 36.5 %copy-start.1 = (f32[256,256]{1,0:T(8,128)S(1)}, f32[256,256]{1,0:T(8,128)}, u32[]{:S(2)}) copy-start(f32[256,256]{1,0:T(8,128)} %constant.31.clone.refs_6_) | copy-start | bytes 786436
  39.9 36.5 %copy-start.4 = (f32[1,256]{1,0:T(1,128)S(1)}, f32[1,256]{1,0:T(1,128)}, u32[]{:S(2)}) copy-start(f32[1,256]{1,0:T(1,128)} %constant.33.clone.refs_8_) | copy-start | bytes 3076
  66.0 8.5 %collective-permute-start.1 = (f32[3,11,8,128]{3,2,1,0:T(8,128)S(1)}, f32[3,11,8,128]{3,2,1,0:T(8,128)S(1)}, u32[]{:S(2)}, u32[]{:S(2)}) collective-permute-start(f32[3,11,8,128]{3,2,1,0:T(8,128)S(1)} %get-tuple-element.23), channel_id=1, source_target_pairs={{16,0},{32,16},{48,32},{64,48},{80,64},{96,80},{112,96},{128,112},... | collective-permute-start | bytes 405512 | tf_op jit(solution)/shard_map/ppermute | solution.py:809
  68.4 8.0 %collective-permute-start = (f32[3,11,8,128]{3,2,1,0:T(8,128)S(1)}, f32[3,11,8,128]{3,2,1,0:T(8,128)S(1)}, u32[]{:S(2)}, u32[]{:S(2)}) collective-permute-start(f32[3,11,8,128]{3,2,1,0:T(8,128)S(1)} %get-tuple-element.24), channel_id=1, source_target_pairs={{0,16},{16,32},{32,48},{48,64},{64,80},{80,96},{96,112},{112,128},... | collective-permute-start | bytes 405512 | tf_op jit(solution)/shard_map/ppermute | solution.py:808
  82.3 21.1 %all-to-all-start.2 = ((f32[32,8,128]{2,1,0:T(8,128)}), f32[32,8,128]{2,1,0:T(8,128)S(1)}, u32[]{:S(2)}, u32[]{:S(2)}) async-start(f32[32,8,128]{2,1,0:T(8,128)} %get-tuple-element.19), calls=%async_computation.2 | async-start | bytes 262144 | tf_op jit(solution)/shard_map/all_to_all | solution.py:814
